TPU v7x, 512 devices: a whole 4x4x16 slice. The times are simulated.
512 devices in a mesh: slab: 64 (over y, z), angle: 8 (over x, core).
Axes of the slice: x: 4, y: 4, z: 16, core: 2. Of those that a mesh axis runs over, the one named last changes fastest.
Arguments:
- object_density: bfloat16 [2, 512, 128, 320], P(None, 'slab', 'angle'), may hold values from -6 to 6
- resampling_matrices: bfloat16 [8, 64, 128], replicated, may hold values from -0.02734375 to 0.02734375
- receiving_tile_number: int32 [8, 64, 8], replicated, may hold values from 0 to 4
- illumination_modes: bfloat16 [4, 2, 256, 256], replicated, may hold values from -3 to 3
- window_corners: int32 [8, 64, 2], P('angle', 'slab'), may hold values from 1 to 63
- observed_power: float32 [8, 64, 256, 256], P('angle', 'slab'), may hold values from 0.5 to 2
Outputs:
- vol_grad: float32 [2, 512, 128, 320], P(None, 'slab', 'angle')
- probe_grad: float32 [4, 2, 256, 256], P(None, None, 'slab')
- power_mismatch: float32 [8, 64, 256, 256], P('angle', 'slab')
- locus_derivative: float32 [8, 64, 2], P('angle', 'slab')
All inputs are finite; a program needn't handle non-finite values.
Results may differ from a plain program's by a relative error of at most 0.00035.
Values sent between devices are 32-bit elements; how exact they have to be, the bound alone decides.
No kernel may reach another device: no remote copies, remote signals or barrier semaphores. Data moves between devices by JAX's collectives and lax.ppermute only.
A program may use at most 64 MiB of HBM per device.

v0:
```python
import math

import jax
import jax.numpy as jnp
from jax import lax
from jax.sharding import PartitionSpec as P

NUB = 5


HIGHEST = lax.Precision.HIGHEST


def dft_tables(length):
    freq = jnp.arange(length, dtype=jnp.int32)
    phase_ids = freq[:, None] * freq[None, :] % length
    phases = phase_ids.astype(jnp.float32) * (2.0 * math.pi / length)
    factor = 1.0 / math.sqrt(length)
    return (jnp.cos(phases) * factor, jnp.sin(phases) * factor)


def transform(real, imag, cosine, sine):
    mid_real = jnp.einsum("kn,mnz->mkz", cosine, real, precision=HIGHEST) + jnp.einsum(
        "kn,mnz->mkz", sine, imag, precision=HIGHEST
    )
    mid_imag = jnp.einsum("kn,mnz->mkz", cosine, imag, precision=HIGHEST) - jnp.einsum(
        "kn,mnz->mkz", sine, real, precision=HIGHEST
    )
    out_real = jnp.einsum("mkn,nz->mkz", mid_real, cosine, precision=HIGHEST) + jnp.einsum(
        "mkn,nz->mkz", mid_imag, sine, precision=HIGHEST
    )
    out_imag = jnp.einsum("mkn,nz->mkz", mid_imag, cosine, precision=HIGHEST) - jnp.einsum(
        "mkn,nz->mkz", mid_real, sine, precision=HIGHEST
    )
    return (out_real, out_imag)


def spot_loss(patch, illumination_modes, recorded_diffraction, cosine, sine):
    absorb = jnp.exp(-patch[1])
    t_real = absorb * jnp.cos(patch[0])
    t_imag = absorb * jnp.sin(patch[0])
    e_real = illumination_modes[:, 0] * t_real - illumination_modes[:, 1] * t_imag
    e_imag = illumination_modes[:, 0] * t_imag + illumination_modes[:, 1] * t_real
    far_real, far_imag = transform(e_real, e_imag, cosine, sine)
    inten = jnp.sum(far_real * far_real + far_imag * far_imag, axis=0)
    resid = inten - recorded_diffraction
    return (0.5 * jnp.sum(resid * resid), resid)


def local(
    object_density,
    resampling_matrices,
    receiving_tile_number,
    illumination_modes,
    window_corners,
    observed_power,
):
    n_angle = lax.axis_size("angle")
    my_angle = lax.axis_index("angle")
    my_slab = lax.axis_index("slab")
    x_cells = object_density.shape[1]
    z_cells = object_density.shape[3]
    tile_rows = resampling_matrices.shape[2]
    y_cells = tile_rows // x_cells
    tiles_here = object_density.shape[2] // y_cells
    blk_cols = resampling_matrices.shape[1]
    det_cols = blk_cols * NUB
    kernel_four = resampling_matrices.reshape(
        resampling_matrices.shape[0], blk_cols, x_cells, y_cells
    )
    vol_five = object_density.reshape(2, x_cells, tiles_here, y_cells, z_cells)
    blocks = jnp.einsum(
        "auxy,cxtyz->atcuz", kernel_four, vol_five, preferred_element_type=jnp.float32
    )
    angle_ids = lax.dynamic_index_in_dim(receiving_tile_number, my_angle, 0, keepdims=False)
    block_range = jnp.arange(NUB, dtype=jnp.int32)
    received = lax.all_to_all(blocks, "angle", split_axis=0, concat_axis=0, tiled=True)
    items = received.reshape(n_angle * tiles_here, 2, blk_cols, z_cells)
    dest_ids = lax.dynamic_index_in_dim(angle_ids, my_slab, 0, keepdims=False)
    onehot = (dest_ids[:, None] == block_range[None, :]).astype(jnp.float32)
    partial_value = jnp.einsum("id,icuz->cduz", onehot, items, precision=HIGHEST).reshape(
        2, det_cols, z_cells
    )
    sinogram_views = lax.psum(partial_value, "slab")
    probe_f = illumination_modes.astype(jnp.float32)
    probe_side = illumination_modes.shape[2]
    cosine, sine = dft_tables(probe_side)
    blank_detector = jnp.zeros((2, det_cols, z_cells), jnp.float32)
    probe_gradient_total = jnp.zeros_like(probe_f)
    zero_index = jnp.int32(0)
    col_off = window_corners[0, 0, 0]
    row_off = window_corners[0, 0, 1]
    recorded_diffraction = observed_power[0, 0]
    window = lax.dynamic_slice(
        sinogram_views, (zero_index, col_off - 1, row_off - 1), (2, probe_side + 2, probe_side + 2)
    )
    patch = window[:, 1:-1, 1:-1]
    loss, pull, resid = jax.vjp(
        lambda patch_in, probe_in: spot_loss(
            patch_in, probe_in, recorded_diffraction, cosine, sine
        ),
        patch,
        probe_f,
        has_aux=True,
    )
    patch_grad, probe_term = pull(jnp.ones((), jnp.float32))
    current = lax.dynamic_slice(
        blank_detector, (zero_index, col_off, row_off), (2, probe_side, probe_side)
    )
    blank_detector = lax.dynamic_update_slice(
        blank_detector, current + patch_grad, (zero_index, col_off, row_off)
    )
    shift_col = (
        jnp.sum(patch_grad * (window[:, 2:, 1:-1] - window[:, :-2, 1:-1])) * 0.5 / probe_side
    )
    shift_row = (
        jnp.sum(patch_grad * (window[:, 1:-1, 2:] - window[:, 1:-1, :-2])) * 0.5 / probe_side
    )
    probe_gradient_total = probe_gradient_total + probe_term
    resid_list = [resid]
    shift_list = [jnp.stack([shift_col, shift_row])]
    power_mismatch = jnp.stack(resid_list)[None]
    locus_derivative = jnp.stack(shift_list)[None]
    sinogram_derivative = lax.psum(blank_detector, "slab")
    send_ids = lax.dynamic_index_in_dim(angle_ids, my_slab, 0, keepdims=False)
    send_hot = (send_ids[:, None] == block_range[None, :]).astype(jnp.float32)
    outgoing = jnp.einsum(
        "id,cduz->icuz",
        send_hot,
        sinogram_derivative.reshape(2, NUB, blk_cols, z_cells),
        precision=HIGHEST,
    )
    outgoing = outgoing.reshape(n_angle, tiles_here, 2, blk_cols, z_cells)
    incoming = lax.all_to_all(outgoing, "angle", split_axis=0, concat_axis=0, tiled=True)
    tile_grad = jnp.einsum(
        "auxy,atcuz->cxtyz", kernel_four.astype(jnp.float32), incoming, precision=HIGHEST
    )
    vol_grad = tile_grad.reshape(2, x_cells, tiles_here * y_cells, z_cells)
    across = lax.psum(probe_gradient_total, "angle")
    probe_grad = lax.psum_scatter(across, "slab", scatter_dimension=2, tiled=True)
    return (vol_grad, probe_grad, power_mismatch, locus_derivative)


def solution(mesh):
    in_specs = (
        P(None, "slab", "angle", None),
        P(),
        P(),
        P(),
        P("angle", "slab", None),
        P("angle", "slab", None, None),
    )
    out_specs = (
        P(None, "slab", "angle", None),
        P(None, None, "slab", None),
        P("angle", "slab", None, None),
        P("angle", "slab", None),
    )
    return jax.shard_map(local, mesh=mesh, in_specs=in_specs, out_specs=out_specs, check_vma=False)
```

profile of v0, /device:TPU:1, one launch (start us, length us, event | category | flops | bytes accessed | tf_op | source)
XLA Modules:
  0.0 710.3 jit_solution(16630258983009779786)
XLA Ops:
  10.0 10.3 %all-to-all-start = ((f32[8,1,2,64,320]{4,3,2,1,0:T(8,128)}), f32[8,1,2,64,320]{4,3,2,1,0:T(8,128)S(1)}, u32[]{:S(2)}, u32[]{:S(2)}) async-start(f32[8,1,2,64,320]{4,3,2,1,0:T(8,128)} %copy.45), calls=%async_computation | async-start | bytes 3145728 | tf_op jit(solution)/shard_map/all_to_all | solution.py:77
  21.2 19.7 %all-to-all-done = f32[8,1,2,64,320]{4,3,2,1,0:T(8,128)S(1)} async-done(((f32[8,1,2,64,320]{4,3,2,1,0:T(8,128)}), f32[8,1,2,64,320]{4,3,2,1,0:T(8,128)S(1)}, u32[]{:S(2)}, u32[]{:S(2)}) %all-to-all-start) | async-done | bytes 1310752 | tf_op jit(solution)/shard_map/all_to_all | solution.py:77
  40.9 1.7 fusion.6
  42.9 1.3 copy.49
  52.1 254.5 %all-reduce.12.cloned.1.call-done = f32[2,320,320]{1,2,0:T(8,128)} async-done(((f32[2,320,320]{1,2,0:T(8,128)}), f32[2,320,320]{1,2,0:T(8,128)}) %all-reduce.12.cloned.1.call-update) | async-done | bytes 819216 | tf_op jit(solution)/shard_map/psum | solution.py:84
  306.6 2.3 multiply_bitcast_fusion.5
  308.9 2.0 fusion.63
  311.0 2.0 fusion.59
  313.0 2.0 fusion.14
  315.0 2.0 fusion.13
  317.1 2.7 fusion.57
  319.8 2.9 fusion.61
  322.7 2.7 convolution_add_fusion.4
  325.5 2.8 add_reduce_fusion
  328.4 2.0 fusion.20
  330.4 2.0 fusion.22
  332.4 2.4 fusion.12
  334.8 2.7 fusion.18
  337.5 2.7 fusion.54
  340.2 2.0 fusion.11
  342.2 2.7 fusion.9
  344.9 4.4 multiply_bitcast_fusion.3
  349.6 2.0 copy.64
  351.7 2.3 fusion.41
  355.5 7.3 %dynamic_update_slice.3 = f32[2,320,320]{2,1,0:T(8,128)S(1)} dynamic-update-slice(f32[2,320,320]{2,1,0:T(8,128)S(1)} %broadcast_in_dim.14, f32[2,256,256]{2,1,0:T(8,128)S(1)} %copy.59, s32[]{:T(128)} %constant.62.clone.1, s32[]{:T(128)S(6)} %select_n.69, s32[]{:T(128)S(6)} %select_n.70) | dynamic-update-slice | bytes 1048580 | tf_op jit(solution)/shard_map/dynamic_update_slice | solution.py:110
  362.9 1.8 copy.60
  364.7 284.8 %all-reduce.14.cloned.1.call-done = (f32[2,5,64,320]{3,1,2,0:T(8,128)}, f32[4,2,256,256]{3,0,1,2:T(4,128)}) async-done(((f32[2,5,64,320]{3,1,2,0:T(8,128)}, f32[4,2,256,256]{3,0,1,2:T(4,128)}), (f32[2,5,64,320]{3,1,2,0:T(8,128)}, f32[4,2,256,256]{3,0,1,2:T(4,128)})) %all-reduce.14.cloned.1.call-update) | async-done | bytes 2916368 | tf_op jit(solution)/shard_map/psum | solution.py:124
  649.5 2.3 convolution_bitcast_fusion
  651.8 1.4 copy.61
  653.2 13.6 %all-to-all-start.1 = ((f32[8,1,2,64,320]{4,3,2,1,0:T(8,128)}), f32[8,1,2,64,320]{4,3,2,1,0:T(8,128)S(1)}, u32[]{:S(2)}, u32[]{:S(2)}) async-start(f32[8,1,2,64,320]{4,3,2,1,0:T(8,128)} %copy.61), calls=%async_computation.1 | async-start | bytes 3145728 | tf_op jit(solution)/shard_map/all_to_all | solution.py:134
  672.1 29.1 %psum.24 = f32[4,2,4,256]{3,0,1,2:T(4,128)S(1)} all-reduce(f32[4,2,4,256]{3,0,1,2:T(4,128)S(1)} %constant_dynamic-slice_fusion), channel_id=1, replica_groups=mesh['slab'=64,'angle'=8] {'angle'}, use_global_device_ids=true, to_apply=%region_7.8 | all-reduce | flops 8192 | bytes 65536 | tf_op jit(solution)/shard_map/psum | solution.py:139
  701.7 1.5 fusion.15
  (39 shorter events, 11.1 us)
Async XLA Ops:
  7.2 1.1 copy-start
  8.3 1.7 copy-start.2
  10.0 30.9 %all-to-all-start = ((f32[8,1,2,64,320]{4,3,2,1,0:T(8,128)}), f32[8,1,2,64,320]{4,3,2,1,0:T(8,128)S(1)}, u32[]{:S(2)}, u32[]{:S(2)}) async-start(f32[8,1,2,64,320]{4,3,2,1,0:T(8,128)} %copy.45), calls=%async_computation | async-start | bytes 3145728 | tf_op jit(solution)/shard_map/all_to_all | solution.py:77
  20.3 286.3 %all-reduce.12.cloned.1.call-start = ((), (), s32[]{:S(2)}) async-start(), calls=%async_computation.2 | async-start | bytes 1966080 | tf_op jit(solution)/shard_map/psum | solution.py:84
  42.9 1.4 copy-start.7
  42.9 7.2 %copy-start.6 = (bf16[4,2,256,256]{3,2,1,0:T(8,128)(2,1)S(1)}, bf16[4,2,256,256]{3,2,1,0:T(8,128)(2,1)}, u32[]{:S(2)}) copy-start(bf16[4,2,256,256]{3,2,1,0:T(8,128)(2,1)} %param.9) | copy-start | bytes 3145732
  44.3 605.2 %all-reduce.14.cloned.1.call-start = ((), (), s32[]{:S(2)}) async-start(), calls=%async_computation.3 | async-start | bytes 7340032 | tf_op jit(solution)/shard_map/psum | solution.py:124
  325.5 2.8 copy-start.4
  349.6 2.0 copy-start.1
  653.2 17.4 %copy-start.5 = (f32[1,1,256,256]{3,2,1,0:T(8,128)S(1)}, f32[1,1,256,256]{3,2,1,0:T(8,128)}, u32[]{:S(2)}) copy-start(f32[1,1,256,256]{3,2,1,0:T(8,128)} %param.11) | copy-start | bytes 786436
  653.2 48.5 %copy-start.3 = (bf16[8,64,128]{1,2,0:T(8,128)(2,1)S(1)}, bf16[8,64,128]{1,2,0:T(8,128)(2,1)}, u32[]{:S(2)}) copy-start(bf16[8,64,128]{1,2,0:T(8,128)(2,1)} %copy-done.2) | copy-start | bytes 393220
  653.2 48.5 %all-to-all-start.1 = ((f32[8,1,2,64,320]{4,3,2,1,0:T(8,128)}), f32[8,1,2,64,320]{4,3,2,1,0:T(8,128)S(1)}, u32[]{:S(2)}, u32[]{:S(2)}) async-start(f32[8,1,2,64,320]{4,3,2,1,0:T(8,128)} %copy.61), calls=%async_computation.1 | async-start | bytes 3145728 | tf_op jit(solution)/shard_map/all_to_all | solution.py:134
Sparse Core Ops, SparseCore 0:
  44.4 262.1 all-reduce.11
  364.8 284.6 all-reduce.13
where the time goes:
time: 716 us; the launch traced here: 710 us
  waiting for transfers between devices  559 us (78%)
  matrix products  46.1 us (6%)
  blocking collectives  29.1 us (4%)
  starting transfers between devices  23.9 us (3%)
  between operations  23 us (3%)
  local copies, waits for them, and re-layouts  21.4 us (3%)
  other arithmetic  7.74 us (1%)
    psum x1, waiting for transfers between devices, local(): sinogram_derivative = lax.psum(blank_detector, 'slab')  285 us
    psum x1, waiting for transfers between devices, local(): sinogram_views = lax.psum(partial_value, 'slab')  254 us
    psum x1, blocking collectives, local(): across = lax.psum(probe_gradient_total, 'angle')  29.1 us
    all_to_all x1, waiting for transfers between devices, local(): lax.all_to_all(blocks, 'angle', split_axis=0, concat_axis=0, tiled=True)  19.7 us
  transfers between devices with their start and end apart: 4, of which 3 were waited for; matrix products, arithmetic and copies ran while one was open for 1% of the time, Pallas kernels for 0%

commit v1 on v0

v1 whole, which is shorter than its diff:
```python
import numpy as np

import jax
import jax.numpy as jnp
from jax import lax
from jax.sharding import Mesh
from jax.sharding import PartitionSpec as P

NY, NZ, NX, NC = 4, 16, 4, 2
NA = NX * NC
NUB, UB, SIDE, DET = 5, 64, 256, 320
QC = UB // NY
LANES = 2 * DET
SLAB = ("y", "z")
ANGLE = ("x", "core")
HIGH = lax.Precision.HIGH


def dft_tables():
    k = np.arange(SIDE)
    ph = (k[:, None] * k[None, :] % SIDE) * (2.0 * np.pi / SIDE)
    c, s = np.cos(ph) / np.sqrt(SIDE), np.sin(ph) / np.sqrt(SIDE)
    fwd = np.block([[c, -s], [s, c]])
    return fwd.astype(np.float32)


def exchange(x, axes):
    return lax.all_to_all(x, axes, split_axis=0, concat_axis=0, tiled=True)


def to_tiles(q):
    n = q.shape[0] // 8
    return q.reshape(n, 8, 5, 128).transpose(0, 2, 1, 3).reshape(n * 5, 8, 128)


def from_tiles(t):
    n = t.shape[0] // 5
    return t.reshape(n, 5, 8, 128).transpose(0, 2, 1, 3).reshape(n * 8, LANES)


def sum_over_z(tiles):
    padded = jnp.pad(tiles, ((0, 14), (0, 0), (0, 0))).reshape(NZ, 4, 8, 128)
    mine = exchange(padded, "z").sum(0)
    copies = jnp.broadcast_to(mine[None], (NZ, 4, 8, 128))
    return exchange(copies, "z").reshape(64, 8, 128)[:50]


def local(volume, matrices, tile_ids, modes, corners, power):
    y, z = lax.axis_index("y"), lax.axis_index("z")
    angle = lax.axis_index(ANGLE)
    tile = volume.reshape(2, 128, DET).transpose(1, 0, 2).reshape(128, LANES)
    kern = matrices.reshape(NA, NY, QC, 128).transpose(1, 0, 2, 3).reshape(512, 128)
    ids = lax.dynamic_index_in_dim(tile_ids, angle, 0, keepdims=False)
    ids = lax.dynamic_index_in_dim(ids.reshape(NY, NZ, NA), z, 1, keepdims=False).reshape(32)

    rays = jnp.dot(kern, tile, preferred_element_type=jnp.float32).reshape(32, QC, LANES)
    items = exchange(rays, ("y", "x", "core"))
    quarter = jnp.stack(
        [jnp.sum(jnp.where((ids == d)[:, None, None], items, 0.0), axis=0) for d in range(NUB)]
    )
    summed = sum_over_z(to_tiles(quarter.reshape(NUB * QC, LANES)))
    every = lax.all_gather(summed, "y", axis=0, tiled=False)
    det = from_tiles(every.reshape(200, 8, 128))
    det = det.reshape(NY, NUB, QC, LANES).transpose(1, 0, 2, 3).reshape(DET, LANES)

    col, row = corners[0, 0, 0], corners[0, 0, 1]
    wins = [lax.dynamic_slice(det, (col - 1, k * DET + row - 1), (SIDE + 2, SIDE + 2)) for k in range(2)]
    p0, p1 = wins[0][1:-1, 1:-1], wins[1][1:-1, 1:-1]
    absorb = jnp.exp(-p1)
    tr, ti = absorb * jnp.cos(p0), absorb * jnp.sin(p0)
    probe = modes.astype(jnp.float32)
    pr, pi = probe[:, 0], probe[:, 1]
    er, ei = pr * tr - pi * ti, pr * ti + pi * tr

    fwd = jnp.asarray(dft_tables())
    ex = jnp.concatenate([er, ei], axis=2).reshape(4 * SIDE, 2 * SIDE)
    mid = jnp.dot(ex, fwd, precision=HIGH).reshape(4, SIDE, 2, SIDE)
    mid = mid.transpose(2, 1, 0, 3).reshape(2 * SIDE, 4 * SIDE)
    far = lax.dot_general(fwd, mid, (((0,), (0,)), ((), ())), precision=HIGH)
    fr, fi = far[:SIDE].reshape(SIDE, 4, SIDE), far[SIDE:].reshape(SIDE, 4, SIDE)
    resid = jnp.sum(fr * fr + fi * fi, axis=1) - power[0, 0]
    pull = far.reshape(2, SIDE, 4, SIDE) * (2.0 * resid)[None, :, None, :]
    back = jnp.dot(fwd, pull.reshape(2 * SIDE, 4 * SIDE), precision=HIGH)
    back = back.reshape(2, SIDE, 4, SIDE).transpose(2, 1, 0, 3).reshape(4 * SIDE, 2 * SIDE)
    g = lax.dot_general(back, fwd, (((1,), (1,)), ((), ())), precision=HIGH).reshape(4, SIDE, 2, SIDE)
    gr, gi = g[:, :, 0], g[:, :, 1]
    qr, qi = tr * gr + ti * gi, tr * gi - ti * gr
    grads = [
        jnp.sum(pr * qi - pi * qr, axis=0),
        -jnp.sum(pr * qr + pi * qi, axis=0),
    ]

    d_col = sum(jnp.sum(g_ * (w[2:, 1:-1] - w[:-2, 1:-1])) for g_, w in zip(grads, wins))
    d_row = sum(jnp.sum(g_ * (w[1:-1, 2:] - w[1:-1, :-2])) for g_, w in zip(grads, wins))
    locus = (jnp.stack([d_col, d_row]) * (0.5 / SIDE))[None, None]

    terms = jnp.stack([qr, qi], axis=1).reshape(NA, SIDE, SIDE)
    piece = exchange(terms, ANGLE).sum(0).reshape(64, 8, 128)
    piece = exchange(piece, SLAB).sum(0)
    probe_grad = lax.all_gather(piece, ANGLE, axis=0, tiled=False).reshape(4, 2, 4, SIDE)

    pad = DET - SIDE
    placed = jnp.concatenate(
        [
            lax.dynamic_slice(jnp.pad(g_, pad), (pad - col, pad - row), (DET, DET))
            for g_ in grads
        ],
        axis=1,
    )
    placed = placed.reshape(NUB, NY, QC, LANES).transpose(1, 0, 2, 3).reshape(DET, LANES)
    part = exchange(to_tiles(placed).reshape(NY, 50, 8, 128), "y").sum(0)
    quarter = from_tiles(sum_over_z(part)).reshape(NUB, QC, LANES)
    sent = quarter[0][None]
    for d in range(1, NUB):
        sent = jnp.where((ids == d)[:, None, None], quarter[d][None], sent)
    blocks = exchange(sent, ("y", "x", "core")).reshape(512, LANES)
    vol = lax.dot_general(
        kern.astype(jnp.float32), blocks, (((0,), (0,)), ((), ())), precision=HIGH
    )
    vol_grad = vol.reshape(128, 2, DET).transpose(1, 0, 2).reshape(2, 8, 16, DET)
    return vol_grad, probe_grad, resid[None, None], locus


def solution(mesh):
    mesh = Mesh(mesh.devices.reshape(NY, NZ, NX, NC), ("y", "z", "x", "core"))
    in_specs = (
        P(None, SLAB, ANGLE, None),
        P(),
        P(),
        P(),
        P(ANGLE, SLAB, None),
        P(ANGLE, SLAB, None, None),
    )
    out_specs = (
        P(None, SLAB, ANGLE, None),
        P(None, None, SLAB, None),
        P(ANGLE, SLAB, None, None),
        P(ANGLE, SLAB, None),
    )
    return jax.shard_map(local, mesh=mesh, in_specs=in_specs, out_specs=out_specs, check_vma=False)
```

time: 716 us -> 295 us (0.41)
  waiting for transfers between devices: 559 us -> 88.5 us
  starting transfers between devices: 23.9 us -> 67.6 us
  blocking collectives: 29.1 us -> 70.8 us
  matrix products: 46.1 us -> 13.2 us
  between operations: 23 us -> 10.1 us
  other arithmetic: 7.74 us -> 15.2 us
    psum x2 -> x0, waiting for transfers between devices: 539 us -> none  [the longest x1 285 us: local(): sinogram_derivative = lax.psum(blank_detector, 'slab')]
    all_to_all x2 -> x7, waiting for transfers between devices: 19.7 us -> 88.5 us  [exchange(): return lax.all_to_all(x, axes, split_axis=0, concat_axis=0, tiled=True)]
    all_to_all x2 -> x7, starting transfers between devices: 23.9 us -> 67.6 us  [exchange(): return lax.all_to_all(x, axes, split_axis=0, concat_axis=0, tiled=True)]
    all_to_all x0 -> x2, blocking collectives: none -> 36.4 us  [exchange(): return lax.all_to_all(x, axes, split_axis=0, concat_axis=0, tiled=True)]
    all_gather x0 -> x2, blocking collectives: none -> 34.5 us  [the longest x1 21 us: local(): lax.all_gather(piece, ANGLE, axis=0, tiled=False).reshape(4, 2, 4, SIDE)]
    dot_general x20 -> x6, matrix products: 46.1 us -> 13.2 us  [the longest x1 3.84 us: local(): lax.dot_general(back, fwd, (((1,), (1,)), ((), ())), precision=HIGH)]
    psum x1 -> x0, blocking collectives: 29.1 us -> none  [local(): across = lax.psum(probe_gradient_total, 'angle')]
    dynamic_update_slice x1 -> x0, local copies, waits for them, and re-layouts: 7.34 us -> none  [local(): lax.dynamic_update_slice(blank_detector, current + patch_grad, (zero_inde...]
  transfers between devices with their start and end apart: 4 -> 7, of which waited for: 3 -> 6; matrix products, arithmetic and copies ran while one was open for 1% -> 3% of each run, Pallas kernels for 0% -> 0%
where the time goes in v1:
time: 295 us; the launch traced here: 294 us
  waiting for transfers between devices  88.5 us (30%)
  blocking collectives  70.8 us (24%)
  starting transfers between devices  67.6 us (23%)
  local copies, waits for them, and re-layouts  28.5 us (10%)
  other arithmetic  15.2 us (5%)
  matrix products  13.2 us (4%)
  between operations  10.1 us (3%)
    all_to_all x7, waiting for transfers between devices, exchange(): return lax.all_to_all(x, axes, split_axis=0, concat_axis=0, tiled=True)  88.5 us
    all_to_all x7, starting transfers between devices, exchange(): return lax.all_to_all(x, axes, split_axis=0, concat_axis=0, tiled=True)  67.6 us
    all_to_all x2, blocking collectives, exchange(): return lax.all_to_all(x, axes, split_axis=0, concat_axis=0, tiled=True)  36.4 us
    all_gather x1, blocking collectives, local(): lax.all_gather(piece, ANGLE, axis=0, tiled=False).reshape(4, 2, 4, SIDE)  21 us
    all_gather x1, blocking collectives, local(): every = lax.all_gather(summed, 'y', axis=0, tiled=False)  13.5 us
  transfers between devices with their start and end apart: 7, of which 6 were waited for; matrix products, arithmetic and copies ran while one was open for 3% of the time, Pallas kernels for 0%

profile of v1, /device:TPU:1, one launch (start us, length us, event | category | flops | bytes accessed | tf_op | source)
XLA Modules:
  0.0 293.8 jit_solution(17622046203980061840)
XLA Ops:
  2.7 1.4 fusion.23
  4.1 10.4 %all-to-all-start = ((f32[32,16,640]{2,1,0:T(8,128)}), f32[32,16,640]{2,1,0:T(8,128)S(1)}, u32[]{:S(2)}, u32[]{:S(2)}) async-start(f32[32,16,640]{2,1,0:T(8,128)} %fusion.23), calls=%async_computation | async-start | bytes 2621440 | tf_op jit(solution)/shard_map/all_to_all | solution.py:28
  15.3 18.6 %all-to-all-done = f32[32,16,640]{2,1,0:T(8,128)S(1)} async-done(((f32[32,16,640]{2,1,0:T(8,128)}), f32[32,16,640]{2,1,0:T(8,128)S(1)}, u32[]{:S(2)}, u32[]{:S(2)}) %all-to-all-start) | async-done | bytes 1310752 | tf_op jit(solution)/shard_map/all_to_all | solution.py:28
  34.6 25.5 %all_to_all.45 = f32[16,4,8,128]{3,2,1,0:T(8,128)S(1)} all-to-all(f32[16,4,8,128]{3,2,1,0:T(8,128)S(1)} %bitcast.206), channel_id=1, replica_groups=mesh['y'=4,'z'=16,'x'=4,'core'=2] {'z'}, dimensions={0} | all-to-all | bytes 524288 | tf_op jit(solution)/shard_map/all_to_all | solution.py:28
  60.8 10.8 %all-to-all-start.2 = ((f32[16,4,8,128]{3,2,1,0:T(8,128)}), f32[16,4,8,128]{3,2,1,0:T(8,128)S(1)}, u32[]{:S(2)}, u32[]{:S(2)}) async-start(f32[16,4,8,128]{3,2,1,0:T(8,128)} %broadcast_in_dim.136), calls=%async_computation.2 | async-start | bytes 524288 | tf_op jit(solution)/shard_map/all_to_all | solution.py:28
  78.7 1.4 copy_convert_fusion
  80.2 4.2 %all-to-all-done.2 = f32[16,4,8,128]{3,2,1,0:T(8,128)S(1)} async-done(((f32[16,4,8,128]{3,2,1,0:T(8,128)}), f32[16,4,8,128]{3,2,1,0:T(8,128)S(1)}, u32[]{:S(2)}, u32[]{:S(2)}) %all-to-all-start.2) | async-done | bytes 262176 | tf_op jit(solution)/shard_map/all_to_all | solution.py:28
  84.4 13.5 %all-gather = f32[200,8,128]{2,1,0:T(8,128)S(1)} all-gather(f32[50,8,128]{2,1,0:T(8,128)S(1)} %slice.106), channel_id=2, replica_groups=mesh['y'=4,'z'=16,'x'=4,'core'=2] {'y'}, dimensions={0}, use_global_device_ids=true | all-gather | bytes 1024000 | tf_op jit(solution)/shard_map/all_gather | solution.py:62
  100.4 1.9 fusion.5
  102.2 1.4 copy.109
  104.8 2.0 fusion.24
  108.0 2.7 add.110
  110.7 2.5 reduce_sum.161
  115.8 3.2 %fusion.3 = f32[512,1024]{1,0:T(8,128)} fusion(f32[512,512]{1,0:T(8,128)S(1)} %copy-done.4, f32[512,1024]{1,0:T(8,128)S(1)} %fusion.24, f32[512,1024]{1,0:T(8,128)S(1)} %bitcast.193), kind=kOutput, calls=%fused_computation.5 | convolution fusion | flops 1611137024 | bytes 7340032 | tf_op jit(solution)/shard_map/dot_general | solution.py:83
  119.0 2.4 reshape.274
  121.4 2.9 copy.110
  124.3 3.9 %reshape.293 = f32[4,256,512,1]{2,1,0,3:T(8,128)} reshape(f32[4,256,2,256]{3,2,1,0:T(2,128)} %copy.110) | data formatting | bytes 4194304 | tf_op jit(solution)/shard_map/dot_general | solution.py:85
  128.3 3.8 %fusion.25 = f32[4,256,2,256]{3,1,0,2:T(8,128)S(1)} fusion(f32[4,256,512,1]{2,1,0,3:T(8,128)} %reshape.293, f32[2,256,512,1]{2,1,3,0:T(8,128)} %constant.90), kind=kOutput, calls=%fused_computation.80 | convolution fusion | flops 1610612736 | bytes 5242880 | tf_op jit(solution)/shard_map/dot_general | solution.py:85
  134.6 10.9 %all_to_all.46 = f32[4,50,8,128]{3,2,1,0:T(8,128)S(1)} all-to-all(f32[4,50,8,128]{3,2,1,0:T(8,128)S(1)} %bitcast.201), channel_id=1, replica_groups=mesh['y'=4,'z'=16,'x'=4,'core'=2] {'y'}, dimensions={0} | all-to-all | bytes 1638400 | tf_op jit(solution)/shard_map/all_to_all | solution.py:28
  146.2 1.6 pad.17
  147.9 9.8 %all-to-all-start.4 = ((f32[16,4,8,128]{3,2,1,0:T(8,128)}), f32[16,4,8,128]{3,2,1,0:T(8,128)S(1)}, u32[]{:S(2)}, u32[]{:S(2)}) async-start(f32[16,4,8,128]{3,2,1,0:T(8,128)} %bitcast.49), calls=%async_computation.4 | async-start | bytes 524288 | tf_op jit(solution)/shard_map/all_to_all | solution.py:28
  158.1 1.5 copy.116
  159.6 10.9 %all-to-all-done.4 = f32[16,4,8,128]{3,2,1,0:T(8,128)S(1)} async-done(((f32[16,4,8,128]{3,2,1,0:T(8,128)}), f32[16,4,8,128]{3,2,1,0:T(8,128)S(1)}, u32[]{:S(2)}, u32[]{:S(2)}) %all-to-all-start.4) | async-done | bytes 262176 | tf_op jit(solution)/shard_map/all_to_all | solution.py:28
  171.2 11.5 %all-to-all-start.7 = ((f32[8,256,256]{2,1,0:T(8,128)}), f32[8,256,256]{2,1,0:T(8,128)S(1)}, u32[]{:S(2)}, u32[]{:S(2)}) async-start(f32[8,256,256]{2,1,0:T(8,128)} %bitcast.194), calls=%async_computation.7 | async-start | bytes 4194304 | tf_op jit(solution)/shard_map/all_to_all | solution.py:28
  183.7 25.3 %all-to-all-done.7 = f32[8,256,256]{2,1,0:T(8,128)S(1)} async-done(((f32[8,256,256]{2,1,0:T(8,128)}), f32[8,256,256]{2,1,0:T(8,128)S(1)}, u32[]{:S(2)}, u32[]{:S(2)}) %all-to-all-start.7) | async-done | bytes 2097184 | tf_op jit(solution)/shard_map/all_to_all | solution.py:28
  209.6 4.3 %all-to-all-start.5 = ((f32[16,4,8,128]{3,2,1,0:T(8,128)}), f32[16,4,8,128]{3,2,1,0:T(8,128)S(1)}, u32[]{:S(2)}, u32[]{:S(2)}) async-start(f32[16,4,8,128]{3,2,1,0:T(8,128)} %broadcast_in_dim.137), calls=%async_computation.5 | async-start | bytes 524288 | tf_op jit(solution)/shard_map/all_to_all | solution.py:28
  214.8 12.0 %all-to-all-done.5 = f32[16,4,8,128]{3,2,1,0:T(8,128)S(1)} async-done(((f32[16,4,8,128]{3,2,1,0:T(8,128)}), f32[16,4,8,128]{3,2,1,0:T(8,128)S(1)}, u32[]{:S(2)}, u32[]{:S(2)}) %all-to-all-start.5) | async-done | bytes 262176 | tf_op jit(solution)/shard_map/all_to_all | solution.py:28
  226.8 12.7 %all-to-all-start.8 = ((f32[64,8,128]{2,1,0:T(8,128)}), f32[64,8,128]{2,1,0:T(8,128)S(1)}, u32[]{:S(2)}, u32[]{:S(2)}) async-start(f32[64,8,128]{2,1,0:T(8,128)} %reshape.284), calls=%async_computation.8 | async-start | bytes 524288 | tf_op jit(solution)/shard_map/all_to_all | solution.py:28
  239.6 1.4 select_select_fusion
  241.0 17.6 %all-to-all-done.8 = f32[64,8,128]{2,1,0:T(8,128)S(1)} async-done(((f32[64,8,128]{2,1,0:T(8,128)}), f32[64,8,128]{2,1,0:T(8,128)S(1)}, u32[]{:S(2)}, u32[]{:S(2)}) %all-to-all-start.8) | async-done | bytes 262176 | tf_op jit(solution)/shard_map/all_to_all | solution.py:28
  258.6 7.9 %all-to-all-start.6 = ((f32[32,16,640]{2,1,0:T(8,128)}), f32[32,16,640]{2,1,0:T(8,128)S(1)}, u32[]{:S(2)}, u32[]{:S(2)}) async-start(f32[32,16,640]{2,1,0:T(8,128)} %select_select_fusion), calls=%async_computation.6 | async-start | bytes 2621440 | tf_op jit(solution)/shard_map/all_to_all | solution.py:28
  270.4 21.0 %all-gather.1 = f32[64,128]{1,0:T(8,128)S(1)} all-gather(f32[8,128]{1,0:T(8,128)S(1)} %reduce_sum.167), channel_id=3, replica_groups=mesh['y'=4,'z'=16,'x'=4,'core'=2] {'x','core'}, dimensions={0}, use_global_device_ids=true | all-gather | bytes 36864 | tf_op jit(solution)/shard_map/all_gather | solution.py:100
  (76 shorter events, 22.7 us)
Async XLA Ops:
  0.6 14.0 %copy-start = (s32[8,64,8]{1,2,0:T(8,128)S(1)}, s32[8,64,8]{1,2,0:T(8,128)}, u32[]{:S(2)}) copy-start(s32[8,64,8]{1,2,0:T(8,128)} %param.9) | copy-start | bytes 49156
  1.6 2.5 copy-start.6
  4.1 29.8 %all-to-all-start = ((f32[32,16,640]{2,1,0:T(8,128)}), f32[32,16,640]{2,1,0:T(8,128)S(1)}, u32[]{:S(2)}, u32[]{:S(2)}) async-start(f32[32,16,640]{2,1,0:T(8,128)} %fusion.23), calls=%async_computation | async-start | bytes 2621440 | tf_op jit(solution)/shard_map/all_to_all | solution.py:28
  14.6 57.1 %copy-start.11 = (s32[1,1,2]{2,1,0:T(1,128)S(1)}, s32[1,1,2]{2,1,0:T(1,128)}, u32[]{:S(2)}) copy-start(s32[1,1,2]{2,1,0:T(1,128)} %param.11) | copy-start | bytes 28
  60.8 23.6 %all-to-all-start.2 = ((f32[16,4,8,128]{3,2,1,0:T(8,128)}), f32[16,4,8,128]{3,2,1,0:T(8,128)S(1)}, u32[]{:S(2)}, u32[]{:S(2)}) async-start(f32[16,4,8,128]{3,2,1,0:T(8,128)} %broadcast_in_dim.136), calls=%async_computation.2 | async-start | bytes 524288 | tf_op jit(solution)/shard_map/all_to_all | solution.py:28
  80.1 19.3 %copy-start.1 = (f32[4,2,256,256]{3,2,0,1:T(8,128)}, f32[4,2,256,256]{3,2,0,1:T(8,128)S(1)}, u32[]{:S(2)}) copy-start(f32[4,2,256,256]{3,2,0,1:T(8,128)S(1)} %copy_convert_fusion) | copy-start | bytes 6291460
  99.1 1.2 copy-start.8
  103.6 1.2 copy-start.3
  114.6 1.2 copy-start.4
  128.3 3.9 %copy-start.2 = (f32[4,2,256,256]{3,2,0,1:T(8,128)S(1)}, f32[4,2,256,256]{3,2,0,1:T(8,128)}, u32[]{:S(2)}) copy-start(f32[4,2,256,256]{3,2,0,1:T(8,128)} %copy-done.1) | copy-start | bytes 6291460
  147.9 22.6 %all-to-all-start.4 = ((f32[16,4,8,128]{3,2,1,0:T(8,128)}), f32[16,4,8,128]{3,2,1,0:T(8,128)S(1)}, u32[]{:S(2)}, u32[]{:S(2)}) async-start(f32[16,4,8,128]{3,2,1,0:T(8,128)} %bitcast.49), calls=%async_computation.4 | async-start | bytes 524288 | tf_op jit(solution)/shard_map/all_to_all | solution.py:28
  170.5 0.7 copy-start.10
  171.2 37.7 %all-to-all-start.7 = ((f32[8,256,256]{2,1,0:T(8,128)}), f32[8,256,256]{2,1,0:T(8,128)S(1)}, u32[]{:S(2)}, u32[]{:S(2)}) async-start(f32[8,256,256]{2,1,0:T(8,128)} %bitcast.194), calls=%async_computation.7 | async-start | bytes 4194304 | tf_op jit(solution)/shard_map/all_to_all | solution.py:28
  209.6 17.2 %all-to-all-start.5 = ((f32[16,4,8,128]{3,2,1,0:T(8,128)}), f32[16,4,8,128]{3,2,1,0:T(8,128)S(1)}, u32[]{:S(2)}, u32[]{:S(2)}) async-start(f32[16,4,8,128]{3,2,1,0:T(8,128)} %broadcast_in_dim.137), calls=%async_computation.5 | async-start | bytes 524288 | tf_op jit(solution)/shard_map/all_to_all | solution.py:28
  226.8 31.7 %all-to-all-start.8 = ((f32[64,8,128]{2,1,0:T(8,128)}), f32[64,8,128]{2,1,0:T(8,128)S(1)}, u32[]{:S(2)}, u32[]{:S(2)}) async-start(f32[64,8,128]{2,1,0:T(8,128)} %reshape.284), calls=%async_computation.8 | async-start | bytes 524288 | tf_op jit(solution)/shard_map/all_to_all | solution.py:28
  239.6 30.0 %copy-start.5 = (f32[256,256]{1,0:T(8,128)S(1)}, f32[256,256]{1,0:T(8,128)}, u32[]{:S(2)}) copy-start(f32[256,256]{1,0:T(8,128)} %reduce_sum.161) | copy-start | bytes 786436
  239.6 30.0 %copy-start.9 = (f32[1,1,256,256]{3,2,1,0:T(8,128)S(1)}, f32[1,1,256,256]{3,2,1,0:T(8,128)}, u32[]{:S(2)}) copy-start(f32[1,1,256,256]{3,2,1,0:T(8,128)} %param.12) | copy-start | bytes 786436
  241.0 51.0 %copy-start.7 = (bf16[4,8,16,128]{3,2,1,0:T(8,128)(2,1)S(1)}, bf16[4,8,16,128]{3,2,1,0:T(8,128)(2,1)}, u32[]{:S(2)}) copy-start(bf16[4,8,16,128]{3,2,1,0:T(8,128)(2,1)} %copy-done.6) | copy-start | bytes 393220
  258.6 33.4 %all-to-all-start.6 = ((f32[32,16,640]{2,1,0:T(8,128)}), f32[32,16,640]{2,1,0:T(8,128)S(1)}, u32[]{:S(2)}, u32[]{:S(2)}) async-start(f32[32,16,640]{2,1,0:T(8,128)} %select_select_fusion), calls=%async_computation.6 | async-start | bytes 2621440 | tf_op jit(solution)/shard_map/all_to_all | solution.py:28

commit v2 on v1

v2 whole, which is shorter than its diff:
```python
import numpy as np

import jax
import jax.numpy as jnp
from jax import lax
from jax.experimental import pallas as pl
from jax.experimental.pallas import tpu as pltpu
from jax.sharding import Mesh
from jax.sharding import PartitionSpec as P

NY, NZ, NX, NC = 4, 16, 4, 2
NA = NX * NC
NUB, UB, SIDE, DET = 5, 64, 256, 320
QC = UB // NY
LANES = 2 * DET
SLAB = ("y", "z")
ANGLE = ("x", "core")
HIGH = lax.Precision.HIGH


def dft_tables():
    k = np.arange(SIDE)
    ph = (k[:, None] * k[None, :] % SIDE) * (2.0 * np.pi / SIDE)
    c, s = np.cos(ph) / np.sqrt(SIDE), np.sin(ph) / np.sqrt(SIDE)
    both = np.stack([c, s, -s])
    hi = both.astype(jnp.bfloat16)
    lo = (both - hi.astype(np.float64)).astype(jnp.bfloat16)
    return np.concatenate([hi, lo])


def split(v):
    hi = v.astype(jnp.bfloat16)
    return hi, (v - hi.astype(jnp.float32)).astype(jnp.bfloat16)


def dot(a, b):
    return jnp.dot(a, b, preferred_element_type=jnp.float32)


def times(v, hi, lo):
    vh, vl = split(v)
    return dot(vh, hi) + dot(vl, hi) + dot(vh, lo)


def of(hi, lo, v):
    vh, vl = split(v)
    return dot(hi, vh) + dot(hi, vl) + dot(lo, vh)


def spot_kernel(core_ref, tr_ref, ti_ref, probe_ref, power_ref, tab_ref, resid_ref, keep_ref, send_ref, grads_ref, far_ref, big_ref):
    for k in range(2):
        for t in range(2):
            for i in range(2):
                for j in range(2):
                    of_s = 0 if i == j else (1 if (i > j) == (t == 0) else 2)
                    big_ref[2 * t + k, i * SIDE : (i + 1) * SIDE, j * SIDE : (j + 1) * SIDE] = tab_ref[3 * k + of_s]
    fwd, bwd = (big_ref[0], big_ref[1]), (big_ref[2], big_ref[3])
    first = core_ref[0] == 0
    resid_ref[...] = -power_ref[...]
    for m in range(4):
        tr, ti = tr_ref[...], ti_ref[...]
        pr, pi = (probe_ref[2 * m + k].astype(jnp.float32) for k in range(2))
        mid = times(jnp.concatenate([pr * tr - pi * ti, pr * ti + pi * tr], axis=1), *fwd)
        far = of(*bwd, jnp.concatenate([mid[:, :SIDE], mid[:, SIDE:]], axis=0))
        far_ref[m] = far
        resid_ref[...] += far[:SIDE] * far[:SIDE] + far[SIDE:] * far[SIDE:]
    grads_ref[...] = jnp.zeros_like(grads_ref)
    for m in range(4):
        tr, ti = tr_ref[...], ti_ref[...]
        pr, pi = (probe_ref[2 * m + k].astype(jnp.float32) for k in range(2))
        twice, far = 2.0 * resid_ref[...], far_ref[m]
        back = of(*fwd, jnp.concatenate([far[:SIDE] * twice, far[SIDE:] * twice], axis=0))
        g = times(jnp.concatenate([back[:SIDE], back[SIDE:]], axis=1), *bwd)
        gr, gi = g[:, :SIDE], g[:, SIDE:]
        qr, qi = tr * gr + ti * gi, tr * gi - ti * gr
        keep_ref[m] = jnp.where(first, qr, qi)
        send_ref[m] = jnp.where(first, qi, qr)
        grads_ref[0] += pr * qi - pi * qr
        grads_ref[1] -= pr * qr + pi * qi


def spot(core, tr, ti, probe, power, tab):
    f32 = jnp.float32
    plane = jax.ShapeDtypeStruct((SIDE, SIDE), f32)
    half = jax.ShapeDtypeStruct((4, SIDE, SIDE), f32)
    vmem = pl.BlockSpec(memory_space=pltpu.VMEM)
    return pl.pallas_call(
        spot_kernel,
        out_shape=(plane, half, half, jax.ShapeDtypeStruct((2, SIDE, SIDE), f32)),
        in_specs=[pl.BlockSpec(memory_space=pltpu.SMEM)] + [vmem] * 5,
        out_specs=(vmem,) * 4,
        scratch_shapes=[
            pltpu.VMEM((4, 2 * SIDE, SIDE), f32),
            pltpu.VMEM((4, 2 * SIDE, 2 * SIDE), jnp.bfloat16),
        ],
        name="spot",
    )(core, tr, ti, probe, power, tab)


def exchange(x, axes):
    return lax.all_to_all(x, axes, split_axis=0, concat_axis=0, tiled=True)


def to_tiles(q):
    n = q.shape[0] // 8
    return q.reshape(n, 8, 5, 128).transpose(0, 2, 1, 3).reshape(n * 5, 8, 128)


def from_tiles(t):
    n = t.shape[0] // 5
    return t.reshape(n, 5, 8, 128).transpose(0, 2, 1, 3).reshape(n * 8, LANES)


def sum_over_z(tiles):
    padded = jnp.pad(tiles, ((0, 14), (0, 0), (0, 0))).reshape(NZ, 4, 8, 128)
    return exchange(padded, "z").sum(0)


def shift(x, axis, size, by):
    return lax.ppermute(x, axis, [(i, (i + by) % size) for i in range(size)])


def step(volume, matrices, tile_ids, modes, corners, power):
    y, z = lax.axis_index("y"), lax.axis_index("z")
    angle = lax.axis_index(ANGLE)
    tile = volume.reshape(2, 128, DET).transpose(1, 0, 2).reshape(128, LANES)
    kern = matrices.reshape(NA, NY, QC, 128).transpose(1, 0, 2, 3).reshape(512, 128)
    ids = lax.dynamic_index_in_dim(tile_ids, angle, 0, keepdims=False)
    ids = lax.dynamic_index_in_dim(ids.reshape(NY, NZ, NA), z, 1, keepdims=False).reshape(32)

    rays = jnp.dot(kern, tile, preferred_element_type=jnp.float32).reshape(32, QC, LANES)
    items = exchange(rays, ("y", "x", "core"))
    quarter = jnp.stack(
        [jnp.sum(jnp.where((ids == d)[:, None, None], items, 0.0), axis=0) for d in range(NUB)]
    )
    mine = sum_over_z(to_tiles(quarter.reshape(NUB * QC, LANES)))
    copies = jnp.broadcast_to(mine[None], (NZ, 4, 8, 128))
    summed = exchange(copies, "z").reshape(64, 8, 128)[:50]
    every = lax.all_gather(summed, "y", axis=0, tiled=False)
    det = from_tiles(every.reshape(200, 8, 128))
    det = det.reshape(NY, NUB, QC, LANES).transpose(1, 0, 2, 3).reshape(DET, LANES)

    col, row = corners[0, 0, 0], corners[0, 0, 1]
    wins = [lax.dynamic_slice(det, (col - 1, k * DET + row - 1), (SIDE + 2, SIDE + 2)) for k in range(2)]
    p0, p1 = wins[0][1:-1, 1:-1], wins[1][1:-1, 1:-1]
    absorb = jnp.exp(-p1)
    tr, ti = absorb * jnp.cos(p0), absorb * jnp.sin(p0)
    core = lax.axis_index("core")
    resid, keep, send, grads = spot(
        core.reshape(1), tr, ti, modes.reshape(8, SIDE, SIDE), power[0, 0], jnp.asarray(dft_tables())
    )

    d_col = sum(jnp.sum(g_ * (w[2:, 1:-1] - w[:-2, 1:-1])) for g_, w in zip((grads[0], grads[1]), wins))
    d_row = sum(jnp.sum(g_ * (w[1:-1, 2:] - w[1:-1, :-2])) for g_, w in zip((grads[0], grads[1]), wins))
    locus = (jnp.stack([d_col, d_row]) * (0.5 / SIDE))[None, None]

    planes = keep + shift(send, "core", NC, 1)
    planes = exchange(planes, "x")
    piece = planes.sum(0).reshape(64, 8, 128)
    piece = exchange(piece, SLAB)
    piece = piece.sum(0)
    probe_grad = lax.all_gather(piece, ANGLE, axis=0, tiled=False).reshape(4, 2, 4, SIDE)

    pad = DET - SIDE
    placed = jnp.concatenate(
        [
            lax.dynamic_slice(jnp.pad(g_, pad), (pad - col, pad - row), (DET, DET))
            for g_ in (grads[0], grads[1])
        ],
        axis=1,
    )
    placed = placed.reshape(NUB, NY, QC, LANES).transpose(1, 0, 2, 3).reshape(DET, LANES)
    placed = to_tiles(placed).reshape(NY, 50, 8, 128)
    part = lax.dynamic_index_in_dim(placed, y, 0, keepdims=False)
    for k in (2, 1, 3):
        part += shift(lax.dynamic_index_in_dim(placed, (y + k) % NY, 0, keepdims=False), "y", NY, k)
    mine = sum_over_z(part)
    quarter = lax.all_gather(mine, "z", axis=0, tiled=True)
    quarter = from_tiles(quarter[:50]).reshape(NUB, QC, LANES)
    sent = quarter[0][None]
    for d in range(1, NUB):
        sent = jnp.where((ids == d)[:, None, None], quarter[d][None], sent)
    blocks = exchange(sent, ("y", "x", "core")).reshape(512, LANES)
    vol = lax.dot_general(
        kern.astype(jnp.float32), blocks, (((0,), (0,)), ((), ())), precision=HIGH
    )
    vol_grad = vol.reshape(128, 2, DET).transpose(1, 0, 2).reshape(2, 8, 16, DET)
    return vol_grad, probe_grad, resid[None, None], locus


def solution(mesh):
    mesh = Mesh(mesh.devices.reshape(NY, NZ, NX, NC), ("y", "z", "x", "core"))
    in_specs = (
        P(None, SLAB, ANGLE, None),
        P(),
        P(),
        P(),
        P(ANGLE, SLAB, None),
        P(ANGLE, SLAB, None, None),
    )
    out_specs = (
        P(None, SLAB, ANGLE, None),
        P(None, None, SLAB, None),
        P(ANGLE, SLAB, None, None),
        P(ANGLE, SLAB, None),
    )
    return jax.shard_map(step, mesh=mesh, in_specs=in_specs, out_specs=out_specs, check_vma=False)
```

time: 295 us -> 265 us (0.90)
  waiting for transfers between devices: 88.5 us -> 65.2 us
  local copies, waits for them, and re-layouts: 28.5 us -> 10.5 us
  Pallas kernels: 0 us -> 12.1 us
  matrix products: 13.2 us -> 2.26 us
  blocking collectives: 70.8 us -> 80.6 us
  other arithmetic: 15.2 us -> 9.18 us
  starting transfers between devices: 67.6 us -> 73.5 us
    all_to_all x7 -> x6, waiting for transfers between devices: 88.5 us -> 65.2 us  [exchange(): return lax.all_to_all(x, axes, split_axis=0, concat_axis=0, tiled=True)]
    all_gather x2 -> x3, blocking collectives: 34.5 us -> 55.2 us  [the longest x1 27.3 us: step(): quarter = lax.all_gather(mine, 'z', axis=0, tiled=True)]
    ppermute x0 -> x4, starting transfers between devices: none -> 20.1 us  [shift(): return lax.ppermute(x, axis, [(i, (i + by) % size) for i in range(size)])]
    all_to_all x7 -> x6, starting transfers between devices: 67.6 us -> 53.4 us  [exchange(): return lax.all_to_all(x, axes, split_axis=0, concat_axis=0, tiled=True)]
    pallas_call x0 -> x1, Pallas kernels: none -> 12.1 us  [spot(): pl.pallas_call(spot_kernel, out_shape=(plane, half, half, jax.ShapeDtypeS...]
    dot_general x6 -> x2, matrix products: 13.2 us -> 2.26 us  [the longest x1 1.4 us: step(): jnp.dot(kern, tile, preferred_element_type=jnp.float32)]
    all_to_all x2 -> x1, blocking collectives: 36.4 us -> 25.5 us  [exchange(): return lax.all_to_all(x, axes, split_axis=0, concat_axis=0, tiled=True)]
    transpose x7 -> x4, local copies, waits for them, and re-layouts: 7.36 us -> 2.99 us  [the longest x1 1.09 us: step(): tile = volume.reshape(2, 128, DET).transpose(1, 0, 2).reshape(128, LANES)]
  transfers between devices with their start and end apart: 7 -> 10, of which waited for: 6 -> 5; matrix products, arithmetic and copies ran while one was open for 3% -> 5% of each run, Pallas kernels for 0% -> 0%
where the time goes in v2:
time: 265 us; the launch traced here: 264 us
  blocking collectives  80.6 us (30%)
  starting transfers between devices  73.5 us (28%)
  waiting for transfers between devices  65.2 us (25%)
  Pallas kernels  12.1 us (5%)
  local copies, waits for them, and re-layouts  10.5 us (4%)
  between operations  10.1 us (4%)
  other arithmetic  9.18 us (3%)
    all_to_all x6, waiting for transfers between devices, exchange(): return lax.all_to_all(x, axes, split_axis=0, concat_axis=0, tiled=True)  65.2 us
    all_to_all x6, starting transfers between devices, exchange(): return lax.all_to_all(x, axes, split_axis=0, concat_axis=0, tiled=True)  53.4 us
    all_gather x1, blocking collectives, step(): quarter = lax.all_gather(mine, 'z', axis=0, tiled=True)  27.3 us
    all_to_all x1, blocking collectives, exchange(): return lax.all_to_all(x, axes, split_axis=0, concat_axis=0, tiled=True)  25.5 us
    ppermute x4, starting transfers between devices, shift(): return lax.ppermute(x, axis, [(i, (i + by) % size) for i in range(size)])  20.1 us
    all_gather x1, blocking collectives, step(): lax.all_gather(piece, ANGLE, axis=0, tiled=False).reshape(4, 2, 4, SIDE)  14.4 us
    all_gather x1, blocking collectives, step(): every = lax.all_gather(summed, 'y', axis=0, tiled=False)  13.4 us
    pallas_call x1, Pallas kernels, spot(): pl.pallas_call(spot_kernel, out_shape=(plane, half, half, jax.ShapeDtypeS...  12.1 us
  transfers between devices with their start and end apart: 10, of which 5 were waited for; matrix products, arithmetic and copies ran while one was open for 5% of the time, Pallas kernels for 0%

profile of v2, /device:TPU:1, one launch (start us, length us, event | category | flops | bytes accessed | tf_op | source)
XLA Modules:
  0.0 263.5 jit_solution(3981246872355247743)
XLA Ops:
  0.6 0.9 copy.72
  1.6 1.1 copy.73
  2.7 1.4 fusion.12
  4.1 10.4 %all-to-all-start = ((f32[32,16,640]{2,1,0:T(8,128)}), f32[32,16,640]{2,1,0:T(8,128)S(1)}, u32[]{:S(2)}, u32[]{:S(2)}) async-start(f32[32,16,640]{2,1,0:T(8,128)} %fusion.12), calls=%async_computation | async-start | bytes 2621440 | tf_op jit(solution)/shard_map/all_to_all | solution.py:101
  15.3 18.7 %all-to-all-done = f32[32,16,640]{2,1,0:T(8,128)S(1)} async-done(((f32[32,16,640]{2,1,0:T(8,128)}), f32[32,16,640]{2,1,0:T(8,128)S(1)}, u32[]{:S(2)}, u32[]{:S(2)}) %all-to-all-start) | async-done | bytes 1310752 | tf_op jit(solution)/shard_map/all_to_all | solution.py:101
  34.5 25.5 %all_to_all.35 = f32[16,4,8,128]{3,2,1,0:T(8,128)S(1)} all-to-all(f32[16,4,8,128]{3,2,1,0:T(8,128)S(1)} %bitcast.132), channel_id=1, replica_groups=mesh['y'=4,'z'=16,'x'=4,'core'=2] {'z'}, dimensions={0} | all-to-all | bytes 524288 | tf_op jit(solution)/shard_map/all_to_all | solution.py:101
  60.8 10.8 %all-to-all-start.2 = ((f32[16,4,8,128]{3,2,1,0:T(8,128)}), f32[16,4,8,128]{3,2,1,0:T(8,128)S(1)}, u32[]{:S(2)}, u32[]{:S(2)}) async-start(f32[16,4,8,128]{3,2,1,0:T(8,128)} %broadcast_in_dim.123), calls=%async_computation.2 | async-start | bytes 524288 | tf_op jit(solution)/shard_map/all_to_all | solution.py:101
  78.7 5.6 %all-to-all-done.2 = f32[16,4,8,128]{3,2,1,0:T(8,128)S(1)} async-done(((f32[16,4,8,128]{3,2,1,0:T(8,128)}), f32[16,4,8,128]{3,2,1,0:T(8,128)S(1)}, u32[]{:S(2)}, u32[]{:S(2)}) %all-to-all-start.2) | async-done | bytes 262176 | tf_op jit(solution)/shard_map/all_to_all | solution.py:101
  84.3 13.4 %all-gather = f32[200,8,128]{2,1,0:T(8,128)S(1)} all-gather(f32[50,8,128]{2,1,0:T(8,128)S(1)} %slice.93), channel_id=2, replica_groups=mesh['y'=4,'z'=16,'x'=4,'core'=2] {'y'}, dimensions={0}, use_global_device_ids=true | all-gather | bytes 1024000 | tf_op jit(solution)/shard_map/all_gather | solution.py:139
  97.9 1.8 sine_multiply_fusion
  99.7 12.1 %spot.1 = (f32[256,256]{1,0:T(8,128)}, f32[4,256,256]{2,1,0:T(8,128)}, f32[4,256,256]{2,1,0:T(8,128)}, f32[2,256,256]{2,1,0:T(8,128)}) custom-call(s32[1]{0:T(128)} %bitcast.core_ref, f32[256,256]{1,0:T(8,128)} %get-tuple-element.25.tr_ref, f32[256,256]{1,0:T(8,128)} %get-tuple-element.24.ti_ref, bf16[8,256,256]{2,1,0:T(8,128)(2,1)} %bitcast.131, ...), custom_call_target="tpu_custom_call" | custom-call | tf_op jit(solution)/shard_map/spot/pallas_call | solution.py:87
  111.8 1.1 slice_bitcast_fusion.1
  113.5 0.9 dynamic-slice_bitcast_fusion.2
  114.3 3.2 %collective-permute-start = (f32[50,8,128]{2,1,0:T(8,128)}, f32[50,8,128]{2,1,0:T(8,128)S(1)}, u32[]{:S(2)}, u32[]{:S(2)}) collective-permute-start(f32[50,8,128]{2,1,0:T(8,128)} %get-tuple-element.21), channel_id=1, source_target_pairs={{0,256},{128,384},{256,0},{384,128},{1,257},{129,385},{257,1},{385... | collective-permute-start | bytes 614408 | tf_op jit(solution)/shard_map/ppermute | solution.py:120
  117.5 2.3 collective-permute-start.1
  119.8 4.2 %collective-permute-start.2 = (f32[50,8,128]{2,1,0:T(8,128)}, f32[50,8,128]{2,1,0:T(8,128)S(1)}, u32[]{:S(2)}, u32[]{:S(2)}) collective-permute-start(f32[50,8,128]{2,1,0:T(8,128)} %get-tuple-element.22), channel_id=1, source_target_pairs={{0,384},{128,0},{256,128},{384,256},{1,385},{129,1},{257,129},{385... | collective-permute-start | bytes 614408 | tf_op jit(solution)/shard_map/ppermute | solution.py:120
  124.1 10.4 %collective-permute-start.3 = (f32[4,256,256]{2,1,0:T(8,128)}, f32[4,256,256]{2,1,0:T(8,128)}, u32[]{:S(2)}, u32[]{:S(2)}) collective-permute-start(f32[4,256,256]{2,1,0:T(8,128)} %get-tuple-element.10), channel_id=1, source_target_pairs={{0,1},{1,0},{2,3},{3,2},{4,5},{5,4},{6,7},{7,6},{8,9},{9,8},{10,11... | collective-permute-start | bytes 3145736 | tf_op jit(solution)/shard_map/ppermute | solution.py:120
  135.3 5.8 %all-to-all-start.3 = ((f32[16,4,8,128]{3,2,1,0:T(8,128)}), f32[16,4,8,128]{3,2,1,0:T(8,128)S(1)}, u32[]{:S(2)}, u32[]{:S(2)}) async-start(f32[16,4,8,128]{3,2,1,0:T(8,128)} %bitcast.49), calls=%async_computation.3 | async-start | bytes 524288 | tf_op jit(solution)/shard_map/all_to_all | solution.py:101
  141.2 2.3 add.143
  143.5 10.4 %all-to-all-done.3 = f32[16,4,8,128]{3,2,1,0:T(8,128)S(1)} async-done(((f32[16,4,8,128]{3,2,1,0:T(8,128)}), f32[16,4,8,128]{3,2,1,0:T(8,128)S(1)}, u32[]{:S(2)}, u32[]{:S(2)}) %all-to-all-start.3) | async-done | bytes 262176 | tf_op jit(solution)/shard_map/all_to_all | solution.py:101
  153.9 3.5 %all-to-all-start.5 = ((f32[4,256,256]{2,1,0:T(8,128)}), f32[4,256,256]{2,1,0:T(8,128)S(1)}, u32[]{:S(2)}, u32[]{:S(2)}) async-start(f32[4,256,256]{2,1,0:T(8,128)} %add.143), calls=%async_computation.5 | async-start | bytes 2097152 | tf_op jit(solution)/shard_map/all_to_all | solution.py:101
  157.4 27.3 %all_gather.17 = f32[64,8,128]{2,1,0:T(8,128)S(1)} all-gather(f32[4,8,128]{2,1,0:T(8,128)S(1)} %reduce_sum.123), channel_id=1, replica_groups=mesh['y'=4,'z'=16,'x'=4,'core'=2] {'z'}, dimensions={0}, use_global_device_ids=true | all-gather | bytes 278528 | tf_op jit(solution)/shard_map/all_gather | solution.py:178
  184.8 1.4 select_select_fusion
  186.2 14.5 %all-to-all-start.4 = ((f32[32,16,640]{2,1,0:T(8,128)}), f32[32,16,640]{2,1,0:T(8,128)S(1)}, u32[]{:S(2)}, u32[]{:S(2)}) async-start(f32[32,16,640]{2,1,0:T(8,128)} %select_select_fusion), calls=%async_computation.4 | async-start | bytes 2621440 | tf_op jit(solution)/shard_map/all_to_all | solution.py:101
  201.5 1.7 reshape.185
  203.2 16.8 %all-to-all-done.4 = f32[32,16,640]{2,1,0:T(8,128)S(1)} async-done(((f32[32,16,640]{2,1,0:T(8,128)}), f32[32,16,640]{2,1,0:T(8,128)S(1)}, u32[]{:S(2)}, u32[]{:S(2)}) %all-to-all-start.4) | async-done | bytes 1310752 | tf_op jit(solution)/shard_map/all_to_all | solution.py:101
  220.0 8.3 %all-to-all-start.6 = ((f32[64,8,128]{2,1,0:T(8,128)}), f32[64,8,128]{2,1,0:T(8,128)S(1)}, u32[]{:S(2)}, u32[]{:S(2)}) async-start(f32[64,8,128]{2,1,0:T(8,128)} %reshape.185), calls=%async_computation.6 | async-start | bytes 524288 | tf_op jit(solution)/shard_map/all_to_all | solution.py:101
  228.2 1.3 fusion.5
  232.8 0.9 fusion.13
  233.7 0.9 copy.78
  234.6 13.8 %all-to-all-done.6 = f32[64,8,128]{2,1,0:T(8,128)S(1)} async-done(((f32[64,8,128]{2,1,0:T(8,128)}), f32[64,8,128]{2,1,0:T(8,128)S(1)}, u32[]{:S(2)}, u32[]{:S(2)}) %all-to-all-start.6) | async-done | bytes 262176 | tf_op jit(solution)/shard_map/all_to_all | solution.py:101
  248.5 14.4 %all-gather.1 = f32[64,128]{1,0:T(8,128)S(1)} all-gather(f32[8,128]{1,0:T(8,128)S(1)} %reduce_sum.125), channel_id=3, replica_groups=mesh['y'=4,'z'=16,'x'=4,'core'=2] {'x','core'}, dimensions={0}, use_global_device_ids=true | all-gather | bytes 36864 | tf_op jit(solution)/shard_map/all_gather | solution.py:162
  (47 shorter events, 6.2 us)
Async XLA Ops:
  0.6 13.9 %copy-start = (s32[8,64,8]{1,2,0:T(8,128)S(1)}, s32[8,64,8]{1,2,0:T(8,128)}, u32[]{:S(2)}) copy-start(s32[8,64,8]{1,2,0:T(8,128)} %param.9) | copy-start | bytes 49156
  4.1 29.8 %all-to-all-start = ((f32[32,16,640]{2,1,0:T(8,128)}), f32[32,16,640]{2,1,0:T(8,128)S(1)}, u32[]{:S(2)}, u32[]{:S(2)}) async-start(f32[32,16,640]{2,1,0:T(8,128)} %fusion.12), calls=%async_computation | async-start | bytes 2621440 | tf_op jit(solution)/shard_map/all_to_all | solution.py:101
  34.4 37.2 %copy-start.3 = (s32[1,1,2]{2,1,0:T(1,128)S(1)}, s32[1,1,2]{2,1,0:T(1,128)}, u32[]{:S(2)}) copy-start(s32[1,1,2]{2,1,0:T(1,128)} %param.11) | copy-start | bytes 28
  60.8 23.6 %all-to-all-start.2 = ((f32[16,4,8,128]{3,2,1,0:T(8,128)}), f32[16,4,8,128]{3,2,1,0:T(8,128)S(1)}, u32[]{:S(2)}, u32[]{:S(2)}) async-start(f32[16,4,8,128]{3,2,1,0:T(8,128)} %broadcast_in_dim.123), calls=%async_computation.2 | async-start | bytes 524288 | tf_op jit(solution)/shard_map/all_to_all | solution.py:101
  114.3 26.8 %copy-start.2 = (f32[4,256,256]{2,1,0:T(8,128)S(1)}, f32[4,256,256]{2,1,0:T(8,128)}, u32[]{:S(2)}) copy-start(f32[4,256,256]{2,1,0:T(8,128)} %get-tuple-element.9) | copy-start | bytes 3145732
  114.3 20.2 %collective-permute-start = (f32[50,8,128]{2,1,0:T(8,128)}, f32[50,8,128]{2,1,0:T(8,128)S(1)}, u32[]{:S(2)}, u32[]{:S(2)}) collective-permute-start(f32[50,8,128]{2,1,0:T(8,128)} %get-tuple-element.21), channel_id=1, source_target_pairs={{0,256},{128,384},{256,0},{384,128},{1,257},{129,385},{257,1},{385... | collective-permute-start | bytes 614408 | tf_op jit(solution)/shard_map/ppermute | solution.py:120
  117.5 17.0 %collective-permute-start.1 = (f32[50,8,128]{2,1,0:T(8,128)}, f32[50,8,128]{2,1,0:T(8,128)S(1)}, u32[]{:S(2)}, u32[]{:S(2)}) collective-permute-start(f32[50,8,128]{2,1,0:T(8,128)} %get-tuple-element.23), channel_id=1, source_target_pairs={{0,128},{128,256},{256,384},{384,0},{1,129},{129,257},{257,385},{3... | collective-permute-start | bytes 614408 | tf_op jit(solution)/shard_map/ppermute | solution.py:120
  119.8 14.7 %collective-permute-start.2 = (f32[50,8,128]{2,1,0:T(8,128)}, f32[50,8,128]{2,1,0:T(8,128)S(1)}, u32[]{:S(2)}, u32[]{:S(2)}) collective-permute-start(f32[50,8,128]{2,1,0:T(8,128)} %get-tuple-element.22), channel_id=1, source_target_pairs={{0,384},{128,0},{256,128},{384,256},{1,385},{129,1},{257,129},{385... | collective-permute-start | bytes 614408 | tf_op jit(solution)/shard_map/ppermute | solution.py:120
  124.1 17.1 %collective-permute-start.3 = (f32[4,256,256]{2,1,0:T(8,128)}, f32[4,256,256]{2,1,0:T(8,128)}, u32[]{:S(2)}, u32[]{:S(2)}) collective-permute-start(f32[4,256,256]{2,1,0:T(8,128)} %get-tuple-element.10), channel_id=1, source_target_pairs={{0,1},{1,0},{2,3},{3,2},{4,5},{5,4},{6,7},{7,6},{8,9},{9,8},{10,11... | collective-permute-start | bytes 3145736 | tf_op jit(solution)/shard_map/ppermute | solution.py:120
  135.3 18.6 %all-to-all-start.3 = ((f32[16,4,8,128]{3,2,1,0:T(8,128)}), f32[16,4,8,128]{3,2,1,0:T(8,128)S(1)}, u32[]{:S(2)}, u32[]{:S(2)}) async-start(f32[16,4,8,128]{3,2,1,0:T(8,128)} %bitcast.49), calls=%async_computation.3 | async-start | bytes 524288 | tf_op jit(solution)/shard_map/all_to_all | solution.py:101
  153.9 32.3 %all-to-all-start.5 = ((f32[4,256,256]{2,1,0:T(8,128)}), f32[4,256,256]{2,1,0:T(8,128)S(1)}, u32[]{:S(2)}, u32[]{:S(2)}) async-start(f32[4,256,256]{2,1,0:T(8,128)} %add.143), calls=%async_computation.5 | async-start | bytes 2097152 | tf_op jit(solution)/shard_map/all_to_all | solution.py:101
  186.2 33.8 %all-to-all-start.4 = ((f32[32,16,640]{2,1,0:T(8,128)}), f32[32,16,640]{2,1,0:T(8,128)S(1)}, u32[]{:S(2)}, u32[]{:S(2)}) async-start(f32[32,16,640]{2,1,0:T(8,128)} %select_select_fusion), calls=%async_computation.4 | async-start | bytes 2621440 | tf_op jit(solution)/shard_map/all_to_all | solution.py:101
  201.5 26.8 %copy-start.1 = (f32[2,256,256]{2,1,0:T(8,128)S(1)}, f32[2,256,256]{2,1,0:T(8,128)}, u32[]{:S(2)}) copy-start(f32[2,256,256]{2,1,0:T(8,128)} %get-tuple-element.8) | copy-start | bytes 1572868
  220.0 28.5 %all-to-all-start.6 = ((f32[64,8,128]{2,1,0:T(8,128)}), f32[64,8,128]{2,1,0:T(8,128)S(1)}, u32[]{:S(2)}, u32[]{:S(2)}) async-start(f32[64,8,128]{2,1,0:T(8,128)} %reshape.185), calls=%async_computation.6 | async-start | bytes 524288 | tf_op jit(solution)/shard_map/all_to_all | solution.py:101

commit v3 on v2

--- a/solution.py
+++ b/solution.py
@@ -13,6 +13,7 @@
 NUB, UB, SIDE, DET = 5, 64, 256, 320
 QC = UB // NY
 LANES = 2 * DET
+LIMIT = 16 << 20
 SLAB = ("y", "z")
 ANGLE = ("x", "core")
 HIGH = lax.Precision.HIGH
@@ -47,7 +48,7 @@
     return dot(hi, vh) + dot(hi, vl) + dot(lo, vh)
 
 
-def spot_kernel(core_ref, tr_ref, ti_ref, probe_ref, power_ref, tab_ref, resid_ref, keep_ref, send_ref, grads_ref, far_ref, big_ref):
+def spot_kernel(where_ref, tr_ref, ti_ref, probe_ref, power_ref, tab_ref, resid_ref, keep_ref, send_ref, grads_ref, placed_ref, far_ref, big_ref, det_ref):
     for k in range(2):
         for t in range(2):
             for i in range(2):
@@ -55,7 +56,7 @@
                     of_s = 0 if i == j else (1 if (i > j) == (t == 0) else 2)
                     big_ref[2 * t + k, i * SIDE : (i + 1) * SIDE, j * SIDE : (j + 1) * SIDE] = tab_ref[3 * k + of_s]
     fwd, bwd = (big_ref[0], big_ref[1]), (big_ref[2], big_ref[3])
-    first = core_ref[0] == 0
+    first = where_ref[0] == 0
     resid_ref[...] = -power_ref[...]
     for m in range(4):
         tr, ti = tr_ref[...], ti_ref[...]
@@ -77,24 +78,46 @@
         send_ref[m] = jnp.where(first, qi, qr)
         grads_ref[0] += pr * qi - pi * qr
         grads_ref[1] -= pr * qr + pi * qi
-
-
-def spot(core, tr, ti, probe, power, tab):
+    col, row = where_ref[1], where_ref[2]
+    blank = jnp.zeros((SIDE, 128), jnp.float32)
+    g0 = pltpu.roll(jnp.concatenate([grads_ref[0], blank], axis=1), row, 1)
+    g1 = pltpu.roll(jnp.concatenate([grads_ref[1], blank], axis=1), row + 64, 1)
+    det_ref[...] = jnp.zeros_like(det_ref)
+    wide = jnp.concatenate([g0[:, :256], g0[:, 256:] + g1[:, :128], g1[:, 128:]], axis=1)
+    wide = jnp.concatenate([wide, jnp.zeros((8, LANES), jnp.float32)], axis=0)
+    start = pl.multiple_of((col >> 3) << 3, 8)
+    det_ref[pl.ds(start, SIDE + 8), :] = pltpu.roll(wide, col & 7, 0)
+    for y in range(NY):
+        for g in range(10):
+            at = (g // 2) * UB + y * QC + (g % 2) * 8
+            for t in range(5):
+                placed_ref[y, g * 5 + t] = det_ref[at : at + 8, t * 128 : (t + 1) * 128]
+
+
+def spot(where, tr, ti, probe, power, tab):
     f32 = jnp.float32
     plane = jax.ShapeDtypeStruct((SIDE, SIDE), f32)
     half = jax.ShapeDtypeStruct((4, SIDE, SIDE), f32)
     vmem = pl.BlockSpec(memory_space=pltpu.VMEM)
     return pl.pallas_call(
         spot_kernel,
-        out_shape=(plane, half, half, jax.ShapeDtypeStruct((2, SIDE, SIDE), f32)),
+        out_shape=(
+            plane,
+            half,
+            half,
+            jax.ShapeDtypeStruct((2, SIDE, SIDE), f32),
+            jax.ShapeDtypeStruct((NY, 50, 8, 128), f32),
+        ),
         in_specs=[pl.BlockSpec(memory_space=pltpu.SMEM)] + [vmem] * 5,
-        out_specs=(vmem,) * 4,
+        out_specs=(vmem,) * 5,
         scratch_shapes=[
             pltpu.VMEM((4, 2 * SIDE, SIDE), f32),
             pltpu.VMEM((4, 2 * SIDE, 2 * SIDE), jnp.bfloat16),
+            pltpu.VMEM((DET, LANES), f32),
         ],
+        compiler_params=pltpu.CompilerParams(vmem_limit_bytes=LIMIT),
         name="spot",
-    )(core, tr, ti, probe, power, tab)
+    )(where, tr, ti, probe, power, tab)
 
 
 def exchange(x, axes):
@@ -111,9 +134,12 @@
     return t.reshape(n, 5, 8, 128).transpose(0, 2, 1, 3).reshape(n * 8, LANES)
 
 
-def sum_over_z(tiles):
-    padded = jnp.pad(tiles, ((0, 14), (0, 0), (0, 0))).reshape(NZ, 4, 8, 128)
-    return exchange(padded, "z").sum(0)
+def chunks_of_z(tiles):
+    return jnp.pad(tiles, ((0, 14), (0, 0), (0, 0))).reshape(NZ, 4, 8, 128)
+
+
+def pick(x, i, n):
+    return lax.dynamic_index_in_dim(x, i % n, 0, keepdims=False)
 
 
 def shift(x, axis, size, by):
@@ -133,7 +159,7 @@
     quarter = jnp.stack(
         [jnp.sum(jnp.where((ids == d)[:, None, None], items, 0.0), axis=0) for d in range(NUB)]
     )
-    mine = sum_over_z(to_tiles(quarter.reshape(NUB * QC, LANES)))
+    mine = exchange(chunks_of_z(to_tiles(quarter.reshape(NUB * QC, LANES))), "z").sum(0)
     copies = jnp.broadcast_to(mine[None], (NZ, 4, 8, 128))
     summed = exchange(copies, "z").reshape(64, 8, 128)[:50]
     every = lax.all_gather(summed, "y", axis=0, tiled=False)
@@ -146,41 +172,35 @@
     absorb = jnp.exp(-p1)
     tr, ti = absorb * jnp.cos(p0), absorb * jnp.sin(p0)
     core = lax.axis_index("core")
-    resid, keep, send, grads = spot(
-        core.reshape(1), tr, ti, modes.reshape(8, SIDE, SIDE), power[0, 0], jnp.asarray(dft_tables())
+    resid, keep, send, grads, placed = spot(
+        jnp.stack([core, col, row]), tr, ti, modes.reshape(8, SIDE, SIDE), power[0, 0], jnp.asarray(dft_tables())
     )
 
     d_col = sum(jnp.sum(g_ * (w[2:, 1:-1] - w[:-2, 1:-1])) for g_, w in zip((grads[0], grads[1]), wins))
     d_row = sum(jnp.sum(g_ * (w[1:-1, 2:] - w[1:-1, :-2])) for g_, w in zip((grads[0], grads[1]), wins))
     locus = (jnp.stack([d_col, d_row]) * (0.5 / SIDE))[None, None]
 
-    planes = keep + shift(send, "core", NC, 1)
-    planes = exchange(planes, "x")
-    piece = planes.sum(0).reshape(64, 8, 128)
-    piece = exchange(piece, SLAB)
-    piece = piece.sum(0)
-    probe_grad = lax.all_gather(piece, ANGLE, axis=0, tiled=False).reshape(4, 2, 4, SIDE)
-
-    pad = DET - SIDE
-    placed = jnp.concatenate(
-        [
-            lax.dynamic_slice(jnp.pad(g_, pad), (pad - col, pad - row), (DET, DET))
-            for g_ in (grads[0], grads[1])
-        ],
-        axis=1,
-    )
-    placed = placed.reshape(NUB, NY, QC, LANES).transpose(1, 0, 2, 3).reshape(DET, LANES)
-    placed = to_tiles(placed).reshape(NY, 50, 8, 128)
-    part = lax.dynamic_index_in_dim(placed, y, 0, keepdims=False)
-    for k in (2, 1, 3):
-        part += shift(lax.dynamic_index_in_dim(placed, (y + k) % NY, 0, keepdims=False), "y", NY, k)
-    mine = sum_over_z(part)
-    quarter = lax.all_gather(mine, "z", axis=0, tiled=True)
-    quarter = from_tiles(quarter[:50]).reshape(NUB, QC, LANES)
+    other = shift(send, "core", NC, 1)
+    planes = keep + other
+    got = [shift(pick(planes, lax.axis_index("x") + k, NX), "x", NX, k) for k in (2, 1, 3)]
+    rows = (pick(planes, lax.axis_index("x"), NX) + got[0] + got[1] + got[2]).reshape(NY, 64, SIDE)
+    got = [shift(pick(rows, y + k, NY), "y", NY, k) for k in (2, 1, 3)]
+    rows = (pick(rows, y, NY) + got[0] + got[1] + got[2]).reshape(NZ, 1, 8, 128)
+
+    part = exchange(placed, "y")
+    part = part.sum(0)
+    part = exchange(chunks_of_z(part), "z")
+    mine = part.sum(0)
+    got = exchange(jnp.concatenate([jnp.broadcast_to(mine[None], (NZ, 4, 8, 128)), rows], axis=1), "z")
+    piece = got[:, 4].sum(0)
+    quarter = got[:, :4].reshape(64, 8, 128)[:50].reshape(NUB, 10, 8, 128)
     sent = quarter[0][None]
     for d in range(1, NUB):
-        sent = jnp.where((ids == d)[:, None, None], quarter[d][None], sent)
-    blocks = exchange(sent, ("y", "x", "core")).reshape(512, LANES)
+        sent = jnp.where((ids == d)[:, None, None, None], quarter[d][None], sent)
+    sent = jnp.concatenate([sent, jnp.broadcast_to(piece[None, None], (32, 1, 8, 128))], axis=1)
+    got = exchange(sent, ("y", "x", "core"))
+    probe_grad = lax.dynamic_slice_in_dim(got[:, 10], y * NA, NA, 0).reshape(4, 2, 4, SIDE)
+    blocks = from_tiles(got[:, :10].reshape(320, 8, 128))
     vol = lax.dot_general(
         kern.astype(jnp.float32), blocks, (((0,), (0,)), ((), ())), precision=HIGH
     )

time: 265 us -> 246 us (0.928)
  blocking collectives: 80.6 us -> 63.3 us
  other arithmetic: 9.18 us -> 11.9 us
    all_gather x2 -> x0, blocking collectives: 41.7 us -> none  [the longest x1 27.3 us: step(): quarter = lax.all_gather(mine, 'z', axis=0, tiled=True)]
    all_to_all x1 -> x2, blocking collectives: 25.5 us -> 49.9 us  [exchange(): return lax.all_to_all(x, axes, split_axis=0, concat_axis=0, tiled=True)]
    all_to_all x6 -> x5, waiting for transfers between devices: 65.2 us -> 54.4 us  [exchange(): return lax.all_to_all(x, axes, split_axis=0, concat_axis=0, tiled=True)]
    ppermute x4 -> x7, waiting for transfers between devices: 0.01 us -> 8.41 us  [shift(): return lax.ppermute(x, axis, [(i, (i + by) % size) for i in range(size)])]
    ppermute x4 -> x7, starting transfers between devices: 20.1 us -> 28.5 us  [shift(): return lax.ppermute(x, axis, [(i, (i + by) % size) for i in range(size)])]
    all_to_all x6 -> x5, starting transfers between devices: 53.4 us -> 46.6 us  [exchange(): return lax.all_to_all(x, axes, split_axis=0, concat_axis=0, tiled=True)]
  transfers between devices with their start and end apart: 10 -> 12, of which waited for: 5 -> 7; matrix products, arithmetic and copies ran while one was open for 5% -> 5% of each run, Pallas kernels for 0% -> 0%
where the time goes in v3:
time: 246 us; the launch traced here: 245 us
  starting transfers between devices  75.1 us (31%)
  blocking collectives  63.3 us (26%)
  waiting for transfers between devices  62.8 us (26%)
  other arithmetic  11.9 us (5%)
  local copies, waits for them, and re-layouts  10.9 us (4%)
  Pallas kernels  10.9 us (4%)
  between operations  7.61 us (3%)
    all_to_all x5, waiting for transfers between devices, exchange(): return lax.all_to_all(x, axes, split_axis=0, concat_axis=0, tiled=True)  54.4 us
    all_to_all x2, blocking collectives, exchange(): return lax.all_to_all(x, axes, split_axis=0, concat_axis=0, tiled=True)  49.9 us
    all_to_all x5, starting transfers between devices, exchange(): return lax.all_to_all(x, axes, split_axis=0, concat_axis=0, tiled=True)  46.6 us
    ppermute x7, starting transfers between devices, shift(): return lax.ppermute(x, axis, [(i, (i + by) % size) for i in range(size)])  28.5 us
    all_gather x1, blocking collectives, step(): every = lax.all_gather(summed, 'y', axis=0, tiled=False)  13.4 us
    pallas_call x1, Pallas kernels, spot(): pl.pallas_call(spot_kernel, out_shape=(plane, half, half, jax.ShapeDtypeS...  10.9 us
    ppermute x7, waiting for transfers between devices, shift(): return lax.ppermute(x, axis, [(i, (i + by) % size) for i in range(size)])  8.41 us
  transfers between devices with their start and end apart: 12, of which 7 were waited for; matrix products, arithmetic and copies ran while one was open for 5% of the time, Pallas kernels for 0%

profile of v3, /device:TPU:1, one launch (start us, length us, event | category | flops | bytes accessed | tf_op | source)
XLA Modules:
  0.0 244.8 jit_solution(2055965780254748714)
XLA Ops:
  1.6 1.1 copy.68
  2.7 1.4 fusion.15
  4.1 10.4 %all-to-all-start = ((f32[32,16,640]{2,1,0:T(8,128)}), f32[32,16,640]{2,1,0:T(8,128)S(1)}, u32[]{:S(2)}, u32[]{:S(2)}) async-start(f32[32,16,640]{2,1,0:T(8,128)} %fusion.15), calls=%async_computation | async-start | bytes 2621440 | tf_op jit(solution)/shard_map/all_to_all | solution.py:124
  15.3 18.7 %all-to-all-done = f32[32,16,640]{2,1,0:T(8,128)S(1)} async-done(((f32[32,16,640]{2,1,0:T(8,128)}), f32[32,16,640]{2,1,0:T(8,128)S(1)}, u32[]{:S(2)}, u32[]{:S(2)}) %all-to-all-start) | async-done | bytes 1310752 | tf_op jit(solution)/shard_map/all_to_all | solution.py:124
  34.6 25.5 %all_to_all.35 = f32[16,4,8,128]{3,2,1,0:T(8,128)S(1)} all-to-all(f32[16,4,8,128]{3,2,1,0:T(8,128)S(1)} %bitcast.124), channel_id=1, replica_groups=mesh['y'=4,'z'=16,'x'=4,'core'=2] {'z'}, dimensions={0} | all-to-all | bytes 524288 | tf_op jit(solution)/shard_map/all_to_all | solution.py:124
  60.8 10.8 %all-to-all-start.2 = ((f32[16,4,8,128]{3,2,1,0:T(8,128)}), f32[16,4,8,128]{3,2,1,0:T(8,128)S(1)}, u32[]{:S(2)}, u32[]{:S(2)}) async-start(f32[16,4,8,128]{3,2,1,0:T(8,128)} %broadcast_in_dim.134), calls=%async_computation.2 | async-start | bytes 524288 | tf_op jit(solution)/shard_map/all_to_all | solution.py:124
  76.1 1.4 pad_add_fusion.where_ref
  77.5 6.9 %all-to-all-done.2 = f32[16,4,8,128]{3,2,1,0:T(8,128)S(1)} async-done(((f32[16,4,8,128]{3,2,1,0:T(8,128)}), f32[16,4,8,128]{3,2,1,0:T(8,128)S(1)}, u32[]{:S(2)}, u32[]{:S(2)}) %all-to-all-start.2) | async-done | bytes 262176 | tf_op jit(solution)/shard_map/all_to_all | solution.py:124
  84.4 13.4 %all-gather = f32[200,8,128]{2,1,0:T(8,128)S(1)} all-gather(f32[50,8,128]{2,1,0:T(8,128)S(1)} %slice.109), channel_id=2, replica_groups=mesh['y'=4,'z'=16,'x'=4,'core'=2] {'y'}, dimensions={0}, use_global_device_ids=true | all-gather | bytes 1024000 | tf_op jit(solution)/shard_map/all_gather | solution.py:165
  97.9 1.1 sine_multiply_fusion
  99.3 10.9 %spot.1 = (f32[256,256]{1,0:T(8,128)}, f32[4,256,256]{2,1,0:T(8,128)S(1)}, f32[4,256,256]{2,1,0:T(8,128)S(1)}, f32[2,256,256]{2,1,0:T(8,128)S(1)}, f32[4,50,8,128]{3,2,1,0:T(8,128)}) custom-call(s32[3]{0:T(128)S(1)} %pad_add_fusion.where_ref, f32[256,256]{1,0:T(8,128)S(1)} %get-tuple-element.27.tr_ref, f32[256,256]{1,0:T(8,128)S(1)} %get-tuple-element.26.ti_ref, ...), custom_call_target="tpu_custom_call" | custom-call | tf_op jit(solution)/shard_map/spot/pallas_call | solution.py:102
  110.2 9.6 %collective-permute-start = (f32[4,256,256]{2,1,0:T(8,128)S(1)}, f32[4,256,256]{2,1,0:T(8,128)}, u32[]{:S(2)}, u32[]{:S(2)}) collective-permute-start(f32[4,256,256]{2,1,0:T(8,128)S(1)} %get-tuple-element.11), channel_id=1, source_target_pairs={{0,1},{1,0},{2,3},{3,2},{4,5},{5,4},{6,7},{7,6},{8,9},{9,8},{10,11... | collective-permute-start | bytes 3145736 | tf_op jit(solution)/shard_map/ppermute | solution.py:146
  119.8 4.2 %all-to-all-start.3 = ((f32[4,50,8,128]{3,2,1,0:T(8,128)}), f32[4,50,8,128]{3,2,1,0:T(8,128)}, u32[]{:S(2)}, u32[]{:S(2)}) async-start(f32[4,50,8,128]{3,2,1,0:T(8,128)} %get-tuple-element.9), calls=%async_computation.3 | async-start | bytes 1638400 | tf_op jit(solution)/shard_map/all_to_all | solution.py:124
  124.1 12.7 %all-to-all-done.3 = f32[4,50,8,128]{3,2,1,0:T(8,128)} async-done(((f32[4,50,8,128]{3,2,1,0:T(8,128)}), f32[4,50,8,128]{3,2,1,0:T(8,128)}, u32[]{:S(2)}, u32[]{:S(2)}) %all-to-all-start.3) | async-done | bytes 819232 | tf_op jit(solution)/shard_map/all_to_all | solution.py:124
  136.8 1.9 reduce_sum.123
  138.7 1.7 pad.8
  140.3 5.9 %all-to-all-start.4 = ((f32[16,4,8,128]{3,2,1,0:T(8,128)}), f32[16,4,8,128]{3,2,1,0:T(8,128)}, u32[]{:S(2)}, u32[]{:S(2)}) async-start(f32[16,4,8,128]{3,2,1,0:T(8,128)} %bitcast.123), calls=%async_computation.4 | async-start | bytes 524288 | tf_op jit(solution)/shard_map/all_to_all | solution.py:124
  146.3 1.4 add.157
  148.4 3.7 %collective-permute-start.1 = (f32[256,256]{1,0:T(8,128)}, f32[256,256]{1,0:T(8,128)S(1)}, u32[]{:S(2)}, u32[]{:S(2)}) collective-permute-start(f32[256,256]{1,0:T(8,128)} %get-tuple-element.23), channel_id=1, source_target_pairs={{0,4},{2,6},{4,0},{6,2},{1,5},{3,7},{5,1},{7,3},{8,12},{10,14},{12... | collective-permute-start | bytes 786440 | tf_op jit(solution)/shard_map/ppermute | solution.py:146
  152.1 2.6 %collective-permute-start.2 = (f32[256,256]{1,0:T(8,128)S(1)}, f32[256,256]{1,0:T(8,128)S(1)}, u32[]{:S(2)}, u32[]{:S(2)}) collective-permute-start(f32[256,256]{1,0:T(8,128)S(1)} %get-tuple-element.25), channel_id=1, source_target_pairs={{0,2},{2,4},{4,6},{6,0},{1,3},{3,5},{5,7},{7,1},{8,10},{10,12},{12... | collective-permute-start | bytes 786440 | tf_op jit(solution)/shard_map/ppermute | solution.py:146
  154.7 3.9 %collective-permute-start.3 = (f32[256,256]{1,0:T(8,128)S(1)}, f32[256,256]{1,0:T(8,128)}, u32[]{:S(2)}, u32[]{:S(2)}) collective-permute-start(f32[256,256]{1,0:T(8,128)S(1)} %get-tuple-element.24), channel_id=1, source_target_pairs={{0,6},{2,0},{4,2},{6,4},{1,7},{3,1},{5,3},{7,5},{8,14},{10,8},{12,... | collective-permute-start | bytes 786440 | tf_op jit(solution)/shard_map/ppermute | solution.py:146
  158.8 6.7 %collective-permute-done.2 = f32[256,256]{1,0:T(8,128)S(1)} collective-permute-done((f32[256,256]{1,0:T(8,128)S(1)}, f32[256,256]{1,0:T(8,128)S(1)}, u32[]{:S(2)}, u32[]{:S(2)}) %collective-permute-start.2) | collective-permute-done | bytes 262176 | tf_op jit(solution)/shard_map/ppermute | solution.py:146
  166.5 2.2 collective-permute-start.4
  168.8 3.0 %collective-permute-start.5 = (f32[64,256]{1,0:T(8,128)S(1)}, f32[64,256]{1,0:T(8,128)S(1)}, u32[]{:S(2)}, u32[]{:S(2)}) collective-permute-start(f32[64,256]{1,0:T(8,128)S(1)} %get-tuple-element.35), channel_id=1, source_target_pairs={{0,128},{128,256},{256,384},{384,0},{1,129},{129,257},{257,385},{3... | collective-permute-start | bytes 196616 | tf_op jit(solution)/shard_map/ppermute | solution.py:146
  171.8 3.5 %collective-permute-start.6 = (f32[64,256]{1,0:T(8,128)S(1)}, f32[64,256]{1,0:T(8,128)S(1)}, u32[]{:S(2)}, u32[]{:S(2)}) collective-permute-start(f32[64,256]{1,0:T(8,128)S(1)} %get-tuple-element.34), channel_id=1, source_target_pairs={{0,384},{128,0},{256,128},{384,256},{1,385},{129,1},{257,129},{385... | collective-permute-start | bytes 196616 | tf_op jit(solution)/shard_map/ppermute | solution.py:146
  175.3 1.6 collective-permute-done.6
  178.0 24.4 %all_to_all.36 = f32[16,5,8,128]{3,2,1,0:T(8,128)S(1)} all-to-all(f32[16,5,8,128]{3,2,1,0:T(8,128)S(1)} %pad_maximum_fusion.1), channel_id=1, replica_groups=mesh['y'=4,'z'=16,'x'=4,'core'=2] {'z'}, dimensions={0} | all-to-all | bytes 655360 | tf_op jit(solution)/shard_map/all_to_all | solution.py:124
  202.9 1.2 pad_maximum_fusion
  204.1 15.2 %all-to-all-start.6 = ((f32[32,11,8,128]{3,2,1,0:T(8,128)}), f32[32,11,8,128]{3,2,1,0:T(8,128)}, u32[]{:S(2)}, u32[]{:S(2)}) async-start(f32[32,11,8,128]{3,2,1,0:T(8,128)} %pad_maximum_fusion), calls=%async_computation.6 | async-start | bytes 2883584 | tf_op jit(solution)/shard_map/all_to_all | solution.py:124
  219.4 1.3 fusion.5
  223.9 16.1 %all-to-all-done.6 = f32[32,11,8,128]{3,2,1,0:T(8,128)} async-done(((f32[32,11,8,128]{3,2,1,0:T(8,128)}), f32[32,11,8,128]{3,2,1,0:T(8,128)}, u32[]{:S(2)}, u32[]{:S(2)}) %all-to-all-start.6) | async-done | bytes 1441824 | tf_op jit(solution)/shard_map/all_to_all | solution.py:124
  240.0 1.4 slice.117
  (62 shorter events, 11.3 us)
Async XLA Ops:
  0.6 13.9 %copy-start = (s32[8,64,8]{1,2,0:T(8,128)S(1)}, s32[8,64,8]{1,2,0:T(8,128)}, u32[]{:S(2)}) copy-start(s32[8,64,8]{1,2,0:T(8,128)} %param.9) | copy-start | bytes 49156
  1.6 2.5 %copy-start.4 = (bf16[4,8,16,128]{3,2,1,0:T(8,128)(2,1)}, bf16[4,8,16,128]{3,2,1,0:T(8,128)(2,1)S(1)}, u32[]{:S(2)}) copy-start(bf16[4,8,16,128]{3,2,1,0:T(8,128)(2,1)S(1)} %copy.67) | copy-start | bytes 393220
  4.1 29.8 %all-to-all-start = ((f32[32,16,640]{2,1,0:T(8,128)}), f32[32,16,640]{2,1,0:T(8,128)S(1)}, u32[]{:S(2)}, u32[]{:S(2)}) async-start(f32[32,16,640]{2,1,0:T(8,128)} %fusion.15), calls=%async_computation | async-start | bytes 2621440 | tf_op jit(solution)/shard_map/all_to_all | solution.py:124
  34.5 37.2 %copy-start.6 = (s32[1,1,2]{2,1,0:T(1,128)S(1)}, s32[1,1,2]{2,1,0:T(1,128)}, u32[]{:S(2)}) copy-start(s32[1,1,2]{2,1,0:T(1,128)} %param.11) | copy-start | bytes 28
  60.8 23.6 %all-to-all-start.2 = ((f32[16,4,8,128]{3,2,1,0:T(8,128)}), f32[16,4,8,128]{3,2,1,0:T(8,128)S(1)}, u32[]{:S(2)}, u32[]{:S(2)}) async-start(f32[16,4,8,128]{3,2,1,0:T(8,128)} %broadcast_in_dim.134), calls=%async_computation.2 | async-start | bytes 524288 | tf_op jit(solution)/shard_map/all_to_all | solution.py:124
  97.8 1.2 copy-start.1
  97.8 1.4 copy-start.2
  97.8 1.5 copy-start.3
  110.2 36.0 %collective-permute-start = (f32[4,256,256]{2,1,0:T(8,128)S(1)}, f32[4,256,256]{2,1,0:T(8,128)}, u32[]{:S(2)}, u32[]{:S(2)}) collective-permute-start(f32[4,256,256]{2,1,0:T(8,128)S(1)} %get-tuple-element.11), channel_id=1, source_target_pairs={{0,1},{1,0},{2,3},{3,2},{4,5},{5,4},{6,7},{7,6},{8,9},{9,8},{10,11... | collective-permute-start | bytes 3145736 | tf_op jit(solution)/shard_map/ppermute | solution.py:146
  119.8 17.0 %all-to-all-start.3 = ((f32[4,50,8,128]{3,2,1,0:T(8,128)}), f32[4,50,8,128]{3,2,1,0:T(8,128)}, u32[]{:S(2)}, u32[]{:S(2)}) async-start(f32[4,50,8,128]{3,2,1,0:T(8,128)} %get-tuple-element.9), calls=%async_computation.3 | async-start | bytes 1638400 | tf_op jit(solution)/shard_map/all_to_all | solution.py:124
  140.3 36.6 %all-to-all-start.4 = ((f32[16,4,8,128]{3,2,1,0:T(8,128)}), f32[16,4,8,128]{3,2,1,0:T(8,128)}, u32[]{:S(2)}, u32[]{:S(2)}) async-start(f32[16,4,8,128]{3,2,1,0:T(8,128)} %bitcast.123), calls=%async_computation.4 | async-start | bytes 524288 | tf_op jit(solution)/shard_map/all_to_all | solution.py:124
  148.4 10.4 %collective-permute-start.1 = (f32[256,256]{1,0:T(8,128)}, f32[256,256]{1,0:T(8,128)S(1)}, u32[]{:S(2)}, u32[]{:S(2)}) collective-permute-start(f32[256,256]{1,0:T(8,128)} %get-tuple-element.23), channel_id=1, source_target_pairs={{0,4},{2,6},{4,0},{6,2},{1,5},{3,7},{5,1},{7,3},{8,12},{10,14},{12... | collective-permute-start | bytes 786440 | tf_op jit(solution)/shard_map/ppermute | solution.py:146
  152.1 13.4 %collective-permute-start.2 = (f32[256,256]{1,0:T(8,128)S(1)}, f32[256,256]{1,0:T(8,128)S(1)}, u32[]{:S(2)}, u32[]{:S(2)}) collective-permute-start(f32[256,256]{1,0:T(8,128)S(1)} %get-tuple-element.25), channel_id=1, source_target_pairs={{0,2},{2,4},{4,6},{6,0},{1,3},{3,5},{5,7},{7,1},{8,10},{10,12},{12... | collective-permute-start | bytes 786440 | tf_op jit(solution)/shard_map/ppermute | solution.py:146
  154.7 10.8 %collective-permute-start.3 = (f32[256,256]{1,0:T(8,128)S(1)}, f32[256,256]{1,0:T(8,128)}, u32[]{:S(2)}, u32[]{:S(2)}) collective-permute-start(f32[256,256]{1,0:T(8,128)S(1)} %get-tuple-element.24), channel_id=1, source_target_pairs={{0,6},{2,0},{4,2},{6,4},{1,7},{3,1},{5,3},{7,5},{8,14},{10,8},{12,... | collective-permute-start | bytes 786440 | tf_op jit(solution)/shard_map/ppermute | solution.py:146
  166.5 8.8 %collective-permute-start.4 = (f32[64,256]{1,0:T(8,128)S(1)}, f32[64,256]{1,0:T(8,128)S(1)}, u32[]{:S(2)}, u32[]{:S(2)}) collective-permute-start(f32[64,256]{1,0:T(8,128)S(1)} %get-tuple-element.33), channel_id=1, source_target_pairs={{0,256},{128,384},{256,0},{384,128},{1,257},{129,385},{257,1},{385... | collective-permute-start | bytes 196616 | tf_op jit(solution)/shard_map/ppermute | solution.py:146
  168.8 6.5 %collective-permute-start.5 = (f32[64,256]{1,0:T(8,128)S(1)}, f32[64,256]{1,0:T(8,128)S(1)}, u32[]{:S(2)}, u32[]{:S(2)}) collective-permute-start(f32[64,256]{1,0:T(8,128)S(1)} %get-tuple-element.35), channel_id=1, source_target_pairs={{0,128},{128,256},{256,384},{384,0},{1,129},{129,257},{257,385},{3... | collective-permute-start | bytes 196616 | tf_op jit(solution)/shard_map/ppermute | solution.py:146
  171.8 5.1 %collective-permute-start.6 = (f32[64,256]{1,0:T(8,128)S(1)}, f32[64,256]{1,0:T(8,128)S(1)}, u32[]{:S(2)}, u32[]{:S(2)}) collective-permute-start(f32[64,256]{1,0:T(8,128)S(1)} %get-tuple-element.34), channel_id=1, source_target_pairs={{0,384},{128,0},{256,128},{384,256},{1,385},{129,1},{257,129},{385... | collective-permute-start | bytes 196616 | tf_op jit(solution)/shard_map/ppermute | solution.py:146
  204.1 35.9 %all-to-all-start.6 = ((f32[32,11,8,128]{3,2,1,0:T(8,128)}), f32[32,11,8,128]{3,2,1,0:T(8,128)}, u32[]{:S(2)}, u32[]{:S(2)}) async-start(f32[32,11,8,128]{3,2,1,0:T(8,128)} %pad_maximum_fusion), calls=%async_computation.6 | async-start | bytes 2883584 | tf_op jit(solution)/shard_map/all_to_all | solution.py:124
  223.9 17.5 %copy-start.5 = (bf16[4,8,16,128]{3,2,1,0:T(8,128)(2,1)S(1)}, bf16[4,8,16,128]{3,2,1,0:T(8,128)(2,1)}, u32[]{:S(2)}) copy-start(bf16[4,8,16,128]{3,2,1,0:T(8,128)(2,1)} %copy-done.4) | copy-start | bytes 393220

commit v4 on v3

--- a/solution.py
+++ b/solution.py
@@ -16,7 +16,6 @@
 LIMIT = 16 << 20
 SLAB = ("y", "z")
 ANGLE = ("x", "core")
-HIGH = lax.Precision.HIGH
 
 
 def dft_tables():
@@ -120,6 +119,67 @@
     )(where, tr, ti, probe, power, tab)
 
 
+def rays_kernel(vol_ref, mat_ref, out_ref, tile_ref):
+    tile_ref[:, :DET] = vol_ref[0].astype(jnp.float32)
+    tile_ref[:, DET:] = vol_ref[1].astype(jnp.float32)
+    tile = tile_ref[...].astype(jnp.bfloat16)
+    for a in range(NA):
+        sums = dot(mat_ref[a], tile)
+        for y in range(NY):
+            out_ref[y * NA + a] = sums[y * QC : (y + 1) * QC]
+
+
+def rays_of(volume, matrices):
+    vmem = pl.BlockSpec(memory_space=pltpu.VMEM)
+    return pl.pallas_call(
+        rays_kernel,
+        out_shape=jax.ShapeDtypeStruct((32, QC, LANES), jnp.float32),
+        in_specs=[vmem] * 2,
+        out_specs=vmem,
+        scratch_shapes=[pltpu.VMEM((128, LANES), jnp.float32)],
+        compiler_params=pltpu.CompilerParams(vmem_limit_bytes=LIMIT),
+        name="rays",
+    )(volume, matrices)
+
+
+def volume_kernel(y_ref, got_ref, mat_ref, vol_ref, probe_ref, hi_ref, lo_ref):
+    for a in range(NA):
+        for y in range(NY):
+            at = a * UB + y * QC
+            for t in range(5):
+                v = jnp.concatenate([got_ref[y * NA + a, t], got_ref[y * NA + a, 5 + t]], axis=0)
+                hi, lo = split(v)
+                hi_ref[at : at + QC, t * 128 : (t + 1) * 128] = hi
+                lo_ref[at : at + QC, t * 128 : (t + 1) * 128] = lo
+    back = lambda ref: lax.dot_general(
+        mat_ref[...], ref[...], (((0,), (0,)), ((), ())), preferred_element_type=jnp.float32
+    )
+    grad = back(hi_ref) + back(lo_ref)
+    vol_ref[0] = grad[:, :DET]
+    vol_ref[1] = pltpu.roll(grad, DET, 1)[:, :DET]
+    for a in range(NA):
+        piece = got_ref[y_ref[0] * NA + a, 10]
+        for r in range(4):
+            for k in range(2):
+                probe_ref[a, r : r + 1, k * 128 : (k + 1) * 128] = piece[2 * r + k : 2 * r + k + 1]
+
+
+def volume_of(y, got, matrices):
+    vmem = pl.BlockSpec(memory_space=pltpu.VMEM)
+    return pl.pallas_call(
+        volume_kernel,
+        out_shape=(
+            jax.ShapeDtypeStruct((2, 128, DET), jnp.float32),
+            jax.ShapeDtypeStruct((NA, 4, SIDE), jnp.float32),
+        ),
+        in_specs=[pl.BlockSpec(memory_space=pltpu.SMEM)] + [vmem] * 2,
+        out_specs=(vmem,) * 2,
+        scratch_shapes=[pltpu.VMEM((512, LANES), jnp.bfloat16)] * 2,
+        compiler_params=pltpu.CompilerParams(vmem_limit_bytes=LIMIT),
+        name="volume",
+    )(y, got, matrices)
+
+
 def exchange(x, axes):
     return lax.all_to_all(x, axes, split_axis=0, concat_axis=0, tiled=True)
 
@@ -135,7 +195,7 @@
 
 
 def chunks_of_z(tiles):
-    return jnp.pad(tiles, ((0, 14), (0, 0), (0, 0))).reshape(NZ, 4, 8, 128)
+    return tiles.reshape(NZ, 25, 1, 128)
 
 
 def pick(x, i, n):
@@ -149,19 +209,16 @@
 def step(volume, matrices, tile_ids, modes, corners, power):
     y, z = lax.axis_index("y"), lax.axis_index("z")
     angle = lax.axis_index(ANGLE)
-    tile = volume.reshape(2, 128, DET).transpose(1, 0, 2).reshape(128, LANES)
-    kern = matrices.reshape(NA, NY, QC, 128).transpose(1, 0, 2, 3).reshape(512, 128)
     ids = lax.dynamic_index_in_dim(tile_ids, angle, 0, keepdims=False)
     ids = lax.dynamic_index_in_dim(ids.reshape(NY, NZ, NA), z, 1, keepdims=False).reshape(32)
 
-    rays = jnp.dot(kern, tile, preferred_element_type=jnp.float32).reshape(32, QC, LANES)
-    items = exchange(rays, ("y", "x", "core"))
+    items = exchange(rays_of(volume.reshape(2, 128, DET), matrices), ("y", "x", "core"))
     quarter = jnp.stack(
         [jnp.sum(jnp.where((ids == d)[:, None, None], items, 0.0), axis=0) for d in range(NUB)]
     )
     mine = exchange(chunks_of_z(to_tiles(quarter.reshape(NUB * QC, LANES))), "z").sum(0)
-    copies = jnp.broadcast_to(mine[None], (NZ, 4, 8, 128))
-    summed = exchange(copies, "z").reshape(64, 8, 128)[:50]
+    copies = jnp.broadcast_to(mine[None], (NZ, 25, 1, 128))
+    summed = exchange(copies, "z").reshape(50, 8, 128)
     every = lax.all_gather(summed, "y", axis=0, tiled=False)
     det = from_tiles(every.reshape(200, 8, 128))
     det = det.reshape(NY, NUB, QC, LANES).transpose(1, 0, 2, 3).reshape(DET, LANES)
@@ -185,26 +242,23 @@
     got = [shift(pick(planes, lax.axis_index("x") + k, NX), "x", NX, k) for k in (2, 1, 3)]
     rows = (pick(planes, lax.axis_index("x"), NX) + got[0] + got[1] + got[2]).reshape(NY, 64, SIDE)
     got = [shift(pick(rows, y + k, NY), "y", NY, k) for k in (2, 1, 3)]
-    rows = (pick(rows, y, NY) + got[0] + got[1] + got[2]).reshape(NZ, 1, 8, 128)
+    rows = (pick(rows, y, NY) + got[0] + got[1] + got[2]).reshape(NZ, 8, 1, 128)
 
     part = exchange(placed, "y")
     part = part.sum(0)
     part = exchange(chunks_of_z(part), "z")
     mine = part.sum(0)
-    got = exchange(jnp.concatenate([jnp.broadcast_to(mine[None], (NZ, 4, 8, 128)), rows], axis=1), "z")
-    piece = got[:, 4].sum(0)
-    quarter = got[:, :4].reshape(64, 8, 128)[:50].reshape(NUB, 10, 8, 128)
+    got = exchange(jnp.concatenate([jnp.broadcast_to(mine[None], (NZ, 25, 1, 128)), rows], axis=1), "z")
+    piece = got[:, 25:].sum(0).reshape(8, 128)
+    quarter = got[:, :25].reshape(NUB, 10, 8, 128)
     sent = quarter[0][None]
     for d in range(1, NUB):
         sent = jnp.where((ids == d)[:, None, None, None], quarter[d][None], sent)
     sent = jnp.concatenate([sent, jnp.broadcast_to(piece[None, None], (32, 1, 8, 128))], axis=1)
     got = exchange(sent, ("y", "x", "core"))
-    probe_grad = lax.dynamic_slice_in_dim(got[:, 10], y * NA, NA, 0).reshape(4, 2, 4, SIDE)
-    blocks = from_tiles(got[:, :10].reshape(320, 8, 128))
-    vol = lax.dot_general(
-        kern.astype(jnp.float32), blocks, (((0,), (0,)), ((), ())), precision=HIGH
-    )
-    vol_grad = vol.reshape(128, 2, DET).transpose(1, 0, 2).reshape(2, 8, 16, DET)
+    vol_grad, probe_grad = volume_of(y.reshape(1), got, matrices.reshape(512, 128))
+    vol_grad = vol_grad.reshape(2, 8, 16, DET)
+    probe_grad = probe_grad.reshape(4, 2, 4, SIDE)
     return vol_grad, probe_grad, resid[None, None], locus
 
 

time: 246 us -> 213 us (0.87)
  waiting for transfers between devices: 62.8 us -> 43.7 us
  local copies, waits for them, and re-layouts: 10.9 us -> 5.59 us
  starting transfers between devices: 75.1 us -> 71.4 us
  blocking collectives: 63.3 us -> 59.8 us
  Pallas kernels: 10.9 us -> 13.8 us
    all_to_all x5, waiting for transfers between devices: 54.4 us -> 41.3 us  [exchange(): return lax.all_to_all(x, axes, split_axis=0, concat_axis=0, tiled=True)]
    all_to_all x5, starting transfers between devices: 46.6 us -> 40.4 us  [exchange(): return lax.all_to_all(x, axes, split_axis=0, concat_axis=0, tiled=True)]
    ppermute x7, waiting for transfers between devices: 8.41 us -> 2.39 us  [shift(): return lax.ppermute(x, axis, [(i, (i + by) % size) for i in range(size)])]
    transpose x3 -> x0, local copies, waits for them, and re-layouts: 2.97 us -> none  [the longest x1 1.14 us: step(): tile = volume.reshape(2, 128, DET).transpose(1, 0, 2).reshape(128, LANES)]
    pallas_call x0 -> x2, Pallas kernels: none -> 2.91 us  [the longest x1 1.52 us: rays_of(): pl.pallas_call(rays_kernel, out_shape=jax.ShapeDtypeStruct((32, QC, LANES...]
    ppermute x7, starting transfers between devices: 28.5 us -> 31 us  [shift(): return lax.ppermute(x, axis, [(i, (i + by) % size) for i in range(size)])]
  transfers between devices with their start and end apart: 12 -> 12, of which waited for: 7 -> 6; matrix products, arithmetic and copies ran while one was open for 5% -> 4% of each run, Pallas kernels for 0% -> 0%
where the time goes in v4:
time: 213 us; the launch traced here: 212 us
  starting transfers between devices  71.4 us (34%)
  blocking collectives  59.8 us (28%)
  waiting for transfers between devices  43.7 us (21%)
  Pallas kernels  13.8 us (6%)
  other arithmetic  10.4 us (5%)
  between operations  7.66 us (4%)
  local copies, waits for them, and re-layouts  5.59 us (3%)
    all_to_all x2, blocking collectives, exchange(): return lax.all_to_all(x, axes, split_axis=0, concat_axis=0, tiled=True)  47.6 us
    all_to_all x5, waiting for transfers between devices, exchange(): return lax.all_to_all(x, axes, split_axis=0, concat_axis=0, tiled=True)  41.3 us
    all_to_all x5, starting transfers between devices, exchange(): return lax.all_to_all(x, axes, split_axis=0, concat_axis=0, tiled=True)  40.4 us
    ppermute x7, starting transfers between devices, shift(): return lax.ppermute(x, axis, [(i, (i + by) % size) for i in range(size)])  31 us
    all_gather x1, blocking collectives, step(): every = lax.all_gather(summed, 'y', axis=0, tiled=False)  12.2 us
    pallas_call x1, Pallas kernels, spot(): pl.pallas_call(spot_kernel, out_shape=(plane, half, half, jax.ShapeDtypeS...  10.8 us
  transfers between devices with their start and end apart: 12, of which 6 were waited for; matrix products, arithmetic and copies ran while one was open for 4% of the time, Pallas kernels for 0%

profile of v4, /device:TPU:1, one launch (start us, length us, event | category | flops | bytes accessed | tf_op | source)
XLA Modules:
  0.0 212.4 jit_solution(12778442298975832164)
XLA Ops:
  0.7 0.9 copy-done.3
  1.6 0.9 copy-done.6
  2.5 1.5 rays.1
  4.0 10.4 %all-to-all-start = ((f32[32,16,640]{2,1,0:T(8,128)}), f32[32,16,640]{2,1,0:T(8,128)S(1)}, u32[]{:S(2)}, u32[]{:S(2)}) async-start(f32[32,16,640]{2,1,0:T(8,128)} %rays.1), calls=%async_computation | async-start | bytes 2621440 | tf_op jit(solution)/shard_map/all_to_all | solution.py:184
  15.2 18.6 %all-to-all-done = f32[32,16,640]{2,1,0:T(8,128)S(1)} async-done(((f32[32,16,640]{2,1,0:T(8,128)}), f32[32,16,640]{2,1,0:T(8,128)S(1)}, u32[]{:S(2)}, u32[]{:S(2)}) %all-to-all-start) | async-done | bytes 1310752 | tf_op jit(solution)/shard_map/all_to_all | solution.py:184
  34.4 25.1 %all_to_all.35 = f32[16,25,1,128]{3,2,1,0:T(1,128)S(1)} all-to-all(f32[16,25,1,128]{3,2,1,0:T(1,128)S(1)} %bitcast.111), channel_id=1, replica_groups=mesh['y'=4,'z'=16,'x'=4,'core'=2] {'z'}, dimensions={0} | all-to-all | bytes 409600 | tf_op jit(solution)/shard_map/all_to_all | solution.py:184
  59.7 0.8 broadcast_in_dim.143
  60.4 8.9 %all-to-all-start.2 = ((f32[16,25,1,128]{3,2,1,0:T(1,128)}), f32[16,25,1,128]{3,2,1,0:T(1,128)S(1)}, u32[]{:S(2)}, u32[]{:S(2)}) async-start(f32[16,25,1,128]{3,2,1,0:T(1,128)} %broadcast_in_dim.143), calls=%async_computation.2 | async-start | bytes 409600 | tf_op jit(solution)/shard_map/all_to_all | solution.py:184
  73.8 1.4 pad_add_fusion.where_ref
  75.2 6.5 %all-to-all-done.2 = f32[16,25,1,128]{3,2,1,0:T(1,128)S(1)} async-done(((f32[16,25,1,128]{3,2,1,0:T(1,128)}), f32[16,25,1,128]{3,2,1,0:T(1,128)S(1)}, u32[]{:S(2)}, u32[]{:S(2)}) %all-to-all-start.2) | async-done | bytes 204832 | tf_op jit(solution)/shard_map/all_to_all | solution.py:184
  81.7 12.2 %all_gather.3 = f32[4,50,8,128]{3,2,1,0:T(8,128)S(1)} all-gather(f32[1,50,8,128]{3,2,1,0:T(8,128)S(1)} %bitcast.110), channel_id=1, replica_groups=mesh['y'=4,'z'=16,'x'=4,'core'=2] {'y'}, dimensions={0}, use_global_device_ids=true | all-gather | bytes 1024000 | tf_op jit(solution)/shard_map/all_gather | solution.py:222
  94.0 1.1 sine_multiply_fusion
  95.7 10.8 %spot.1 = (f32[256,256]{1,0:T(8,128)}, f32[4,256,256]{2,1,0:T(8,128)S(1)}, f32[4,256,256]{2,1,0:T(8,128)S(1)}, f32[2,256,256]{2,1,0:T(8,128)S(1)}, f32[4,50,8,128]{3,2,1,0:T(8,128)}) custom-call(s32[3]{0:T(128)S(1)} %pad_add_fusion.where_ref, f32[256,256]{1,0:T(8,128)S(1)} %get-tuple-element.31.tr_ref, f32[256,256]{1,0:T(8,128)S(1)} %get-tuple-element.30.ti_ref, ...), custom_call_target="tpu_custom_call" | custom-call | tf_op jit(solution)/shard_map/spot/pallas_call | solution.py:101
  106.5 9.3 %collective-permute-start = (f32[4,256,256]{2,1,0:T(8,128)S(1)}, f32[4,256,256]{2,1,0:T(8,128)}, u32[]{:S(2)}, u32[]{:S(2)}) collective-permute-start(f32[4,256,256]{2,1,0:T(8,128)S(1)} %get-tuple-element.13), channel_id=1, source_target_pairs={{0,1},{1,0},{2,3},{3,2},{4,5},{5,4},{6,7},{7,6},{8,9},{9,8},{10,11... | collective-permute-start | bytes 3145736 | tf_op jit(solution)/shard_map/ppermute | solution.py:206
  115.9 3.5 %all-to-all-start.3 = ((f32[4,50,8,128]{3,2,1,0:T(8,128)}), f32[4,50,8,128]{3,2,1,0:T(8,128)S(1)}, u32[]{:S(2)}, u32[]{:S(2)}) async-start(f32[4,50,8,128]{3,2,1,0:T(8,128)} %get-tuple-element.11), calls=%async_computation.3 | async-start | bytes 1638400 | tf_op jit(solution)/shard_map/all_to_all | solution.py:184
  119.5 1.4 add.150
  121.6 3.7 %collective-permute-start.1 = (f32[256,256]{1,0:T(8,128)}, f32[256,256]{1,0:T(8,128)S(1)}, u32[]{:S(2)}, u32[]{:S(2)}) collective-permute-start(f32[256,256]{1,0:T(8,128)} %get-tuple-element.27), channel_id=1, source_target_pairs={{0,4},{2,6},{4,0},{6,2},{1,5},{3,7},{5,1},{7,3},{8,12},{10,14},{12... | collective-permute-start | bytes 786440 | tf_op jit(solution)/shard_map/ppermute | solution.py:206
  125.3 1.9 collective-permute-start.2
  127.3 4.6 %collective-permute-start.3 = (f32[256,256]{1,0:T(8,128)S(1)}, f32[256,256]{1,0:T(8,128)}, u32[]{:S(2)}, u32[]{:S(2)}) collective-permute-start(f32[256,256]{1,0:T(8,128)S(1)} %get-tuple-element.28), channel_id=1, source_target_pairs={{0,6},{2,0},{4,2},{6,4},{1,7},{3,1},{5,3},{7,5},{8,14},{10,8},{12,... | collective-permute-start | bytes 786440 | tf_op jit(solution)/shard_map/ppermute | solution.py:206
  132.8 5.0 %all-to-all-start.4 = ((f32[16,25,1,128]{3,2,1,0:T(1,128)}), f32[16,25,1,128]{3,2,1,0:T(1,128)S(1)}, u32[]{:S(2)}, u32[]{:S(2)}) async-start(f32[16,25,1,128]{3,2,1,0:T(1,128)} %bitcast.28), calls=%async_computation.4 | async-start | bytes 409600 | tf_op jit(solution)/shard_map/all_to_all | solution.py:184
  137.9 1.3 collective-permute-done.2
  139.2 1.1 fusion.10
  140.3 4.8 %collective-permute-start.4 = (f32[64,256]{1,0:T(8,128)S(1)}, f32[64,256]{1,0:T(8,128)S(1)}, u32[]{:S(2)}, u32[]{:S(2)}) collective-permute-start(f32[64,256]{1,0:T(8,128)S(1)} %get-tuple-element.32), channel_id=1, source_target_pairs={{0,256},{128,384},{256,0},{384,128},{1,257},{129,385},{257,1},{385... | collective-permute-start | bytes 196616 | tf_op jit(solution)/shard_map/ppermute | solution.py:206
  145.1 2.2 %collective-permute-start.5 = (f32[64,256]{1,0:T(8,128)S(1)}, f32[64,256]{1,0:T(8,128)S(1)}, u32[]{:S(2)}, u32[]{:S(2)}) collective-permute-start(f32[64,256]{1,0:T(8,128)S(1)} %get-tuple-element.34), channel_id=1, source_target_pairs={{0,128},{128,256},{256,384},{384,0},{1,129},{129,257},{257,385},{3... | collective-permute-start | bytes 196616 | tf_op jit(solution)/shard_map/ppermute | solution.py:206
  147.3 4.5 %collective-permute-start.6 = (f32[64,256]{1,0:T(8,128)S(1)}, f32[64,256]{1,0:T(8,128)S(1)}, u32[]{:S(2)}, u32[]{:S(2)}) collective-permute-start(f32[64,256]{1,0:T(8,128)S(1)} %get-tuple-element.33), channel_id=1, source_target_pairs={{0,384},{128,0},{256,128},{384,256},{1,385},{129,1},{257,129},{385... | collective-permute-start | bytes 196616 | tf_op jit(solution)/shard_map/ppermute | solution.py:206
  151.8 1.1 collective-permute-done.6
  153.5 22.5 %all_to_all.36 = f32[16,33,1,128]{3,2,1,0:T(1,128)S(1)} all-to-all(f32[16,33,1,128]{3,2,1,0:T(1,128)S(1)} %pad_maximum_fusion.1), channel_id=1, replica_groups=mesh['y'=4,'z'=16,'x'=4,'core'=2] {'z'}, dimensions={0} | all-to-all | bytes 540672 | tf_op jit(solution)/shard_map/all_to_all | solution.py:184
  176.6 1.2 pad_maximum_fusion
  177.8 12.6 %all-to-all-start.6 = ((f32[32,11,8,128]{3,2,1,0:T(8,128)}), f32[32,11,8,128]{3,2,1,0:T(8,128)S(1)}, u32[]{:S(2)}, u32[]{:S(2)}) async-start(f32[32,11,8,128]{3,2,1,0:T(8,128)} %pad_maximum_fusion), calls=%async_computation.6 | async-start | bytes 2883584 | tf_op jit(solution)/shard_map/all_to_all | solution.py:184
  190.5 1.3 fusion.5
  195.0 16.0 %all-to-all-done.6.got_ref = f32[32,11,8,128]{3,2,1,0:T(8,128)S(1)} async-done(((f32[32,11,8,128]{3,2,1,0:T(8,128)}), f32[32,11,8,128]{3,2,1,0:T(8,128)S(1)}, u32[]{:S(2)}, u32[]{:S(2)}) %all-to-all-start.6) | async-done | bytes 1441824 | tf_op jit(solution)/shard_map/all_to_all | solution.py:184
  211.0 1.4 volume.1
  (58 shorter events, 6.1 us)
Async XLA Ops:
  0.6 13.8 %copy-start = (s32[8,64,8]{1,2,0:T(8,128)S(1)}, s32[8,64,8]{1,2,0:T(8,128)}, u32[]{:S(2)}) copy-start(s32[8,64,8]{1,2,0:T(8,128)} %param.9) | copy-start | bytes 49156
  0.6 0.9 copy-start.3
  1.6 0.9 copy-start.6
  4.0 29.8 %all-to-all-start = ((f32[32,16,640]{2,1,0:T(8,128)}), f32[32,16,640]{2,1,0:T(8,128)S(1)}, u32[]{:S(2)}, u32[]{:S(2)}) async-start(f32[32,16,640]{2,1,0:T(8,128)} %rays.1), calls=%async_computation | async-start | bytes 2621440 | tf_op jit(solution)/shard_map/all_to_all | solution.py:184
  15.2 54.1 %copy-start.9 = (s32[1,1,2]{2,1,0:T(1,128)S(1)}, s32[1,1,2]{2,1,0:T(1,128)}, u32[]{:S(2)}) copy-start(s32[1,1,2]{2,1,0:T(1,128)} %param.11) | copy-start | bytes 28
  60.4 21.2 %all-to-all-start.2 = ((f32[16,25,1,128]{3,2,1,0:T(1,128)}), f32[16,25,1,128]{3,2,1,0:T(1,128)S(1)}, u32[]{:S(2)}, u32[]{:S(2)}) async-start(f32[16,25,1,128]{3,2,1,0:T(1,128)} %broadcast_in_dim.143), calls=%async_computation.2 | async-start | bytes 409600 | tf_op jit(solution)/shard_map/all_to_all | solution.py:184
  93.9 1.5 copy-start.1
  93.9 1.7 copy-start.2
  93.9 1.8 copy-start.5
  94.0 1.2 copy-start.7
  106.5 12.9 %collective-permute-start = (f32[4,256,256]{2,1,0:T(8,128)S(1)}, f32[4,256,256]{2,1,0:T(8,128)}, u32[]{:S(2)}, u32[]{:S(2)}) collective-permute-start(f32[4,256,256]{2,1,0:T(8,128)S(1)} %get-tuple-element.13), channel_id=1, source_target_pairs={{0,1},{1,0},{2,3},{3,2},{4,5},{5,4},{6,7},{7,6},{8,9},{9,8},{10,11... | collective-permute-start | bytes 3145736 | tf_op jit(solution)/shard_map/ppermute | solution.py:206
  115.9 16.2 %all-to-all-start.3 = ((f32[4,50,8,128]{3,2,1,0:T(8,128)}), f32[4,50,8,128]{3,2,1,0:T(8,128)S(1)}, u32[]{:S(2)}, u32[]{:S(2)}) async-start(f32[4,50,8,128]{3,2,1,0:T(8,128)} %get-tuple-element.11), calls=%async_computation.3 | async-start | bytes 1638400 | tf_op jit(solution)/shard_map/all_to_all | solution.py:184
  121.6 16.3 %collective-permute-start.1 = (f32[256,256]{1,0:T(8,128)}, f32[256,256]{1,0:T(8,128)S(1)}, u32[]{:S(2)}, u32[]{:S(2)}) collective-permute-start(f32[256,256]{1,0:T(8,128)} %get-tuple-element.27), channel_id=1, source_target_pairs={{0,4},{2,6},{4,0},{6,2},{1,5},{3,7},{5,1},{7,3},{8,12},{10,14},{12... | collective-permute-start | bytes 786440 | tf_op jit(solution)/shard_map/ppermute | solution.py:206
  125.3 13.8 %collective-permute-start.2 = (f32[256,256]{1,0:T(8,128)S(1)}, f32[256,256]{1,0:T(8,128)}, u32[]{:S(2)}, u32[]{:S(2)}) collective-permute-start(f32[256,256]{1,0:T(8,128)S(1)} %get-tuple-element.29), channel_id=1, source_target_pairs={{0,2},{2,4},{4,6},{6,0},{1,3},{3,5},{5,7},{7,1},{8,10},{10,12},{12... | collective-permute-start | bytes 786440 | tf_op jit(solution)/shard_map/ppermute | solution.py:206
  127.3 11.9 %collective-permute-start.3 = (f32[256,256]{1,0:T(8,128)S(1)}, f32[256,256]{1,0:T(8,128)}, u32[]{:S(2)}, u32[]{:S(2)}) collective-permute-start(f32[256,256]{1,0:T(8,128)S(1)} %get-tuple-element.28), channel_id=1, source_target_pairs={{0,6},{2,0},{4,2},{6,4},{1,7},{3,1},{5,3},{7,5},{8,14},{10,8},{12,... | collective-permute-start | bytes 786440 | tf_op jit(solution)/shard_map/ppermute | solution.py:206
  132.8 20.2 %all-to-all-start.4 = ((f32[16,25,1,128]{3,2,1,0:T(1,128)}), f32[16,25,1,128]{3,2,1,0:T(1,128)S(1)}, u32[]{:S(2)}, u32[]{:S(2)}) async-start(f32[16,25,1,128]{3,2,1,0:T(1,128)} %bitcast.28), calls=%async_computation.4 | async-start | bytes 409600 | tf_op jit(solution)/shard_map/all_to_all | solution.py:184
  140.3 11.5 %collective-permute-start.4 = (f32[64,256]{1,0:T(8,128)S(1)}, f32[64,256]{1,0:T(8,128)S(1)}, u32[]{:S(2)}, u32[]{:S(2)}) collective-permute-start(f32[64,256]{1,0:T(8,128)S(1)} %get-tuple-element.32), channel_id=1, source_target_pairs={{0,256},{128,384},{256,0},{384,128},{1,257},{129,385},{257,1},{385... | collective-permute-start | bytes 196616 | tf_op jit(solution)/shard_map/ppermute | solution.py:206
  145.1 6.7 %collective-permute-start.5 = (f32[64,256]{1,0:T(8,128)S(1)}, f32[64,256]{1,0:T(8,128)S(1)}, u32[]{:S(2)}, u32[]{:S(2)}) collective-permute-start(f32[64,256]{1,0:T(8,128)S(1)} %get-tuple-element.34), channel_id=1, source_target_pairs={{0,128},{128,256},{256,384},{384,0},{1,129},{129,257},{257,385},{3... | collective-permute-start | bytes 196616 | tf_op jit(solution)/shard_map/ppermute | solution.py:206
  147.3 5.6 %collective-permute-start.6 = (f32[64,256]{1,0:T(8,128)S(1)}, f32[64,256]{1,0:T(8,128)S(1)}, u32[]{:S(2)}, u32[]{:S(2)}) collective-permute-start(f32[64,256]{1,0:T(8,128)S(1)} %get-tuple-element.33), channel_id=1, source_target_pairs={{0,384},{128,0},{256,128},{384,256},{1,385},{129,1},{257,129},{385... | collective-permute-start | bytes 196616 | tf_op jit(solution)/shard_map/ppermute | solution.py:206
  177.8 12.6 %copy-start.8 = (f32[5,4,16,640]{3,2,1,0:T(8,128)S(1)}, f32[5,4,16,640]{3,2,1,0:T(8,128)}, u32[]{:S(2)}) copy-start(f32[5,4,16,640]{3,2,1,0:T(8,128)} %copy-done.7) | copy-start | bytes 2457604
  177.8 33.1 %all-to-all-start.6 = ((f32[32,11,8,128]{3,2,1,0:T(8,128)}), f32[32,11,8,128]{3,2,1,0:T(8,128)S(1)}, u32[]{:S(2)}, u32[]{:S(2)}) async-start(f32[32,11,8,128]{3,2,1,0:T(8,128)} %pad_maximum_fusion), calls=%async_computation.6 | async-start | bytes 2883584 | tf_op jit(solution)/shard_map/all_to_all | solution.py:184
  190.5 20.5 %copy-start.4 = (bf16[8,64,128]{2,1,0:T(8,128)(2,1)S(1)}, bf16[8,64,128]{2,1,0:T(8,128)(2,1)}, u32[]{:S(2)}) copy-start(bf16[8,64,128]{2,1,0:T(8,128)(2,1)} %mat_ref.1) | copy-start | bytes 393220

commit v5 on v4

--- a/solution.py
+++ b/solution.py
@@ -11,6 +11,8 @@
 NY, NZ, NX, NC = 4, 16, 4, 2
 NA = NX * NC
 NUB, UB, SIDE, DET = 5, 64, 256, 320
+HALF = SIDE // 2
+HIGHEST = lax.Precision.HIGHEST
 QC = UB // NY
 LANES = 2 * DET
 LIMIT = 16 << 20
@@ -19,13 +21,20 @@
 
 
 def dft_tables():
-    k = np.arange(SIDE)
-    ph = (k[:, None] * k[None, :] % SIDE) * (2.0 * np.pi / SIDE)
-    c, s = np.cos(ph) / np.sqrt(SIDE), np.sin(ph) / np.sqrt(SIDE)
-    both = np.stack([c, s, -s])
-    hi = both.astype(jnp.bfloat16)
-    lo = (both - hi.astype(np.float64)).astype(jnp.bfloat16)
-    return np.concatenate([hi, lo])
+    n, k = np.arange(HALF)[:, None], 2 * np.arange(HALF)[None, :]
+    out = []
+    for odd in range(2):
+        ph = (n * (k + odd) % SIDE) * (2.0 * np.pi / SIDE)
+        c, s = np.cos(ph) / np.sqrt(SIDE), np.sin(ph) / np.sqrt(SIDE)
+        full = np.block([[c, -s], [s, c]])
+        hi = full.astype(jnp.bfloat16)
+        out += [hi, (full - hi.astype(np.float64)).astype(jnp.bfloat16)]
+    return np.stack(out + [t.T for t in out])
+
+
+def even_first():
+    order = np.concatenate([np.arange(0, SIDE, 2), np.arange(1, SIDE, 2)])
+    return np.eye(SIDE, dtype=np.float32)[order]
 
 
 def split(v):
@@ -47,31 +56,49 @@
     return dot(hi, vh) + dot(hi, vl) + dot(lo, vh)
 
 
-def spot_kernel(where_ref, tr_ref, ti_ref, probe_ref, power_ref, tab_ref, resid_ref, keep_ref, send_ref, grads_ref, placed_ref, far_ref, big_ref, det_ref):
-    for k in range(2):
-        for t in range(2):
-            for i in range(2):
-                for j in range(2):
-                    of_s = 0 if i == j else (1 if (i > j) == (t == 0) else 2)
-                    big_ref[2 * t + k, i * SIDE : (i + 1) * SIDE, j * SIDE : (j + 1) * SIDE] = tab_ref[3 * k + of_s]
-    fwd, bwd = (big_ref[0], big_ref[1]), (big_ref[2], big_ref[3])
+def lanes(*parts):
+    return jnp.concatenate(parts, axis=1)
+
+
+def rows(*parts):
+    return jnp.concatenate(parts, axis=0)
+
+
+def halves(v, axis):
+    a, b = (v[:, :HALF], v[:, HALF:]) if axis else (v[:HALF], v[HALF:])
+    return a + b, a - b
+
+
+def spot_kernel(where_ref, tr_ref, ti_ref, probe_ref, power_ref, tab_ref, resid_ref, keep_ref, send_ref, grads_ref, placed_ref, far_ref, det_ref):
+    even, odd, even_t, odd_t = ((tab_ref[2 * i], tab_ref[2 * i + 1]) for i in range(4))
     first = where_ref[0] == 0
     resid_ref[...] = -power_ref[...]
     for m in range(4):
         tr, ti = tr_ref[...], ti_ref[...]
         pr, pi = (probe_ref[2 * m + k].astype(jnp.float32) for k in range(2))
-        mid = times(jnp.concatenate([pr * tr - pi * ti, pr * ti + pi * tr], axis=1), *fwd)
-        far = of(*bwd, jnp.concatenate([mid[:, :SIDE], mid[:, SIDE:]], axis=0))
-        far_ref[m] = far
-        resid_ref[...] += far[:SIDE] * far[:SIDE] + far[SIDE:] * far[SIDE:]
+        sr, dr = halves(pr * tr - pi * ti, 1)
+        si, di = halves(pr * ti + pi * tr, 1)
+        me, mo = times(lanes(sr, si), *even), times(lanes(dr, di), *odd)
+        sr, dr = halves(lanes(me[:, :HALF], mo[:, :HALF]), 0)
+        si, di = halves(lanes(me[:, HALF:], mo[:, HALF:]), 0)
+        fe, fo = of(*even_t, rows(sr, si)), of(*odd_t, rows(dr, di))
+        far_ref[m, :SIDE] = fe
+        far_ref[m, SIDE:] = fo
+        resid_ref[...] += rows(fe[:HALF] * fe[:HALF] + fe[HALF:] * fe[HALF:], fo[:HALF] * fo[:HALF] + fo[HALF:] * fo[HALF:])
     grads_ref[...] = jnp.zeros_like(grads_ref)
     for m in range(4):
         tr, ti = tr_ref[...], ti_ref[...]
         pr, pi = (probe_ref[2 * m + k].astype(jnp.float32) for k in range(2))
-        twice, far = 2.0 * resid_ref[...], far_ref[m]
-        back = of(*fwd, jnp.concatenate([far[:SIDE] * twice, far[SIDE:] * twice], axis=0))
-        g = times(jnp.concatenate([back[:SIDE], back[SIDE:]], axis=1), *bwd)
-        gr, gi = g[:, :SIDE], g[:, SIDE:]
+        twice = 2.0 * resid_ref[...]
+        te, to = twice[:HALF], twice[HALF:]
+        be = of(*even, far_ref[m, :SIDE] * rows(te, te))
+        bo = of(*odd, far_ref[m, SIDE:] * rows(to, to))
+        top, bottom = be + bo, be - bo
+        br, bi = rows(top[:HALF], bottom[:HALF]), rows(top[HALF:], bottom[HALF:])
+        ge = times(lanes(br[:, :HALF], bi[:, :HALF]), *even_t)
+        go = times(lanes(br[:, HALF:], bi[:, HALF:]), *odd_t)
+        left, right = ge + go, ge - go
+        gr, gi = lanes(left[:, :HALF], right[:, :HALF]), lanes(left[:, HALF:], right[:, HALF:])
         qr, qi = tr * gr + ti * gi, tr * gi - ti * gr
         keep_ref[m] = jnp.where(first, qr, qi)
         send_ref[m] = jnp.where(first, qi, qr)
@@ -111,7 +138,6 @@
         out_specs=(vmem,) * 5,
         scratch_shapes=[
             pltpu.VMEM((4, 2 * SIDE, SIDE), f32),
-            pltpu.VMEM((4, 2 * SIDE, 2 * SIDE), jnp.bfloat16),
             pltpu.VMEM((DET, LANES), f32),
         ],
         compiler_params=pltpu.CompilerParams(vmem_limit_bytes=LIMIT),
@@ -229,9 +255,12 @@
     absorb = jnp.exp(-p1)
     tr, ti = absorb * jnp.cos(p0), absorb * jnp.sin(p0)
     core = lax.axis_index("core")
+    order = jnp.asarray(even_first())
+    turn = lambda p, v: jnp.dot(jnp.dot(p, v, precision=HIGHEST), p.T, precision=HIGHEST)
     resid, keep, send, grads, placed = spot(
-        jnp.stack([core, col, row]), tr, ti, modes.reshape(8, SIDE, SIDE), power[0, 0], jnp.asarray(dft_tables())
-    )
+        jnp.stack([core, col, row]), tr, ti, modes.reshape(8, SIDE, SIDE), turn(order, power[0, 0]), jnp.asarray(dft_tables())
+    )
+    resid = turn(order.T, resid)
 
     d_col = sum(jnp.sum(g_ * (w[2:, 1:-1] - w[:-2, 1:-1])) for g_, w in zip((grads[0], grads[1]), wins))
     d_row = sum(jnp.sum(g_ * (w[1:-1, 2:] - w[1:-1, :-2])) for g_, w in zip((grads[0], grads[1]), wins))

time: 213 us -> 212 us (level)
  waiting for transfers between devices: 43.7 us -> 37.5 us
  matrix products: 0 us -> 4.59 us
  Pallas kernels: 13.8 us -> 10.1 us
    all_to_all x5, waiting for transfers between devices: 41.3 us -> 36.3 us  [exchange(): return lax.all_to_all(x, axes, split_axis=0, concat_axis=0, tiled=True)]
    dot_general x0 -> x4, matrix products: none -> 4.59 us  [the longest x2 2.66 us: step(): jnp.dot(jnp.dot(p, v, precision=HIGHEST), p.T, precision=HIGHEST)]
    pallas_call x1, Pallas kernels: 10.8 us -> 7.21 us  [spot(): pl.pallas_call(spot_kernel, out_shape=(plane, half, half, jax.ShapeDtypeS...]
  transfers between devices with their start and end apart: 12 -> 12, of which waited for: 6 -> 5; matrix products, arithmetic and copies ran while one was open for 4% -> 7% of each run, Pallas kernels for 0% -> 0%
where the time goes in v5:
time: 212 us; the launch traced here: 211 us
  starting transfers between devices  71.8 us (34%)
  blocking collectives  61.1 us (29%)
  waiting for transfers between devices  37.5 us (18%)
  other arithmetic  11.4 us (5%)
  Pallas kernels  10.1 us (5%)
  between operations  7.67 us (4%)
  local copies, waits for them, and re-layouts  6.36 us (3%)
  matrix products  4.59 us (2%)
    all_to_all x2, blocking collectives, exchange(): return lax.all_to_all(x, axes, split_axis=0, concat_axis=0, tiled=True)  48.9 us
    all_to_all x5, starting transfers between devices, exchange(): return lax.all_to_all(x, axes, split_axis=0, concat_axis=0, tiled=True)  41.1 us
    all_to_all x5, waiting for transfers between devices, exchange(): return lax.all_to_all(x, axes, split_axis=0, concat_axis=0, tiled=True)  36.3 us
    ppermute x7, starting transfers between devices, shift(): return lax.ppermute(x, axis, [(i, (i + by) % size) for i in range(size)])  30.7 us
    all_gather x1, blocking collectives, step(): every = lax.all_gather(summed, 'y', axis=0, tiled=False)  12.2 us
    pallas_call x1, Pallas kernels, spot(): pl.pallas_call(spot_kernel, out_shape=(plane, half, half, jax.ShapeDtypeS...  7.21 us
  transfers between devices with their start and end apart: 12, of which 5 were waited for; matrix products, arithmetic and copies ran while one was open for 7% of the time, Pallas kernels for 0%

profile of v5, /device:TPU:1, one launch (start us, length us, event | category | flops | bytes accessed | tf_op | source)
XLA Modules:
  0.0 210.6 jit_solution(4888092366109388440)
XLA Ops:
  0.7 0.9 copy-done.3
  2.5 1.5 rays.1
  4.0 10.4 %all-to-all-start = ((f32[32,16,640]{2,1,0:T(8,128)}), f32[32,16,640]{2,1,0:T(8,128)S(1)}, u32[]{:S(2)}, u32[]{:S(2)}) async-start(f32[32,16,640]{2,1,0:T(8,128)} %rays.1), calls=%async_computation | async-start | bytes 2621440 | tf_op jit(solution)/shard_map/all_to_all | solution.py:210
  15.9 18.0 %all-to-all-done = f32[32,16,640]{2,1,0:T(8,128)S(1)} async-done(((f32[32,16,640]{2,1,0:T(8,128)}), f32[32,16,640]{2,1,0:T(8,128)S(1)}, u32[]{:S(2)}, u32[]{:S(2)}) %all-to-all-start) | async-done | bytes 1310752 | tf_op jit(solution)/shard_map/all_to_all | solution.py:210
  34.5 25.1 %all_to_all.35 = f32[16,25,1,128]{3,2,1,0:T(1,128)S(1)} all-to-all(f32[16,25,1,128]{3,2,1,0:T(1,128)S(1)} %bitcast.120), channel_id=1, replica_groups=mesh['y'=4,'z'=16,'x'=4,'core'=2] {'z'}, dimensions={0} | all-to-all | bytes 409600 | tf_op jit(solution)/shard_map/all_to_all | solution.py:210
  60.5 8.9 %all-to-all-start.2 = ((f32[16,25,1,128]{3,2,1,0:T(1,128)}), f32[16,25,1,128]{3,2,1,0:T(1,128)S(1)}, u32[]{:S(2)}, u32[]{:S(2)}) async-start(f32[16,25,1,128]{3,2,1,0:T(1,128)} %broadcast_in_dim.143), calls=%async_computation.2 | async-start | bytes 409600 | tf_op jit(solution)/shard_map/all_to_all | solution.py:210
  73.9 1.4 pad_add_fusion.where_ref
  76.0 5.7 %all-to-all-done.2 = f32[16,25,1,128]{3,2,1,0:T(1,128)S(1)} async-done(((f32[16,25,1,128]{3,2,1,0:T(1,128)}), f32[16,25,1,128]{3,2,1,0:T(1,128)S(1)}, u32[]{:S(2)}, u32[]{:S(2)}) %all-to-all-start.2) | async-done | bytes 204832 | tf_op jit(solution)/shard_map/all_to_all | solution.py:210
  81.7 12.2 %all_gather.3 = f32[4,50,8,128]{3,2,1,0:T(8,128)S(1)} all-gather(f32[1,50,8,128]{3,2,1,0:T(8,128)S(1)} %bitcast.119), channel_id=1, replica_groups=mesh['y'=4,'z'=16,'x'=4,'core'=2] {'y'}, dimensions={0}, use_global_device_ids=true | all-gather | bytes 1024000 | tf_op jit(solution)/shard_map/all_gather | solution.py:248
  94.0 1.1 sine_multiply_fusion
  95.8 7.2 %spot.1 = (f32[256,256]{1,0:T(8,128)S(1)}, f32[4,256,256]{2,1,0:T(8,128)S(1)}, f32[4,256,256]{2,1,0:T(8,128)S(1)}, f32[2,256,256]{2,1,0:T(8,128)S(1)}, f32[4,50,8,128]{3,2,1,0:T(8,128)}) custom-call(s32[3]{0:T(128)S(1)} %pad_add_fusion.where_ref, f32[256,256]{1,0:T(8,128)S(1)} %get-tuple-element.31.tr_ref, f32[256,256]{1,0:T(8,128)S(1)} %get-tuple-element.30.ti_ref, ...), custom_call_target="tpu_custom_call" | custom-call | tf_op jit(solution)/shard_map/spot/pallas_call | solution.py:128
  103.0 9.3 %collective-permute-start = (f32[4,256,256]{2,1,0:T(8,128)S(1)}, f32[4,256,256]{2,1,0:T(8,128)}, u32[]{:S(2)}, u32[]{:S(2)}) collective-permute-start(f32[4,256,256]{2,1,0:T(8,128)S(1)} %get-tuple-element.13), channel_id=1, source_target_pairs={{0,1},{1,0},{2,3},{3,2},{4,5},{5,4},{6,7},{7,6},{8,9},{9,8},{10,11... | collective-permute-start | bytes 3145736 | tf_op jit(solution)/shard_map/ppermute | solution.py:232
  112.3 4.2 %all-to-all-start.3 = ((f32[4,50,8,128]{3,2,1,0:T(8,128)}), f32[4,50,8,128]{3,2,1,0:T(8,128)}, u32[]{:S(2)}, u32[]{:S(2)}) async-start(f32[4,50,8,128]{3,2,1,0:T(8,128)} %get-tuple-element.11), calls=%async_computation.3 | async-start | bytes 1638400 | tf_op jit(solution)/shard_map/all_to_all | solution.py:210
  116.6 1.4 add.150
  118.8 3.7 %collective-permute-start.1 = (f32[256,256]{1,0:T(8,128)}, f32[256,256]{1,0:T(8,128)S(1)}, u32[]{:S(2)}, u32[]{:S(2)}) collective-permute-start(f32[256,256]{1,0:T(8,128)} %get-tuple-element.27), channel_id=1, source_target_pairs={{0,4},{2,6},{4,0},{6,2},{1,5},{3,7},{5,1},{7,3},{8,12},{10,14},{12... | collective-permute-start | bytes 786440 | tf_op jit(solution)/shard_map/ppermute | solution.py:232
  122.5 1.9 collective-permute-start.2
  124.4 4.6 %collective-permute-start.3 = (f32[256,256]{1,0:T(8,128)S(1)}, f32[256,256]{1,0:T(8,128)}, u32[]{:S(2)}, u32[]{:S(2)}) collective-permute-start(f32[256,256]{1,0:T(8,128)S(1)} %get-tuple-element.28), channel_id=1, source_target_pairs={{0,6},{2,0},{4,2},{6,4},{1,7},{3,1},{5,3},{7,5},{8,14},{10,8},{12,... | collective-permute-start | bytes 786440 | tf_op jit(solution)/shard_map/ppermute | solution.py:232
  129.3 1.9 reduce_sum.123
  131.2 5.0 %all-to-all-start.4 = ((f32[16,25,1,128]{3,2,1,0:T(1,128)}), f32[16,25,1,128]{3,2,1,0:T(1,128)S(1)}, u32[]{:S(2)}, u32[]{:S(2)}) async-start(f32[16,25,1,128]{3,2,1,0:T(1,128)} %bitcast.28), calls=%async_computation.4 | async-start | bytes 409600 | tf_op jit(solution)/shard_map/all_to_all | solution.py:210
  136.3 1.0 fusion.10
  137.4 4.6 %collective-permute-start.4 = (f32[64,256]{1,0:T(8,128)S(1)}, f32[64,256]{1,0:T(8,128)S(1)}, u32[]{:S(2)}, u32[]{:S(2)}) collective-permute-start(f32[64,256]{1,0:T(8,128)S(1)} %get-tuple-element.32), channel_id=1, source_target_pairs={{0,256},{128,384},{256,0},{384,128},{1,257},{129,385},{257,1},{385... | collective-permute-start | bytes 196616 | tf_op jit(solution)/shard_map/ppermute | solution.py:232
  142.0 2.2 %collective-permute-start.5 = (f32[64,256]{1,0:T(8,128)S(1)}, f32[64,256]{1,0:T(8,128)S(1)}, u32[]{:S(2)}, u32[]{:S(2)}) collective-permute-start(f32[64,256]{1,0:T(8,128)S(1)} %get-tuple-element.34), channel_id=1, source_target_pairs={{0,128},{128,256},{256,384},{384,0},{1,129},{129,257},{257,385},{3... | collective-permute-start | bytes 196616 | tf_op jit(solution)/shard_map/ppermute | solution.py:232
  144.3 4.3 %collective-permute-start.6 = (f32[64,256]{1,0:T(8,128)S(1)}, f32[64,256]{1,0:T(8,128)S(1)}, u32[]{:S(2)}, u32[]{:S(2)}) collective-permute-start(f32[64,256]{1,0:T(8,128)S(1)} %get-tuple-element.33), channel_id=1, source_target_pairs={{0,384},{128,0},{256,128},{384,256},{1,385},{129,1},{257,129},{385... | collective-permute-start | bytes 196616 | tf_op jit(solution)/shard_map/ppermute | solution.py:232
  148.6 1.3 collective-permute-done.6
  150.5 23.8 %all_to_all.36 = f32[16,33,1,128]{3,2,1,0:T(1,128)S(1)} all-to-all(f32[16,33,1,128]{3,2,1,0:T(1,128)S(1)} %pad_maximum_fusion.1), channel_id=1, replica_groups=mesh['y'=4,'z'=16,'x'=4,'core'=2] {'z'}, dimensions={0} | all-to-all | bytes 540672 | tf_op jit(solution)/shard_map/all_to_all | solution.py:210
  174.8 1.2 pad_maximum_fusion
  176.1 12.6 %all-to-all-start.6 = ((f32[32,11,8,128]{3,2,1,0:T(8,128)}), f32[32,11,8,128]{3,2,1,0:T(8,128)S(1)}, u32[]{:S(2)}, u32[]{:S(2)}) async-start(f32[32,11,8,128]{3,2,1,0:T(8,128)} %pad_maximum_fusion), calls=%async_computation.6 | async-start | bytes 2883584 | tf_op jit(solution)/shard_map/all_to_all | solution.py:210
  188.7 1.3 fusion.5
  193.1 1.5 fusion.17
  194.7 2.3 %convolution_bitcast_fusion = f32[1,1,256,256]{3,2,1,0:T(8,128)} fusion(f32[256,256]{1,0:T(8,128)S(1)} %fusion.17, f32[256,256]{1,0:T(8,128)} %constant.126.clone), kind=kOutput, calls=%fused_computation.7 | convolution fusion | flops 201326592 | bytes 786432 | tf_op jit(solution)/shard_map/dot_general | solution.py:259
  196.9 12.3 %all-to-all-done.6.got_ref = f32[32,11,8,128]{3,2,1,0:T(8,128)S(1)} async-done(((f32[32,11,8,128]{3,2,1,0:T(8,128)}), f32[32,11,8,128]{3,2,1,0:T(8,128)S(1)}, u32[]{:S(2)}, u32[]{:S(2)}) %all-to-all-start.6) | async-done | bytes 1441824 | tf_op jit(solution)/shard_map/all_to_all | solution.py:210
  209.2 1.4 volume.1
  (62 shorter events, 8.7 us)
Async XLA Ops:
  0.6 74.6 %copy-start = (f32[1,1,256,256]{3,2,1,0:T(8,128)S(1)}, f32[1,1,256,256]{3,2,1,0:T(8,128)}, u32[]{:S(2)}) copy-start(f32[1,1,256,256]{3,2,1,0:T(8,128)} %param.13) | copy-start | bytes 786436
  0.6 0.9 copy-start.3
  1.6 0.9 copy-start.5
  4.0 29.8 %all-to-all-start = ((f32[32,16,640]{2,1,0:T(8,128)}), f32[32,16,640]{2,1,0:T(8,128)S(1)}, u32[]{:S(2)}, u32[]{:S(2)}) async-start(f32[32,16,640]{2,1,0:T(8,128)} %rays.1), calls=%async_computation | async-start | bytes 2621440 | tf_op jit(solution)/shard_map/all_to_all | solution.py:210
  15.9 53.5 %copy-start.9 = (s32[1,1,2]{2,1,0:T(1,128)S(1)}, s32[1,1,2]{2,1,0:T(1,128)}, u32[]{:S(2)}) copy-start(s32[1,1,2]{2,1,0:T(1,128)} %param.12) | copy-start | bytes 28
  15.9 59.3 %copy-start.8 = (f32[256,256]{1,0:T(8,128)S(1)}, f32[256,256]{1,0:T(8,128)}, u32[]{:S(2)}) copy-start(f32[256,256]{1,0:T(8,128)} %constant.126.clone) | copy-start | bytes 786436
  60.5 21.2 %all-to-all-start.2 = ((f32[16,25,1,128]{3,2,1,0:T(1,128)}), f32[16,25,1,128]{3,2,1,0:T(1,128)S(1)}, u32[]{:S(2)}, u32[]{:S(2)}) async-start(f32[16,25,1,128]{3,2,1,0:T(1,128)} %broadcast_in_dim.143), calls=%async_computation.2 | async-start | bytes 409600 | tf_op jit(solution)/shard_map/all_to_all | solution.py:210
  93.9 1.5 copy-start.1
  93.9 1.8 copy-start.2
  94.0 1.2 copy-start.6
  103.0 13.6 %collective-permute-start = (f32[4,256,256]{2,1,0:T(8,128)S(1)}, f32[4,256,256]{2,1,0:T(8,128)}, u32[]{:S(2)}, u32[]{:S(2)}) collective-permute-start(f32[4,256,256]{2,1,0:T(8,128)S(1)} %get-tuple-element.13), channel_id=1, source_target_pairs={{0,1},{1,0},{2,3},{3,2},{4,5},{5,4},{6,7},{7,6},{8,9},{9,8},{10,11... | collective-permute-start | bytes 3145736 | tf_op jit(solution)/shard_map/ppermute | solution.py:232
  112.3 17.0 %all-to-all-start.3 = ((f32[4,50,8,128]{3,2,1,0:T(8,128)}), f32[4,50,8,128]{3,2,1,0:T(8,128)}, u32[]{:S(2)}, u32[]{:S(2)}) async-start(f32[4,50,8,128]{3,2,1,0:T(8,128)} %get-tuple-element.11), calls=%async_computation.3 | async-start | bytes 1638400 | tf_op jit(solution)/shard_map/all_to_all | solution.py:210
  118.8 17.5 %collective-permute-start.1 = (f32[256,256]{1,0:T(8,128)}, f32[256,256]{1,0:T(8,128)S(1)}, u32[]{:S(2)}, u32[]{:S(2)}) collective-permute-start(f32[256,256]{1,0:T(8,128)} %get-tuple-element.27), channel_id=1, source_target_pairs={{0,4},{2,6},{4,0},{6,2},{1,5},{3,7},{5,1},{7,3},{8,12},{10,14},{12... | collective-permute-start | bytes 786440 | tf_op jit(solution)/shard_map/ppermute | solution.py:232
  122.5 13.8 %collective-permute-start.2 = (f32[256,256]{1,0:T(8,128)S(1)}, f32[256,256]{1,0:T(8,128)S(1)}, u32[]{:S(2)}, u32[]{:S(2)}) collective-permute-start(f32[256,256]{1,0:T(8,128)S(1)} %get-tuple-element.29), channel_id=1, source_target_pairs={{0,2},{2,4},{4,6},{6,0},{1,3},{3,5},{5,7},{7,1},{8,10},{10,12},{12... | collective-permute-start | bytes 786440 | tf_op jit(solution)/shard_map/ppermute | solution.py:232
  124.4 11.9 %collective-permute-start.3 = (f32[256,256]{1,0:T(8,128)S(1)}, f32[256,256]{1,0:T(8,128)}, u32[]{:S(2)}, u32[]{:S(2)}) collective-permute-start(f32[256,256]{1,0:T(8,128)S(1)} %get-tuple-element.28), channel_id=1, source_target_pairs={{0,6},{2,0},{4,2},{6,4},{1,7},{3,1},{5,3},{7,5},{8,14},{10,8},{12,... | collective-permute-start | bytes 786440 | tf_op jit(solution)/shard_map/ppermute | solution.py:232
  131.2 18.7 %all-to-all-start.4 = ((f32[16,25,1,128]{3,2,1,0:T(1,128)}), f32[16,25,1,128]{3,2,1,0:T(1,128)S(1)}, u32[]{:S(2)}, u32[]{:S(2)}) async-start(f32[16,25,1,128]{3,2,1,0:T(1,128)} %bitcast.28), calls=%async_computation.4 | async-start | bytes 409600 | tf_op jit(solution)/shard_map/all_to_all | solution.py:210
  137.4 11.2 %collective-permute-start.4 = (f32[64,256]{1,0:T(8,128)S(1)}, f32[64,256]{1,0:T(8,128)S(1)}, u32[]{:S(2)}, u32[]{:S(2)}) collective-permute-start(f32[64,256]{1,0:T(8,128)S(1)} %get-tuple-element.32), channel_id=1, source_target_pairs={{0,256},{128,384},{256,0},{384,128},{1,257},{129,385},{257,1},{385... | collective-permute-start | bytes 196616 | tf_op jit(solution)/shard_map/ppermute | solution.py:232
  142.0 6.5 %collective-permute-start.5 = (f32[64,256]{1,0:T(8,128)S(1)}, f32[64,256]{1,0:T(8,128)S(1)}, u32[]{:S(2)}, u32[]{:S(2)}) collective-permute-start(f32[64,256]{1,0:T(8,128)S(1)} %get-tuple-element.34), channel_id=1, source_target_pairs={{0,128},{128,256},{256,384},{384,0},{1,129},{129,257},{257,385},{3... | collective-permute-start | bytes 196616 | tf_op jit(solution)/shard_map/ppermute | solution.py:232
  144.3 5.6 %collective-permute-start.6 = (f32[64,256]{1,0:T(8,128)S(1)}, f32[64,256]{1,0:T(8,128)S(1)}, u32[]{:S(2)}, u32[]{:S(2)}) collective-permute-start(f32[64,256]{1,0:T(8,128)S(1)} %get-tuple-element.33), channel_id=1, source_target_pairs={{0,384},{128,0},{256,128},{384,256},{1,385},{129,1},{257,129},{385... | collective-permute-start | bytes 196616 | tf_op jit(solution)/shard_map/ppermute | solution.py:232
  176.0 12.6 %copy-start.7 = (f32[5,4,16,640]{3,2,1,0:T(8,128)S(1)}, f32[5,4,16,640]{3,2,1,0:T(8,128)}, u32[]{:S(2)}) copy-start(f32[5,4,16,640]{3,2,1,0:T(8,128)} %copy-done.6) | copy-start | bytes 2457604
  176.1 33.1 %all-to-all-start.6 = ((f32[32,11,8,128]{3,2,1,0:T(8,128)}), f32[32,11,8,128]{3,2,1,0:T(8,128)S(1)}, u32[]{:S(2)}, u32[]{:S(2)}) async-start(f32[32,11,8,128]{3,2,1,0:T(8,128)} %pad_maximum_fusion), calls=%async_computation.6 | async-start | bytes 2883584 | tf_op jit(solution)/shard_map/all_to_all | solution.py:210
  189.9 19.3 %copy-start.4 = (bf16[8,64,128]{2,1,0:T(8,128)(2,1)S(1)}, bf16[8,64,128]{2,1,0:T(8,128)(2,1)}, u32[]{:S(2)}) copy-start(bf16[8,64,128]{2,1,0:T(8,128)(2,1)} %mat_ref.1) | copy-start | bytes 393220

commit v6 on v5

--- a/solution.py
+++ b/solution.py
@@ -145,7 +145,13 @@
     )(where, tr, ti, probe, power, tab)
 
 
-def rays_kernel(vol_ref, mat_ref, out_ref, tile_ref):
+def rays_kernel(vol_hbm, mat_hbm, out_ref, vol_ref, mat_ref, tile_ref, sems):
+    first = pltpu.make_async_copy(vol_hbm, vol_ref, sems.at[0])
+    second = pltpu.make_async_copy(mat_hbm, mat_ref, sems.at[1])
+    first.start()
+    second.start()
+    first.wait()
+    second.wait()
     tile_ref[:, :DET] = vol_ref[0].astype(jnp.float32)
     tile_ref[:, DET:] = vol_ref[1].astype(jnp.float32)
     tile = tile_ref[...].astype(jnp.bfloat16)
@@ -160,10 +166,14 @@
     return pl.pallas_call(
         rays_kernel,
         out_shape=jax.ShapeDtypeStruct((32, QC, LANES), jnp.float32),
-        in_specs=[vmem] * 2,
+        in_specs=[pl.BlockSpec(memory_space=pltpu.HBM)] * 2,
         out_specs=vmem,
-        scratch_shapes=[pltpu.VMEM((128, LANES), jnp.float32)],
-        compiler_params=pltpu.CompilerParams(vmem_limit_bytes=LIMIT),
+        scratch_shapes=[
+            pltpu.VMEM((2, 128, DET), jnp.bfloat16),
+            pltpu.VMEM((NA, UB, 128), jnp.bfloat16),
+            pltpu.VMEM((128, LANES), jnp.float32),
+            pltpu.SemaphoreType.DMA((2,)),
+        ],
         name="rays",
     )(volume, matrices)
 
@@ -206,6 +216,26 @@
     )(y, got, matrices)
 
 
+def blocks_kernel(ids_ref, quarter_ref, piece_ref, out_ref):
+    for i in range(32):
+        at = ids_ref[i] * 10
+        for v in range(10):
+            out_ref[i, v] = quarter_ref[at + v]
+        out_ref[i, 10] = piece_ref[...]
+
+
+def blocks_of(ids, quarter, piece):
+    vmem = pl.BlockSpec(memory_space=pltpu.VMEM)
+    return pl.pallas_call(
+        blocks_kernel,
+        out_shape=jax.ShapeDtypeStruct((32, 11, 8, 128), jnp.float32),
+        in_specs=[pl.BlockSpec(memory_space=pltpu.SMEM)] + [vmem] * 2,
+        out_specs=vmem,
+        compiler_params=pltpu.CompilerParams(vmem_limit_bytes=LIMIT),
+        name="blocks",
+    )(ids, quarter, piece)
+
+
 def exchange(x, axes):
     return lax.all_to_all(x, axes, split_axis=0, concat_axis=0, tiled=True)
 
@@ -279,11 +309,7 @@
     mine = part.sum(0)
     got = exchange(jnp.concatenate([jnp.broadcast_to(mine[None], (NZ, 25, 1, 128)), rows], axis=1), "z")
     piece = got[:, 25:].sum(0).reshape(8, 128)
-    quarter = got[:, :25].reshape(NUB, 10, 8, 128)
-    sent = quarter[0][None]
-    for d in range(1, NUB):
-        sent = jnp.where((ids == d)[:, None, None, None], quarter[d][None], sent)
-    sent = jnp.concatenate([sent, jnp.broadcast_to(piece[None, None], (32, 1, 8, 128))], axis=1)
+    sent = blocks_of(ids, got[:, :25].reshape(50, 8, 128), piece)
     got = exchange(sent, ("y", "x", "core"))
     vol_grad, probe_grad = volume_of(y.reshape(1), got, matrices.reshape(512, 128))
     vol_grad = vol_grad.reshape(2, 8, 16, DET)

time: 212 us -> 211 us (level)
  Pallas kernels: 10.1 us -> 13.2 us
  local copies, waits for them, and re-layouts: 6.36 us -> 4.12 us
where the time goes in v6:
time: 211 us; the launch traced here: 210 us
  starting transfers between devices  71.9 us (34%)
  blocking collectives  61.1 us (29%)
  waiting for transfers between devices  37.9 us (18%)
  Pallas kernels  13.2 us (6%)
  other arithmetic  9.81 us (5%)
  between operations  7.65 us (4%)
  matrix products  4.59 us (2%)
  local copies, waits for them, and re-layouts  4.12 us (2%)
    all_to_all x2, blocking collectives, exchange(): return lax.all_to_all(x, axes, split_axis=0, concat_axis=0, tiled=True)  48.9 us
    all_to_all x5, starting transfers between devices, exchange(): return lax.all_to_all(x, axes, split_axis=0, concat_axis=0, tiled=True)  41.2 us
    all_to_all x5, waiting for transfers between devices, exchange(): return lax.all_to_all(x, axes, split_axis=0, concat_axis=0, tiled=True)  36.6 us
    ppermute x7, starting transfers between devices, shift(): return lax.ppermute(x, axis, [(i, (i + by) % size) for i in range(size)])  30.7 us
    all_gather x1, blocking collectives, step(): every = lax.all_gather(summed, 'y', axis=0, tiled=False)  12.2 us
    pallas_call x1, Pallas kernels, spot(): pl.pallas_call(spot_kernel, out_shape=(plane, half, half, jax.ShapeDtypeS...  7.44 us
  transfers between devices with their start and end apart: 12, of which 5 were waited for; matrix products, arithmetic and copies ran while one was open for 7% of the time, Pallas kernels for 0%

profile of v6, /device:TPU:1, one launch (start us, length us, event | category | flops | bytes accessed | tf_op | source)
XLA Modules:
  0.0 210.3 jit_solution(11393495905908094771)
XLA Ops:
  0.6 2.6 %rays.1 = f32[32,16,640]{2,1,0:T(8,128)} custom-call(bf16[2,128,320]{2,1,0:T(8,128)(2,1)} %bitcast.102, bf16[8,64,128]{2,1,0:T(8,128)(2,1)} %mat_hbm.1), custom_call_target="tpu_custom_call" | custom-call | tf_op jit(solution)/shard_map/rays/pallas_call | solution.py:166
  3.2 10.5 %all-to-all-start = ((f32[32,16,640]{2,1,0:T(8,128)}), f32[32,16,640]{2,1,0:T(8,128)S(1)}, u32[]{:S(2)}, u32[]{:S(2)}) async-start(f32[32,16,640]{2,1,0:T(8,128)} %rays.1), calls=%async_computation | async-start | bytes 2621440 | tf_op jit(solution)/shard_map/all_to_all | solution.py:240
  14.8 18.3 %all-to-all-done = f32[32,16,640]{2,1,0:T(8,128)S(1)} async-done(((f32[32,16,640]{2,1,0:T(8,128)}), f32[32,16,640]{2,1,0:T(8,128)S(1)}, u32[]{:S(2)}, u32[]{:S(2)}) %all-to-all-start) | async-done | bytes 1310752 | tf_op jit(solution)/shard_map/all_to_all | solution.py:240
  33.7 25.1 %all_to_all.35 = f32[16,25,1,128]{3,2,1,0:T(1,128)S(1)} all-to-all(f32[16,25,1,128]{3,2,1,0:T(1,128)S(1)} %bitcast.101), channel_id=1, replica_groups=mesh['y'=4,'z'=16,'x'=4,'core'=2] {'z'}, dimensions={0} | all-to-all | bytes 409600 | tf_op jit(solution)/shard_map/all_to_all | solution.py:240
  58.9 0.8 broadcast_in_dim.63
  59.7 8.9 %all-to-all-start.2 = ((f32[16,25,1,128]{3,2,1,0:T(1,128)}), f32[16,25,1,128]{3,2,1,0:T(1,128)S(1)}, u32[]{:S(2)}, u32[]{:S(2)}) async-start(f32[16,25,1,128]{3,2,1,0:T(1,128)} %broadcast_in_dim.63), calls=%async_computation.2 | async-start | bytes 409600 | tf_op jit(solution)/shard_map/all_to_all | solution.py:240
  73.1 1.4 pad_add_fusion.where_ref
  75.3 5.7 %all-to-all-done.2 = f32[16,25,1,128]{3,2,1,0:T(1,128)S(1)} async-done(((f32[16,25,1,128]{3,2,1,0:T(1,128)}), f32[16,25,1,128]{3,2,1,0:T(1,128)S(1)}, u32[]{:S(2)}, u32[]{:S(2)}) %all-to-all-start.2) | async-done | bytes 204832 | tf_op jit(solution)/shard_map/all_to_all | solution.py:240
  80.9 12.2 %all_gather.3 = f32[4,50,8,128]{3,2,1,0:T(8,128)S(1)} all-gather(f32[1,50,8,128]{3,2,1,0:T(8,128)S(1)} %bitcast.100), channel_id=1, replica_groups=mesh['y'=4,'z'=16,'x'=4,'core'=2] {'y'}, dimensions={0}, use_global_device_ids=true | all-gather | bytes 1024000 | tf_op jit(solution)/shard_map/all_gather | solution.py:278
  93.2 1.1 sine_multiply_fusion
  95.0 7.4 %spot.1 = (f32[256,256]{1,0:T(8,128)S(1)}, f32[4,256,256]{2,1,0:T(8,128)S(1)}, f32[4,256,256]{2,1,0:T(8,128)S(1)}, f32[2,256,256]{2,1,0:T(8,128)S(1)}, f32[4,50,8,128]{3,2,1,0:T(8,128)}) custom-call(s32[3]{0:T(128)S(1)} %pad_add_fusion.where_ref, f32[256,256]{1,0:T(8,128)S(1)} %get-tuple-element.31.tr_ref, f32[256,256]{1,0:T(8,128)S(1)} %get-tuple-element.30.ti_ref, ...), custom_call_target="tpu_custom_call" | custom-call | tf_op jit(solution)/shard_map/spot/pallas_call | solution.py:128
  102.4 9.3 %collective-permute-start = (f32[4,256,256]{2,1,0:T(8,128)S(1)}, f32[4,256,256]{2,1,0:T(8,128)}, u32[]{:S(2)}, u32[]{:S(2)}) collective-permute-start(f32[4,256,256]{2,1,0:T(8,128)S(1)} %get-tuple-element.13), channel_id=1, source_target_pairs={{0,1},{1,0},{2,3},{3,2},{4,5},{5,4},{6,7},{7,6},{8,9},{9,8},{10,11... | collective-permute-start | bytes 3145736 | tf_op jit(solution)/shard_map/ppermute | solution.py:262
  111.8 4.2 %all-to-all-start.3 = ((f32[4,50,8,128]{3,2,1,0:T(8,128)}), f32[4,50,8,128]{3,2,1,0:T(8,128)}, u32[]{:S(2)}, u32[]{:S(2)}) async-start(f32[4,50,8,128]{3,2,1,0:T(8,128)} %get-tuple-element.11), calls=%async_computation.3 | async-start | bytes 1638400 | tf_op jit(solution)/shard_map/all_to_all | solution.py:240
  116.0 1.4 add.150
  118.2 3.7 %collective-permute-start.1 = (f32[256,256]{1,0:T(8,128)}, f32[256,256]{1,0:T(8,128)S(1)}, u32[]{:S(2)}, u32[]{:S(2)}) collective-permute-start(f32[256,256]{1,0:T(8,128)} %get-tuple-element.27), channel_id=1, source_target_pairs={{0,4},{2,6},{4,0},{6,2},{1,5},{3,7},{5,1},{7,3},{8,12},{10,14},{12... | collective-permute-start | bytes 786440 | tf_op jit(solution)/shard_map/ppermute | solution.py:262
  122.0 1.9 collective-permute-start.2
  123.9 4.6 %collective-permute-start.3 = (f32[256,256]{1,0:T(8,128)S(1)}, f32[256,256]{1,0:T(8,128)}, u32[]{:S(2)}, u32[]{:S(2)}) collective-permute-start(f32[256,256]{1,0:T(8,128)S(1)} %get-tuple-element.28), channel_id=1, source_target_pairs={{0,6},{2,0},{4,2},{6,4},{1,7},{3,1},{5,3},{7,5},{8,14},{10,8},{12,... | collective-permute-start | bytes 786440 | tf_op jit(solution)/shard_map/ppermute | solution.py:262
  128.8 1.9 reduce_sum.123
  130.7 5.0 %all-to-all-start.4 = ((f32[16,25,1,128]{3,2,1,0:T(1,128)}), f32[16,25,1,128]{3,2,1,0:T(1,128)S(1)}, u32[]{:S(2)}, u32[]{:S(2)}) async-start(f32[16,25,1,128]{3,2,1,0:T(1,128)} %bitcast.28), calls=%async_computation.4 | async-start | bytes 409600 | tf_op jit(solution)/shard_map/all_to_all | solution.py:240
  135.8 1.1 fusion.10
  136.9 4.7 %collective-permute-start.4 = (f32[64,256]{1,0:T(8,128)S(1)}, f32[64,256]{1,0:T(8,128)S(1)}, u32[]{:S(2)}, u32[]{:S(2)}) collective-permute-start(f32[64,256]{1,0:T(8,128)S(1)} %get-tuple-element.32), channel_id=1, source_target_pairs={{0,256},{128,384},{256,0},{384,128},{1,257},{129,385},{257,1},{385... | collective-permute-start | bytes 196616 | tf_op jit(solution)/shard_map/ppermute | solution.py:262
  141.6 2.2 %collective-permute-start.5 = (f32[64,256]{1,0:T(8,128)S(1)}, f32[64,256]{1,0:T(8,128)S(1)}, u32[]{:S(2)}, u32[]{:S(2)}) collective-permute-start(f32[64,256]{1,0:T(8,128)S(1)} %get-tuple-element.34), channel_id=1, source_target_pairs={{0,128},{128,256},{256,384},{384,0},{1,129},{129,257},{257,385},{3... | collective-permute-start | bytes 196616 | tf_op jit(solution)/shard_map/ppermute | solution.py:262
  143.8 4.3 %collective-permute-start.6 = (f32[64,256]{1,0:T(8,128)S(1)}, f32[64,256]{1,0:T(8,128)S(1)}, u32[]{:S(2)}, u32[]{:S(2)}) collective-permute-start(f32[64,256]{1,0:T(8,128)S(1)} %get-tuple-element.33), channel_id=1, source_target_pairs={{0,384},{128,0},{256,128},{384,256},{1,385},{129,1},{257,129},{385... | collective-permute-start | bytes 196616 | tf_op jit(solution)/shard_map/ppermute | solution.py:262
  148.1 1.3 collective-permute-done.6
  150.0 23.8 %all_to_all.36 = f32[16,33,1,128]{3,2,1,0:T(1,128)S(1)} all-to-all(f32[16,33,1,128]{3,2,1,0:T(1,128)S(1)} %pad_maximum_fusion), channel_id=1, replica_groups=mesh['y'=4,'z'=16,'x'=4,'core'=2] {'z'}, dimensions={0} | all-to-all | bytes 540672 | tf_op jit(solution)/shard_map/all_to_all | solution.py:240
  173.8 1.8 blocks.1
  175.6 12.6 %all-to-all-start.6 = ((f32[32,11,8,128]{3,2,1,0:T(8,128)}), f32[32,11,8,128]{3,2,1,0:T(8,128)S(1)}, u32[]{:S(2)}, u32[]{:S(2)}) async-start(f32[32,11,8,128]{3,2,1,0:T(8,128)} %blocks.1), calls=%async_computation.6 | async-start | bytes 2883584 | tf_op jit(solution)/shard_map/all_to_all | solution.py:240
  188.2 1.3 fusion.5
  192.7 1.5 fusion.17
  194.3 2.3 %convolution_bitcast_fusion = f32[1,1,256,256]{3,2,1,0:T(8,128)} fusion(f32[256,256]{1,0:T(8,128)S(1)} %fusion.17, f32[256,256]{1,0:T(8,128)} %constant.126.clone), kind=kOutput, calls=%fused_computation.5 | convolution fusion | flops 201326592 | bytes 786432 | tf_op jit(solution)/shard_map/dot_general | solution.py:289
  196.5 12.3 %all-to-all-done.6.got_ref = f32[32,11,8,128]{3,2,1,0:T(8,128)S(1)} async-done(((f32[32,11,8,128]{3,2,1,0:T(8,128)}), f32[32,11,8,128]{3,2,1,0:T(8,128)S(1)}, u32[]{:S(2)}, u32[]{:S(2)}) %all-to-all-start.6) | async-done | bytes 1441824 | tf_op jit(solution)/shard_map/all_to_all | solution.py:240
  208.8 1.4 volume.1
  (51 shorter events, 6.1 us)
Async XLA Ops:
  0.6 73.8 %copy-start = (f32[1,1,256,256]{3,2,1,0:T(8,128)S(1)}, f32[1,1,256,256]{3,2,1,0:T(8,128)}, u32[]{:S(2)}) copy-start(f32[1,1,256,256]{3,2,1,0:T(8,128)} %param.13) | copy-start | bytes 786436
  3.2 29.9 %all-to-all-start = ((f32[32,16,640]{2,1,0:T(8,128)}), f32[32,16,640]{2,1,0:T(8,128)S(1)}, u32[]{:S(2)}, u32[]{:S(2)}) async-start(f32[32,16,640]{2,1,0:T(8,128)} %rays.1), calls=%async_computation | async-start | bytes 2621440 | tf_op jit(solution)/shard_map/all_to_all | solution.py:240
  33.1 35.5 %copy-start.7 = (s32[1,1,2]{2,1,0:T(1,128)S(1)}, s32[1,1,2]{2,1,0:T(1,128)}, u32[]{:S(2)}) copy-start(s32[1,1,2]{2,1,0:T(1,128)} %param.12) | copy-start | bytes 28
  33.1 41.4 %copy-start.6 = (f32[256,256]{1,0:T(8,128)S(1)}, f32[256,256]{1,0:T(8,128)}, u32[]{:S(2)}) copy-start(f32[256,256]{1,0:T(8,128)} %constant.126.clone) | copy-start | bytes 786436
  59.7 21.2 %all-to-all-start.2 = ((f32[16,25,1,128]{3,2,1,0:T(1,128)}), f32[16,25,1,128]{3,2,1,0:T(1,128)S(1)}, u32[]{:S(2)}, u32[]{:S(2)}) async-start(f32[16,25,1,128]{3,2,1,0:T(1,128)} %broadcast_in_dim.63), calls=%async_computation.2 | async-start | bytes 409600 | tf_op jit(solution)/shard_map/all_to_all | solution.py:240
  93.2 1.5 copy-start.1
  93.2 1.8 copy-start.2
  93.2 1.2 copy-start.4
  102.4 13.6 %collective-permute-start = (f32[4,256,256]{2,1,0:T(8,128)S(1)}, f32[4,256,256]{2,1,0:T(8,128)}, u32[]{:S(2)}, u32[]{:S(2)}) collective-permute-start(f32[4,256,256]{2,1,0:T(8,128)S(1)} %get-tuple-element.13), channel_id=1, source_target_pairs={{0,1},{1,0},{2,3},{3,2},{4,5},{5,4},{6,7},{7,6},{8,9},{9,8},{10,11... | collective-permute-start | bytes 3145736 | tf_op jit(solution)/shard_map/ppermute | solution.py:262
  111.8 17.0 %all-to-all-start.3 = ((f32[4,50,8,128]{3,2,1,0:T(8,128)}), f32[4,50,8,128]{3,2,1,0:T(8,128)}, u32[]{:S(2)}, u32[]{:S(2)}) async-start(f32[4,50,8,128]{3,2,1,0:T(8,128)} %get-tuple-element.11), calls=%async_computation.3 | async-start | bytes 1638400 | tf_op jit(solution)/shard_map/all_to_all | solution.py:240
  118.2 17.5 %collective-permute-start.1 = (f32[256,256]{1,0:T(8,128)}, f32[256,256]{1,0:T(8,128)S(1)}, u32[]{:S(2)}, u32[]{:S(2)}) collective-permute-start(f32[256,256]{1,0:T(8,128)} %get-tuple-element.27), channel_id=1, source_target_pairs={{0,4},{2,6},{4,0},{6,2},{1,5},{3,7},{5,1},{7,3},{8,12},{10,14},{12... | collective-permute-start | bytes 786440 | tf_op jit(solution)/shard_map/ppermute | solution.py:262
  122.0 13.8 %collective-permute-start.2 = (f32[256,256]{1,0:T(8,128)S(1)}, f32[256,256]{1,0:T(8,128)S(1)}, u32[]{:S(2)}, u32[]{:S(2)}) collective-permute-start(f32[256,256]{1,0:T(8,128)S(1)} %get-tuple-element.29), channel_id=1, source_target_pairs={{0,2},{2,4},{4,6},{6,0},{1,3},{3,5},{5,7},{7,1},{8,10},{10,12},{12... | collective-permute-start | bytes 786440 | tf_op jit(solution)/shard_map/ppermute | solution.py:262
  123.9 11.9 %collective-permute-start.3 = (f32[256,256]{1,0:T(8,128)S(1)}, f32[256,256]{1,0:T(8,128)}, u32[]{:S(2)}, u32[]{:S(2)}) collective-permute-start(f32[256,256]{1,0:T(8,128)S(1)} %get-tuple-element.28), channel_id=1, source_target_pairs={{0,6},{2,0},{4,2},{6,4},{1,7},{3,1},{5,3},{7,5},{8,14},{10,8},{12,... | collective-permute-start | bytes 786440 | tf_op jit(solution)/shard_map/ppermute | solution.py:262
  130.7 18.8 %all-to-all-start.4 = ((f32[16,25,1,128]{3,2,1,0:T(1,128)}), f32[16,25,1,128]{3,2,1,0:T(1,128)S(1)}, u32[]{:S(2)}, u32[]{:S(2)}) async-start(f32[16,25,1,128]{3,2,1,0:T(1,128)} %bitcast.28), calls=%async_computation.4 | async-start | bytes 409600 | tf_op jit(solution)/shard_map/all_to_all | solution.py:240
  136.9 11.2 %collective-permute-start.4 = (f32[64,256]{1,0:T(8,128)S(1)}, f32[64,256]{1,0:T(8,128)S(1)}, u32[]{:S(2)}, u32[]{:S(2)}) collective-permute-start(f32[64,256]{1,0:T(8,128)S(1)} %get-tuple-element.32), channel_id=1, source_target_pairs={{0,256},{128,384},{256,0},{384,128},{1,257},{129,385},{257,1},{385... | collective-permute-start | bytes 196616 | tf_op jit(solution)/shard_map/ppermute | solution.py:262
  141.6 6.5 %collective-permute-start.5 = (f32[64,256]{1,0:T(8,128)S(1)}, f32[64,256]{1,0:T(8,128)S(1)}, u32[]{:S(2)}, u32[]{:S(2)}) collective-permute-start(f32[64,256]{1,0:T(8,128)S(1)} %get-tuple-element.34), channel_id=1, source_target_pairs={{0,128},{128,256},{256,384},{384,0},{1,129},{129,257},{257,385},{3... | collective-permute-start | bytes 196616 | tf_op jit(solution)/shard_map/ppermute | solution.py:262
  143.8 5.6 %collective-permute-start.6 = (f32[64,256]{1,0:T(8,128)S(1)}, f32[64,256]{1,0:T(8,128)S(1)}, u32[]{:S(2)}, u32[]{:S(2)}) collective-permute-start(f32[64,256]{1,0:T(8,128)S(1)} %get-tuple-element.33), channel_id=1, source_target_pairs={{0,384},{128,0},{256,128},{384,256},{1,385},{129,1},{257,129},{385... | collective-permute-start | bytes 196616 | tf_op jit(solution)/shard_map/ppermute | solution.py:262
  175.6 12.6 %copy-start.5 = (f32[5,4,16,640]{3,2,1,0:T(8,128)S(1)}, f32[5,4,16,640]{3,2,1,0:T(8,128)}, u32[]{:S(2)}) copy-start(f32[5,4,16,640]{3,2,1,0:T(8,128)} %copy-done.4) | copy-start | bytes 2457604
  175.6 33.2 %all-to-all-start.6 = ((f32[32,11,8,128]{3,2,1,0:T(8,128)}), f32[32,11,8,128]{3,2,1,0:T(8,128)S(1)}, u32[]{:S(2)}, u32[]{:S(2)}) async-start(f32[32,11,8,128]{3,2,1,0:T(8,128)} %blocks.1), calls=%async_computation.6 | async-start | bytes 2883584 | tf_op jit(solution)/shard_map/all_to_all | solution.py:240
  189.5 19.4 %copy-start.3 = (bf16[8,64,128]{2,1,0:T(8,128)(2,1)S(1)}, bf16[8,64,128]{2,1,0:T(8,128)(2,1)}, u32[]{:S(2)}) copy-start(bf16[8,64,128]{2,1,0:T(8,128)(2,1)} %mat_hbm.1) | copy-start | bytes 393220

commit v7 on v6

--- a/solution.py
+++ b/solution.py
@@ -236,6 +236,22 @@
     )(ids, quarter, piece)
 
 
+def add_kernel(parts_ref, out_ref):
+    out_ref[...] = (parts_ref[0] + parts_ref[1]) + (parts_ref[2] + parts_ref[3])
+
+
+def add_shares(parts):
+    vmem = pl.BlockSpec(memory_space=pltpu.VMEM)
+    return pl.pallas_call(
+        add_kernel,
+        out_shape=jax.ShapeDtypeStruct((50, 8, 128), jnp.float32),
+        in_specs=[vmem],
+        out_specs=vmem,
+        compiler_params=pltpu.CompilerParams(vmem_limit_bytes=LIMIT),
+        name="add",
+    )(parts)
+
+
 def exchange(x, axes):
     return lax.all_to_all(x, axes, split_axis=0, concat_axis=0, tiled=True)
 
@@ -304,7 +320,7 @@
     rows = (pick(rows, y, NY) + got[0] + got[1] + got[2]).reshape(NZ, 8, 1, 128)
 
     part = exchange(placed, "y")
-    part = part.sum(0)
+    part = add_shares(part)
     part = exchange(chunks_of_z(part), "z")
     mine = part.sum(0)
     got = exchange(jnp.concatenate([jnp.broadcast_to(mine[None], (NZ, 25, 1, 128)), rows], axis=1), "z")

time: 211 us -> 209 us (level)
  transfers between devices with their start and end apart: 12 -> 12, of which waited for: 5 -> 6; matrix products, arithmetic and copies ran while one was open for 7% -> 6% of each run, Pallas kernels for 0% -> 0%
where the time goes in v7:
time: 209 us; the launch traced here: 208 us
  starting transfers between devices  71.3 us (34%)
  blocking collectives  60.1 us (29%)
  waiting for transfers between devices  38.8 us (19%)
  Pallas kernels  14 us (7%)
  other arithmetic  7.9 us (4%)
  between operations  7.65 us (4%)
  matrix products  4.59 us (2%)
  local copies, waits for them, and re-layouts  3.41 us (2%)
    all_to_all x2, blocking collectives, exchange(): return lax.all_to_all(x, axes, split_axis=0, concat_axis=0, tiled=True)  47.9 us
    all_to_all x5, starting transfers between devices, exchange(): return lax.all_to_all(x, axes, split_axis=0, concat_axis=0, tiled=True)  40.4 us
    all_to_all x5, waiting for transfers between devices, exchange(): return lax.all_to_all(x, axes, split_axis=0, concat_axis=0, tiled=True)  37.2 us
    ppermute x7, starting transfers between devices, shift(): return lax.ppermute(x, axis, [(i, (i + by) % size) for i in range(size)])  30.8 us
    all_gather x1, blocking collectives, step(): every = lax.all_gather(summed, 'y', axis=0, tiled=False)  12.2 us
    pallas_call x1, Pallas kernels, spot(): pl.pallas_call(spot_kernel, out_shape=(plane, half, half, jax.ShapeDtypeS...  7.53 us
  transfers between devices with their start and end apart: 12, of which 6 were waited for; matrix products, arithmetic and copies ran while one was open for 6% of the time, Pallas kernels for 0%

profile of v7, /device:TPU:1, one launch (start us, length us, event | category | flops | bytes accessed | tf_op | source)
XLA Modules:
  0.0 207.8 jit_solution(15400515386913716249)
XLA Ops:
  0.6 2.6 %rays.1 = f32[32,16,640]{2,1,0:T(8,128)} custom-call(bf16[2,128,320]{2,1,0:T(8,128)(2,1)} %bitcast.102, bf16[8,64,128]{2,1,0:T(8,128)(2,1)} %mat_hbm.1), custom_call_target="tpu_custom_call" | custom-call | tf_op jit(solution)/shard_map/rays/pallas_call | solution.py:166
  3.2 10.5 %all-to-all-start = ((f32[32,16,640]{2,1,0:T(8,128)}), f32[32,16,640]{2,1,0:T(8,128)S(1)}, u32[]{:S(2)}, u32[]{:S(2)}) async-start(f32[32,16,640]{2,1,0:T(8,128)} %rays.1), calls=%async_computation | async-start | bytes 2621440 | tf_op jit(solution)/shard_map/all_to_all | solution.py:256
  14.8 18.3 %all-to-all-done = f32[32,16,640]{2,1,0:T(8,128)S(1)} async-done(((f32[32,16,640]{2,1,0:T(8,128)}), f32[32,16,640]{2,1,0:T(8,128)S(1)}, u32[]{:S(2)}, u32[]{:S(2)}) %all-to-all-start) | async-done | bytes 1310752 | tf_op jit(solution)/shard_map/all_to_all | solution.py:256
  33.7 25.1 %all_to_all.35 = f32[16,25,1,128]{3,2,1,0:T(1,128)S(1)} all-to-all(f32[16,25,1,128]{3,2,1,0:T(1,128)S(1)} %bitcast.101), channel_id=1, replica_groups=mesh['y'=4,'z'=16,'x'=4,'core'=2] {'z'}, dimensions={0} | all-to-all | bytes 409600 | tf_op jit(solution)/shard_map/all_to_all | solution.py:256
  58.9 0.8 broadcast_in_dim.63
  59.7 8.9 %all-to-all-start.2 = ((f32[16,25,1,128]{3,2,1,0:T(1,128)}), f32[16,25,1,128]{3,2,1,0:T(1,128)S(1)}, u32[]{:S(2)}, u32[]{:S(2)}) async-start(f32[16,25,1,128]{3,2,1,0:T(1,128)} %broadcast_in_dim.63), calls=%async_computation.2 | async-start | bytes 409600 | tf_op jit(solution)/shard_map/all_to_all | solution.py:256
  73.1 1.4 pad_add_fusion.where_ref
  75.3 5.7 %all-to-all-done.2 = f32[16,25,1,128]{3,2,1,0:T(1,128)S(1)} async-done(((f32[16,25,1,128]{3,2,1,0:T(1,128)}), f32[16,25,1,128]{3,2,1,0:T(1,128)S(1)}, u32[]{:S(2)}, u32[]{:S(2)}) %all-to-all-start.2) | async-done | bytes 204832 | tf_op jit(solution)/shard_map/all_to_all | solution.py:256
  80.9 12.2 %all_gather.3 = f32[4,50,8,128]{3,2,1,0:T(8,128)S(1)} all-gather(f32[1,50,8,128]{3,2,1,0:T(8,128)S(1)} %bitcast.100), channel_id=1, replica_groups=mesh['y'=4,'z'=16,'x'=4,'core'=2] {'y'}, dimensions={0}, use_global_device_ids=true | all-gather | bytes 1024000 | tf_op jit(solution)/shard_map/all_gather | solution.py:294
  93.2 1.1 sine_multiply_fusion
  95.0 7.5 %spot.1 = (f32[256,256]{1,0:T(8,128)S(1)}, f32[4,256,256]{2,1,0:T(8,128)S(1)}, f32[4,256,256]{2,1,0:T(8,128)}, f32[2,256,256]{2,1,0:T(8,128)S(1)}, f32[4,50,8,128]{3,2,1,0:T(8,128)}) custom-call(s32[3]{0:T(128)S(1)} %pad_add_fusion.where_ref, f32[256,256]{1,0:T(8,128)S(1)} %get-tuple-element.31.tr_ref, f32[256,256]{1,0:T(8,128)S(1)} %get-tuple-element.30.ti_ref, ...), custom_call_target="tpu_custom_call" | custom-call | tf_op jit(solution)/shard_map/spot/pallas_call | solution.py:128
  102.5 9.3 %collective-permute-start = (f32[4,256,256]{2,1,0:T(8,128)}, f32[4,256,256]{2,1,0:T(8,128)}, u32[]{:S(2)}, u32[]{:S(2)}) collective-permute-start(f32[4,256,256]{2,1,0:T(8,128)} %get-tuple-element.13), channel_id=1, source_target_pairs={{0,1},{1,0},{2,3},{3,2},{4,5},{5,4},{6,7},{7,6},{8,9},{9,8},{10,11... | collective-permute-start | bytes 3145736 | tf_op jit(solution)/shard_map/ppermute | solution.py:278
  111.9 3.5 %all-to-all-start.3 = ((f32[4,50,8,128]{3,2,1,0:T(8,128)}), f32[4,50,8,128]{3,2,1,0:T(8,128)S(1)}, u32[]{:S(2)}, u32[]{:S(2)}) async-start(f32[4,50,8,128]{3,2,1,0:T(8,128)} %get-tuple-element.11), calls=%async_computation.3 | async-start | bytes 1638400 | tf_op jit(solution)/shard_map/all_to_all | solution.py:256
  115.4 1.4 add.151
  116.9 3.7 %collective-permute-start.1 = (f32[256,256]{1,0:T(8,128)S(1)}, f32[256,256]{1,0:T(8,128)S(1)}, u32[]{:S(2)}, u32[]{:S(2)}) collective-permute-start(f32[256,256]{1,0:T(8,128)S(1)} %get-tuple-element.27), channel_id=1, source_target_pairs={{0,4},{2,6},{4,0},{6,2},{1,5},{3,7},{5,1},{7,3},{8,12},{10,14},{12... | collective-permute-start | bytes 786440 | tf_op jit(solution)/shard_map/ppermute | solution.py:278
  120.7 1.9 collective-permute-start.2
  122.6 4.6 %collective-permute-start.3 = (f32[256,256]{1,0:T(8,128)S(1)}, f32[256,256]{1,0:T(8,128)S(1)}, u32[]{:S(2)}, u32[]{:S(2)}) collective-permute-start(f32[256,256]{1,0:T(8,128)S(1)} %get-tuple-element.28), channel_id=1, source_target_pairs={{0,6},{2,0},{4,2},{6,4},{1,7},{3,1},{5,3},{7,5},{8,14},{10,8},{12,... | collective-permute-start | bytes 786440 | tf_op jit(solution)/shard_map/ppermute | solution.py:278
  127.2 0.9 all-to-all-done.3.parts_ref
  128.8 5.0 %all-to-all-start.4 = ((f32[16,25,1,128]{3,2,1,0:T(1,128)}), f32[16,25,1,128]{3,2,1,0:T(1,128)S(1)}, u32[]{:S(2)}, u32[]{:S(2)}) async-start(f32[16,25,1,128]{3,2,1,0:T(1,128)} %bitcast.28), calls=%async_computation.4 | async-start | bytes 409600 | tf_op jit(solution)/shard_map/all_to_all | solution.py:256
  134.2 1.0 fusion.10
  135.3 4.8 %collective-permute-start.4 = (f32[64,256]{1,0:T(8,128)S(1)}, f32[64,256]{1,0:T(8,128)S(1)}, u32[]{:S(2)}, u32[]{:S(2)}) collective-permute-start(f32[64,256]{1,0:T(8,128)S(1)} %get-tuple-element.32), channel_id=1, source_target_pairs={{0,256},{128,384},{256,0},{384,128},{1,257},{129,385},{257,1},{385... | collective-permute-start | bytes 196616 | tf_op jit(solution)/shard_map/ppermute | solution.py:278
  140.0 2.2 %collective-permute-start.5 = (f32[64,256]{1,0:T(8,128)S(1)}, f32[64,256]{1,0:T(8,128)S(1)}, u32[]{:S(2)}, u32[]{:S(2)}) collective-permute-start(f32[64,256]{1,0:T(8,128)S(1)} %get-tuple-element.34), channel_id=1, source_target_pairs={{0,128},{128,256},{256,384},{384,0},{1,129},{129,257},{257,385},{3... | collective-permute-start | bytes 196616 | tf_op jit(solution)/shard_map/ppermute | solution.py:278
  142.2 4.3 %collective-permute-start.6 = (f32[64,256]{1,0:T(8,128)S(1)}, f32[64,256]{1,0:T(8,128)S(1)}, u32[]{:S(2)}, u32[]{:S(2)}) collective-permute-start(f32[64,256]{1,0:T(8,128)S(1)} %get-tuple-element.33), channel_id=1, source_target_pairs={{0,384},{128,0},{256,128},{384,256},{1,385},{129,1},{257,129},{385... | collective-permute-start | bytes 196616 | tf_op jit(solution)/shard_map/ppermute | solution.py:278
  146.6 1.3 collective-permute-done.6
  148.5 22.9 %all_to_all.36 = f32[16,33,1,128]{3,2,1,0:T(1,128)S(1)} all-to-all(f32[16,33,1,128]{3,2,1,0:T(1,128)S(1)} %pad_maximum_fusion), channel_id=1, replica_groups=mesh['y'=4,'z'=16,'x'=4,'core'=2] {'z'}, dimensions={0} | all-to-all | bytes 540672 | tf_op jit(solution)/shard_map/all_to_all | solution.py:256
  171.4 1.8 blocks.1
  173.1 12.6 %all-to-all-start.6 = ((f32[32,11,8,128]{3,2,1,0:T(8,128)}), f32[32,11,8,128]{3,2,1,0:T(8,128)S(1)}, u32[]{:S(2)}, u32[]{:S(2)}) async-start(f32[32,11,8,128]{3,2,1,0:T(8,128)} %blocks.1), calls=%async_computation.6 | async-start | bytes 2883584 | tf_op jit(solution)/shard_map/all_to_all | solution.py:256
  185.8 1.3 fusion.5
  190.2 1.5 fusion.17
  191.8 2.3 %convolution_bitcast_fusion = f32[1,1,256,256]{3,2,1,0:T(8,128)} fusion(f32[256,256]{1,0:T(8,128)S(1)} %fusion.17, f32[256,256]{1,0:T(8,128)} %constant.126.clone), kind=kOutput, calls=%fused_computation.5 | convolution fusion | flops 201326592 | bytes 786432 | tf_op jit(solution)/shard_map/dot_general | solution.py:305
  194.0 12.3 %all-to-all-done.6.got_ref = f32[32,11,8,128]{3,2,1,0:T(8,128)S(1)} async-done(((f32[32,11,8,128]{3,2,1,0:T(8,128)}), f32[32,11,8,128]{3,2,1,0:T(8,128)S(1)}, u32[]{:S(2)}, u32[]{:S(2)}) %all-to-all-start.6) | async-done | bytes 1441824 | tf_op jit(solution)/shard_map/all_to_all | solution.py:256
  206.4 1.4 volume.1
  (53 shorter events, 6.2 us)
Async XLA Ops:
  0.6 73.8 %copy-start = (f32[1,1,256,256]{3,2,1,0:T(8,128)S(1)}, f32[1,1,256,256]{3,2,1,0:T(8,128)}, u32[]{:S(2)}) copy-start(f32[1,1,256,256]{3,2,1,0:T(8,128)} %param.13) | copy-start | bytes 786436
  3.2 29.9 %all-to-all-start = ((f32[32,16,640]{2,1,0:T(8,128)}), f32[32,16,640]{2,1,0:T(8,128)S(1)}, u32[]{:S(2)}, u32[]{:S(2)}) async-start(f32[32,16,640]{2,1,0:T(8,128)} %rays.1), calls=%async_computation | async-start | bytes 2621440 | tf_op jit(solution)/shard_map/all_to_all | solution.py:256
  33.1 35.5 %copy-start.8 = (s32[1,1,2]{2,1,0:T(1,128)S(1)}, s32[1,1,2]{2,1,0:T(1,128)}, u32[]{:S(2)}) copy-start(s32[1,1,2]{2,1,0:T(1,128)} %param.12) | copy-start | bytes 28
  33.1 41.4 %copy-start.6 = (f32[256,256]{1,0:T(8,128)S(1)}, f32[256,256]{1,0:T(8,128)}, u32[]{:S(2)}) copy-start(f32[256,256]{1,0:T(8,128)} %constant.126.clone) | copy-start | bytes 786436
  59.7 21.2 %all-to-all-start.2 = ((f32[16,25,1,128]{3,2,1,0:T(1,128)}), f32[16,25,1,128]{3,2,1,0:T(1,128)S(1)}, u32[]{:S(2)}, u32[]{:S(2)}) async-start(f32[16,25,1,128]{3,2,1,0:T(1,128)} %broadcast_in_dim.63), calls=%async_computation.2 | async-start | bytes 409600 | tf_op jit(solution)/shard_map/all_to_all | solution.py:256
  93.2 1.5 copy-start.1
  93.2 1.8 copy-start.2
  93.2 1.2 copy-start.4
  102.5 12.9 %collective-permute-start = (f32[4,256,256]{2,1,0:T(8,128)}, f32[4,256,256]{2,1,0:T(8,128)}, u32[]{:S(2)}, u32[]{:S(2)}) collective-permute-start(f32[4,256,256]{2,1,0:T(8,128)} %get-tuple-element.13), channel_id=1, source_target_pairs={{0,1},{1,0},{2,3},{3,2},{4,5},{5,4},{6,7},{7,6},{8,9},{9,8},{10,11... | collective-permute-start | bytes 3145736 | tf_op jit(solution)/shard_map/ppermute | solution.py:278
  111.9 16.2 %all-to-all-start.3 = ((f32[4,50,8,128]{3,2,1,0:T(8,128)}), f32[4,50,8,128]{3,2,1,0:T(8,128)S(1)}, u32[]{:S(2)}, u32[]{:S(2)}) async-start(f32[4,50,8,128]{3,2,1,0:T(8,128)} %get-tuple-element.11), calls=%async_computation.3 | async-start | bytes 1638400 | tf_op jit(solution)/shard_map/all_to_all | solution.py:256
  116.8 5.8 %copy-start.7 = (f32[4,256,256]{2,1,0:T(8,128)}, f32[4,256,256]{2,1,0:T(8,128)S(1)}, u32[]{:S(2)}) copy-start(f32[4,256,256]{2,1,0:T(8,128)S(1)} %add.151) | copy-start | bytes 3145732
  116.9 16.9 %collective-permute-start.1 = (f32[256,256]{1,0:T(8,128)S(1)}, f32[256,256]{1,0:T(8,128)S(1)}, u32[]{:S(2)}, u32[]{:S(2)}) collective-permute-start(f32[256,256]{1,0:T(8,128)S(1)} %get-tuple-element.27), channel_id=1, source_target_pairs={{0,4},{2,6},{4,0},{6,2},{1,5},{3,7},{5,1},{7,3},{8,12},{10,14},{12... | collective-permute-start | bytes 786440 | tf_op jit(solution)/shard_map/ppermute | solution.py:278
  120.7 13.5 %collective-permute-start.2 = (f32[256,256]{1,0:T(8,128)S(1)}, f32[256,256]{1,0:T(8,128)S(1)}, u32[]{:S(2)}, u32[]{:S(2)}) collective-permute-start(f32[256,256]{1,0:T(8,128)S(1)} %get-tuple-element.29), channel_id=1, source_target_pairs={{0,2},{2,4},{4,6},{6,0},{1,3},{3,5},{5,7},{7,1},{8,10},{10,12},{12... | collective-permute-start | bytes 786440 | tf_op jit(solution)/shard_map/ppermute | solution.py:278
  122.6 11.6 %collective-permute-start.3 = (f32[256,256]{1,0:T(8,128)S(1)}, f32[256,256]{1,0:T(8,128)S(1)}, u32[]{:S(2)}, u32[]{:S(2)}) collective-permute-start(f32[256,256]{1,0:T(8,128)S(1)} %get-tuple-element.28), channel_id=1, source_target_pairs={{0,6},{2,0},{4,2},{6,4},{1,7},{3,1},{5,3},{7,5},{8,14},{10,8},{12,... | collective-permute-start | bytes 786440 | tf_op jit(solution)/shard_map/ppermute | solution.py:278
  128.8 19.2 %all-to-all-start.4 = ((f32[16,25,1,128]{3,2,1,0:T(1,128)}), f32[16,25,1,128]{3,2,1,0:T(1,128)S(1)}, u32[]{:S(2)}, u32[]{:S(2)}) async-start(f32[16,25,1,128]{3,2,1,0:T(1,128)} %bitcast.28), calls=%async_computation.4 | async-start | bytes 409600 | tf_op jit(solution)/shard_map/all_to_all | solution.py:256
  135.3 11.3 %collective-permute-start.4 = (f32[64,256]{1,0:T(8,128)S(1)}, f32[64,256]{1,0:T(8,128)S(1)}, u32[]{:S(2)}, u32[]{:S(2)}) collective-permute-start(f32[64,256]{1,0:T(8,128)S(1)} %get-tuple-element.32), channel_id=1, source_target_pairs={{0,256},{128,384},{256,0},{384,128},{1,257},{129,385},{257,1},{385... | collective-permute-start | bytes 196616 | tf_op jit(solution)/shard_map/ppermute | solution.py:278
  140.0 6.5 %collective-permute-start.5 = (f32[64,256]{1,0:T(8,128)S(1)}, f32[64,256]{1,0:T(8,128)S(1)}, u32[]{:S(2)}, u32[]{:S(2)}) collective-permute-start(f32[64,256]{1,0:T(8,128)S(1)} %get-tuple-element.34), channel_id=1, source_target_pairs={{0,128},{128,256},{256,384},{384,0},{1,129},{129,257},{257,385},{3... | collective-permute-start | bytes 196616 | tf_op jit(solution)/shard_map/ppermute | solution.py:278
  142.2 5.6 %collective-permute-start.6 = (f32[64,256]{1,0:T(8,128)S(1)}, f32[64,256]{1,0:T(8,128)S(1)}, u32[]{:S(2)}, u32[]{:S(2)}) collective-permute-start(f32[64,256]{1,0:T(8,128)S(1)} %get-tuple-element.33), channel_id=1, source_target_pairs={{0,384},{128,0},{256,128},{384,256},{1,385},{129,1},{257,129},{385... | collective-permute-start | bytes 196616 | tf_op jit(solution)/shard_map/ppermute | solution.py:278
  173.1 12.6 %copy-start.5 = (f32[5,4,16,640]{3,2,1,0:T(8,128)S(1)}, f32[5,4,16,640]{3,2,1,0:T(8,128)}, u32[]{:S(2)}) copy-start(f32[5,4,16,640]{3,2,1,0:T(8,128)} %copy-done.4) | copy-start | bytes 2457604
  173.1 33.2 %all-to-all-start.6 = ((f32[32,11,8,128]{3,2,1,0:T(8,128)}), f32[32,11,8,128]{3,2,1,0:T(8,128)S(1)}, u32[]{:S(2)}, u32[]{:S(2)}) async-start(f32[32,11,8,128]{3,2,1,0:T(8,128)} %blocks.1), calls=%async_computation.6 | async-start | bytes 2883584 | tf_op jit(solution)/shard_map/all_to_all | solution.py:256
  187.0 19.4 %copy-start.3 = (bf16[8,64,128]{2,1,0:T(8,128)(2,1)S(1)}, bf16[8,64,128]{2,1,0:T(8,128)(2,1)}, u32[]{:S(2)}) copy-start(bf16[8,64,128]{2,1,0:T(8,128)(2,1)} %mat_hbm.1) | copy-start | bytes 393220
